TPU v7x, 32 devices: a whole 2x2x4 slice. The times are simulated.
32 devices in a mesh: space: 32 (over z, y, x, core).
Axes of the slice: x: 2, y: 2, z: 4, core: 2. Of those that a mesh axis runs over, the one named last changes fastest.
Arguments:
- positions: float32 [3, 131072], P(None, 'space'), may hold values from 1 to 128, as said below
- velocity: float32 [3, 131072], P(None, 'space'), may hold values from -5 to 5
- deformation: float32 [9, 131072], P(None, 'space'), may hold values from -0.6 to 1.6
- affine: float32 [9, 131072], P(None, 'space'), may hold values from -3 to 3
- particle_mass: float32 [131072], P('space'), may hold values from 0.05 to 0.3
- volume: float32 [131072], P('space'), may hold values from 0.06 to 0.25
- bin_block: int32 [256], P('space'), may hold values from 0 to 255
- live_count: int32 [32], P('space'), may hold values from 2 to 4, as said below
Outputs:
- displacement: float32 [3, 131072], P(None, 'space')
- new_velocity: float32 [3, 131072], P(None, 'space')
- new_deformation: float32 [9, 131072], P(None, 'space')
- new_affine: float32 [9, 131072], P(None, 'space')
Inputs may be any that keep to these rules, and one draw needn't show every extreme that they name: `positions`: each particle lies inside its bin's block: 4 d + 1 to 4 d + 4 along the first dimension for the bins of device d, 4 (bin_block // 16) + 1 to 4 (bin_block // 16) + 4 along the second, 4 (bin_block % 16) + 1 to 4 (bin_block % 16) + 4 along the third. The live bins of device d are its first live_count[d] slots; devices 2 k and 2 k + 1 hold at most 6 live bins together, and some such pair holds exactly 6 in every draw.
All inputs are finite; a program needn't handle non-finite values.
Results may differ from a plain program's by a relative error of at most 0.0003.
Values sent between devices are 32-bit elements; how exact they have to be, the bound alone decides.
No kernel may reach another device: no remote copies, remote signals or barrier semaphores. Data moves between devices by JAX's collectives and lax.ppermute only.
A program may use at most 128 MiB of HBM per device.

v0:
```python
import functools

import jax
import jax.numpy as jnp
from jax import lax
from jax.experimental import pallas as pl
from jax.experimental.pallas import tpu as pltpu
from jax.sharding import PartitionSpec as P

BZ = 16
STEPS = 3
NGY = 66
NGZ = 66

mu_shear = 4.0
lame_first = 6.0
courant = 0.15
sound_speed = 3.7416573867739413
mass_floor = 0.05
gravity_x = 3.0
gravity_z = -9.0

LANES = 128
TILE = 36
PITCH = 40
META = 112
SPEED = 7
BIG = 3.0e38
F32 = jnp.float32
BF16 = jnp.bfloat16
INTERPRET = False

POS, VEL, DEF, AFF, MASS, VOL, TRAV = 0, 3, 6, 15, 24, 25, 26
ROWS = 29


def iota(shape, dim):
    return lax.broadcasted_iota(jnp.int32, shape, dim)


def split(value):
    high = value.astype(BF16)
    low = (value - high.astype(F32)).astype(BF16)
    return high, low


def dot_nt(a, b):
    return lax.dot_general(a, b, (((1,), (1,)), ((), ())), preferred_element_type=F32)


def dot_nn(a, b):
    return lax.dot_general(a, b, (((1,), (0,)), ((), ())), preferred_element_type=F32)


def spline(distance):
    magnitude = jnp.abs(distance)
    outer = jnp.maximum(1.5 - magnitude, 0.0)
    inner = jnp.maximum(0.5 - magnitude, 0.0)
    return 0.5 * outer * outer - 1.5 * inner * inner


def spread(value, bin_index, quarters):
    parts = [
        jnp.broadcast_to(value[row : row + 1, :], (8, LANES))
        for row in range(bin_index * quarters, (bin_index + 1) * quarters)
    ]
    return jnp.concatenate(parts, axis=1)


def bin_weights(local, bin_index, quarters, table):
    along_x, along_y, along_z = [spread(local[axis], bin_index, quarters) for axis in range(3)]
    width = along_x.shape[1]
    first = [spline(float(a) - along_x) for a in range(6)]
    first_moved = [first[a] * (float(a) - along_x) for a in range(6)]
    third_node = iota((8, width), 0)
    third_offset = third_node.astype(F32) - along_z
    third = jnp.where(third_node < 6, spline(third_offset), 0.0)
    third_moved = third * third_offset
    for a in range(6):
        second = spline(float(a) - along_y)
        second_moved = second * (float(a) - along_y)
        table[pl.ds(6 * a, 8), :] = second * third
        table[pl.ds(PITCH + 6 * a, 8), :] = second_moved * third
        table[pl.ds(2 * PITCH + 6 * a, 8), :] = second * third_moved
    return first, first_moved


def clear_pads(table):
    width = table.shape[1]
    for part in range(3):
        table[pl.ds(part * PITCH + PITCH - 8, 8), :] = jnp.zeros((8, width), F32)


def kirchhoff(deform):
    determinant = (
        deform[0] * (deform[4] * deform[8] - deform[5] * deform[7])
        - deform[1] * (deform[3] * deform[8] - deform[5] * deform[6])
        + deform[2] * (deform[3] * deform[7] - deform[4] * deform[6])
    )
    pressure = lame_first * (determinant - 1.0) * determinant
    stress = [None] * 9
    for r in range(3):
        for c in range(r, 3):
            product = (
                deform[3 * r] * deform[3 * c]
                + deform[3 * r + 1] * deform[3 * c + 1]
                + deform[3 * r + 2] * deform[3 * c + 2]
            )
            if r == c:
                stress[3 * r + c] = mu_shear * (product - 1.0) + pressure
            else:
                stress[3 * r + c] = mu_shear * product
                stress[3 * c + r] = stress[3 * r + c]
    return stress


def to_grid(state, local, blocks, device, bins, device_total, table, shuffle, tiles, message):
    rows = state[0].shape[0]
    quarters = rows // bins
    deform = state[DEF : DEF + 9]
    mass, volume = state[MASS], state[VOL]
    velocity = state[VEL : VEL + 3]
    speed = velocity[0] * velocity[0] + velocity[1] * velocity[1] + velocity[2] * velocity[2]
    speed = jnp.max(jnp.where(mass > 0.0, speed, 0.0), axis=0, keepdims=True)
    speed = jnp.max(speed, axis=1, keepdims=True)

    stress = kirchhoff(deform)
    scaled = 4.0 * volume
    span = 8 * rows
    zero = jnp.zeros((rows, LANES), F32)

    def put(matrix, row, value):
        shuffle[pl.ds(matrix * span + row, rows, stride=8), :] = value

    put(0, 0, mass)
    for c in range(3):
        put(0, 1 + c, mass * velocity[c])
        put(0, 4 + c, zero)
    put(0, 7, zero)
    for axis in range(3):
        put(1 + axis, 0, zero)
        put(1 + axis, 7, zero)
        for c in range(3):
            put(1 + axis, 1 + c, mass * state[AFF + 3 * c + axis])
            put(1 + axis, 4 + c, scaled * stress[3 * c + axis])

    for b in range(bins):
        first, first_moved = bin_weights(local, b, quarters, table)

        def channel(matrix):
            begin = matrix * span + 8 * b * quarters
            return jnp.concatenate(
                [shuffle[pl.ds(begin + 8 * q, 8), :] for q in range(quarters)], axis=1
            )

        base, slope_x, slope_y, slope_z = [channel(matrix) for matrix in range(4)]
        lefts = [
            jnp.concatenate([first[a] * base + first_moved[a] * slope_x for a in range(6)], axis=0),
            jnp.concatenate([first[a] * slope_y for a in range(6)], axis=0),
            jnp.concatenate([first[a] * slope_z for a in range(6)], axis=0),
        ]
        total = None
        for part in range(3):
            left_high, left_low = split(lefts[part])
            right_high, right_low = split(table[pl.ds(part * PITCH, PITCH), :])
            product = (
                dot_nt(left_high, right_high)
                + dot_nt(left_high, right_low)
                + dot_nt(left_low, right_high)
            )
            total = product if total is None else total + product
        tiles[:, TILE * b : TILE * (b + 1)] = total[:, 0:TILE]

    lane = iota((1, LANES), 1)
    meta = jnp.where(lane == SPEED, speed, 0.0)
    for b in range(bins):
        meta = jnp.where(lane == b, blocks[b].astype(F32), meta)
    row = iota((8, LANES), 0)
    lanes = iota((8, LANES), 1)
    extra = bins * TILE - LANES

    def packed(plane):
        body = tiles[pl.ds(8 * plane, 8), 0:LANES]
        rest = jnp.where(lanes < extra, tiles[pl.ds(8 * plane, 8), LANES : 2 * LANES], 0.0)
        rest = jnp.where(row == 7, jnp.broadcast_to(meta, (8, LANES)), rest)
        rest = pltpu.roll(rest, 0, 1, stride=extra, stride_axis=0)
        folded = jnp.sum(rest, axis=0, keepdims=True)
        return jnp.where(row == 7, jnp.broadcast_to(folded, (8, LANES)), body)

    low = [packed(0), packed(1)]
    high = [packed(4), packed(5)]

    def send(index, carry):
        message[index, 0:8, :] = low[0]
        message[index, 8:16, :] = low[1]
        return carry

    lax.fori_loop(0, device_total, send, 0)

    @pl.when(device + 1 < device_total)
    def _():
        message[device + 1, 0:8, :] = high[0]
        message[device + 1, 8:16, :] = high[1]


def unpacked(block, bins):
    row = iota((8, LANES), 0)
    lanes = iota((8, LANES), 1)
    extra = bins * TILE - LANES
    folded = jnp.broadcast_to(block[7:8, :], (8, LANES))
    rest = folded
    for bit in (1, 2, 4):
        rest = jnp.where(row & bit > 0, pltpu.roll(rest, LANES - bit * extra, 1), rest)
    rest = jnp.where((lanes < extra) & (row < 7), rest, 0.0)
    body = jnp.where(row < 7, block, 0.0)
    return jnp.concatenate([body, rest], axis=1)


def node_key(block, node):
    block_y = jnp.floor((block + 0.5) * (1.0 / BZ))
    block_z = block - BZ * block_y
    node_y = jnp.floor((node + 0.5) * (1.0 / 6.0))
    node_z = node - 6.0 * node_y
    return 4.0 * block_y + node_y, 4.0 * block_z + node_z


def to_particles(state, local, blocks, device, bins, device_total, tiles, received, table, shuffle, live):
    rows = state[0].shape[0]
    quarters = rows // bins
    width = bins * LANES
    nodes = bins * TILE
    speeds = jnp.max(received[:, 7, :], axis=0, keepdims=True)
    lane = iota((1, LANES), 1)
    fastest = jnp.max(jnp.where(lane == META + SPEED, speeds, 0.0), axis=1, keepdims=True)
    time_step = courant / (jnp.sqrt(fastest) + sound_speed)

    left_index = jnp.maximum(device - 1, 0)
    right_index = jnp.minimum(device + 1, device_total - 1)
    left_live = jnp.where(device > 0, 1.0, 0.0)
    right_live = jnp.where(device + 1 < device_total, 1.0, 0.0)
    left_block = received[left_index]
    right_block = received[right_index]
    left_meta = left_block[7:8, :]
    right_meta = right_block[7:8, :]

    position = iota((1, width), 1)
    column_bin = position // LANES
    column_slot = position - LANES * column_bin
    column_part = jnp.where(column_slot >= 2 * PITCH, 2, jnp.where(column_slot >= PITCH, 1, 0))
    column_node = column_slot - PITCH * column_part
    column_valid = (column_node < TILE) & (column_slot < 3 * PITCH)
    column_block = jnp.zeros((1, width), F32)
    for b in range(bins):
        column_block = jnp.where(column_bin == b, blocks[b].astype(F32), column_block)
    column_y, column_z = node_key(column_block, column_node.astype(F32))
    column_key = jnp.where(column_valid, LANES * column_y + column_z, -1.0)

    source = iota((nodes, 1), 0).astype(F32)
    source_bin = jnp.floor((source + 0.5) * (1.0 / TILE))
    source_node = source - TILE * source_bin

    def placing(values):
        source_block = jnp.zeros((nodes, 1), F32)
        for b in range(bins):
            source_block = jnp.where(source_bin == float(b), values[b], source_block)
        row_y, row_z = node_key(source_block, source_node)
        return jnp.where(LANES * row_y + row_z == column_key, 1.0, 0.0).astype(BF16)

    def meta_values(meta):
        return [
            jnp.max(jnp.where(lane == META + b, meta, 0.0), axis=1, keepdims=True)
            for b in range(bins)
        ]

    def placed(values, selector):
        count = values.shape[0]
        high, low = split(values)
        result = dot_nn(jnp.concatenate([high, low], axis=0), selector)
        return result[0:count] + result[count : 2 * count]

    own = placed(tiles[:, 0:nodes], placing([blocks[b].astype(F32) for b in range(bins)]))
    left_values = jnp.concatenate(
        [unpacked(left_block[0:8, :], bins), unpacked(left_block[8:16, :], bins)], axis=0
    )
    right_values = jnp.concatenate(
        [unpacked(right_block[0:8, :], bins), unpacked(right_block[8:16, :], bins)], axis=0
    )
    left = placed(left_values[:, 0:nodes] * left_live, placing(meta_values(left_meta)))
    right = placed(right_values[:, 0:nodes] * right_live, placing(meta_values(right_meta)))

    sub = iota((8, width), 0)
    wide_y = jnp.broadcast_to(column_y, (8, width))
    wide_z = jnp.broadcast_to(column_z, (8, width))
    wide_valid = jnp.broadcast_to(column_key, (8, width)) >= 0.0
    component = (sub >= 1) & (sub <= 3) & wide_valid
    floor_of = jnp.where(
        ((sub == 2) & (wide_y < 2.0)) | ((sub == 3) & (wide_z < 2.0)), 0.0, -BIG
    )
    roof_of = jnp.where(
        ((sub == 2) & (wide_y >= NGY - 2.0)) | ((sub == 3) & (wide_z >= NGZ - 2.0)), 0.0, BIG
    )
    pull = time_step * jnp.where(
        sub == 1, gravity_x, jnp.where(sub == 3, gravity_z, 0.0)
    )
    plane_total = 4 * device_total
    slot = iota((8, LANES), 1)
    lower_half, upper_half = [], []
    for a in range(6):
        sums = own[8 * a : 8 * a + 8]
        if a < 2:
            sums = sums + left[8 * a : 8 * a + 8]
        if a >= 4:
            sums = sums + right[8 * a - 32 : 8 * a - 24]
        plane = 4 * device + a
        node_mass = jnp.maximum(jnp.broadcast_to(sums[0:1, :], (8, width)), mass_floor)
        per_step = pltpu.roll(sums, 5, 0)
        motion = (sums - time_step * per_step) / node_mass + pull
        lowest = jnp.where(plane < 2, 0.0, -BIG)
        highest = jnp.where(plane >= plane_total - 2, 0.0, BIG)
        motion = jnp.maximum(motion, jnp.where(sub == 1, lowest, floor_of))
        motion = jnp.minimum(motion, jnp.where(sub == 1, highest, roof_of))
        inside = jnp.where(plane < plane_total, 1, 0)
        motion = jnp.where(component & (inside > 0), motion, 0.0)
        moved = pltpu.roll(motion, 3, 0)
        for b in range(bins):
            here = motion[:, LANES * b : LANES * (b + 1)]
            there = moved[:, LANES * b : LANES * (b + 1)]
            lower_half.append(
                jnp.where(slot < PITCH, here, jnp.where(slot < 2 * PITCH, there, 0.0))
            )
            upper_half.append(jnp.where(slot >= 2 * PITCH, here, 0.0))

    span = 8 * rows
    for b in range(bins):
        first, first_moved = bin_weights(local, b, quarters, table)
        motions = jnp.concatenate(
            [half[bins * a + b] for a in range(6) for half in (lower_half, upper_half)], axis=0
        )[:, 0 : 3 * PITCH]
        count = motions.shape[0]
        high, low = split(motions)
        right_high, right_low = split(table[pl.ds(0, 3 * PITCH), :])
        product = dot_nn(jnp.concatenate([high, low], axis=0), right_high)
        product = product[0:count] + product[count : 2 * count] + dot_nn(high, right_low)
        sums = [None, None, None]
        for a in range(6):
            top = product[16 * a : 16 * a + 8]
            bottom = product[16 * a + 8 : 16 * a + 16]
            terms = (first[a] * top, first[a] * bottom, first_moved[a] * top)
            sums = [t if s is None else s + t for s, t in zip(sums, terms)]
        for kind in range(3):
            for q in range(quarters):
                begin = kind * span + 8 * (b * quarters + q)
                shuffle[pl.ds(begin, 8), :] = sums[kind][:, LANES * q : LANES * (q + 1)]

    def take(kind, row):
        return shuffle[pl.ds(kind * span + row, rows, stride=8), :]

    velocity = [take(0, 1 + c) for c in range(3)]
    affine = [None] * 9
    for c in range(3):
        affine[3 * c] = 4.0 * take(2, 1 + c)
        affine[3 * c + 1] = 4.0 * take(0, 4 + c)
        affine[3 * c + 2] = 4.0 * take(1, 1 + c)
    old = state[DEF : DEF + 9]
    deform = []
    for r in range(3):
        for c in range(3):
            change = (
                affine[3 * r] * old[c] + affine[3 * r + 1] * old[3 + c] + affine[3 * r + 2] * old[6 + c]
            )
            deform.append(old[3 * r + c] + time_step * change)
    steps = [time_step * velocity[c] for c in range(3)]
    moved = [local[c] + steps[c] for c in range(3)]
    travelled = [state[TRAV + c] + steps[c] for c in range(3)]
    return moved + velocity + deform + affine + [state[MASS], state[VOL]] + travelled


def read_state(ref, rows):
    return [ref[pl.ds(rows * number, rows), :] for number in range(ROWS)]


def write_state(ref, state):
    rows = state[0].shape[0]
    for number in range(ROWS):
        ref[pl.ds(rows * number, rows), :] = state[number]


def first_kernel(
    bins, device_total, blocks, live, x_ref, v_ref, f_ref, c_ref, m_ref, vol_ref,
    state_ref, tiles, message, table, shuffle, device_of,
):
    device = device_of()
    rows = state_ref.shape[0] // ROWS
    quarters = rows // bins
    begin = 0
    for ref, count in ((x_ref, 3), (v_ref, 3), (f_ref, 9), (c_ref, 9)):
        for number in range(count):
            for s in range(rows):
                target = rows * (begin + number) + s
                state_ref[pl.ds(target, 1), :] = ref[
                    pl.ds(number, 1), pl.ds(LANES * s, LANES)
                ]
        begin += count
    for ref, number in ((m_ref, MASS), (vol_ref, VOL)):
        for b in range(bins):
            alive = jnp.where(b < live[0], 1.0, 0.0)
            for q in range(quarters):
                s = quarters * b + q
                piece = ref[pl.ds(LANES * s, LANES)].reshape(1, LANES)
                state_ref[pl.ds(rows * number + s, 1), :] = piece * alive
    home = jnp.zeros((rows, LANES), F32)
    home_y, home_z = home, home
    row_bin = iota((rows, LANES), 0) // quarters
    for b in range(bins):
        block = blocks[b]
        block_y = block // BZ
        block_z = block - BZ * block_y
        home_y = jnp.where(row_bin == b, (4 * block_y).astype(F32), home_y)
        home_z = jnp.where(row_bin == b, (4 * block_z).astype(F32), home_z)
    anchors = (home + (4 * device).astype(F32), home_y, home_z)
    for axis in range(3):
        place = pl.ds(rows * axis, rows)
        state_ref[place, :] = state_ref[place, :] - anchors[axis]
        state_ref[pl.ds(rows * (TRAV + axis), rows), :] = home
    clear_pads(table)
    state = read_state(state_ref, rows)
    to_grid(
        state, state[0:3], blocks, device, bins, device_total, table, shuffle, tiles, message
    )


def middle_kernel(
    bins, device_total, blocks, live, old_ref, old_tiles, received,
    state_ref, tiles, message, table, shuffle, device_of,
):
    device = device_of()
    rows = state_ref.shape[0] // ROWS
    clear_pads(table)
    state = read_state(old_ref, rows)
    state = to_particles(
        state, state[0:3], blocks, device, bins, device_total, old_tiles, received, table,
        shuffle, live,
    )
    write_state(state_ref, state)
    state = read_state(state_ref, rows)
    to_grid(
        state, state[0:3], blocks, device, bins, device_total, table, shuffle, tiles, message
    )


def last_kernel(
    bins, device_total, blocks, live, old_ref, old_tiles, received,
    d_out, v_out, f_out, c_out, table, shuffle, device_of,
):
    device = device_of()
    rows = old_ref.shape[0] // ROWS
    quarters = rows // bins
    clear_pads(table)
    state = read_state(old_ref, rows)
    state = to_particles(
        state, state[0:3], blocks, device, bins, device_total, old_tiles, received, table,
        shuffle, live,
    )
    row_bin = iota((rows, LANES), 0) // quarters
    alive = row_bin < live[0]
    half = rows * LANES
    for ref, begin, count in ((d_out, TRAV, 3), (v_out, VEL, 3), (f_out, DEF, 9), (c_out, AFF, 9)):
        for number in range(count):
            value = jnp.where(alive, state[begin + number], 0.0)
            for s in range(rows):
                ref[pl.ds(number, 1), pl.ds(LANES * s, LANES)] = value[s : s + 1, :]
        total = ref.shape[1]
        ref[:, pl.ds(half, total - half)] = jnp.zeros((count, total - half), F32)


def local(positions, velocity, deformation, affine, particle_mass, volume, bin_block, live_count):
    slot_total = bin_block.shape[0]
    per_bin = positions.shape[1] // slot_total
    bins = slot_total // 2
    device_total = lax.axis_size("space")
    rows = bins * per_bin // LANES
    half = rows * LANES
    nodes = bins * TILE
    state_shape = jax.ShapeDtypeStruct((ROWS * rows, LANES), F32)
    tiles_shape = jax.ShapeDtypeStruct((48, 2 * LANES), F32)
    message_shape = jax.ShapeDtypeStruct((device_total, 16, LANES), F32)
    smem = pl.BlockSpec(memory_space=pltpu.SMEM)
    vmem = pl.BlockSpec(memory_space=pltpu.VMEM)
    scratch = [
        pltpu.VMEM((3 * PITCH, per_bin), F32),
        pltpu.VMEM((4 * 8 * rows, LANES), F32),
    ]
    me = lax.axis_index("space").astype(jnp.int32).reshape(1)

    def call(body, in_specs, out_shape, out_specs, arguments, grid=None):
        def kernel(blocks, live, me_ref, *refs):
            functools.partial(body, bins, device_total, blocks, live)(
                *refs, device_of=lambda: me_ref[0]
            )

        extra = {} if grid is None else {"grid": grid}
        return pl.pallas_call(
            kernel,
            in_specs=[smem, smem, smem] + in_specs,
            out_shape=out_shape,
            out_specs=out_specs,
            scratch_shapes=scratch,
            interpret=INTERPRET,
            **extra,
        )(bin_block, live_count, me, *arguments)

    def first_half(count):
        return pl.BlockSpec((count, half), lambda i: (0, 0))

    flat_half = pl.BlockSpec((half,), lambda i: (0,))
    middle_shapes = (state_shape, tiles_shape, message_shape)
    state, tiles, message = call(
        first_kernel,
        [first_half(3), first_half(3), first_half(9), first_half(9), flat_half, flat_half],
        middle_shapes,
        tuple(
            pl.BlockSpec(shape.shape, lambda i, rank=len(shape.shape): (0,) * rank)
            for shape in middle_shapes
        ),
        (positions, velocity, deformation, affine, particle_mass, volume),
        grid=(1,),
    )
    for step in range(STEPS):
        received = lax.all_to_all(message, "space", 0, 0, tiled=True)
        if step < STEPS - 1:
            state, tiles, message = call(
                middle_kernel, [vmem, vmem, vmem], middle_shapes, (vmem, vmem, vmem),
                (state, tiles, received),
            )
        else:
            total = positions.shape[1]
            out_shape = tuple(jax.ShapeDtypeStruct((count, total), F32) for count in (3, 3, 9, 9))
            return call(
                last_kernel, [vmem, vmem, vmem], out_shape, (vmem,) * 4, (state, tiles, received)
            )


def solution(mesh):
    in_specs = (
        P(None, "space"),
        P(None, "space"),
        P(None, "space"),
        P(None, "space"),
        P("space"),
        P("space"),
        P("space"),
        P("space"),
    )
    out_specs = (P(None, "space"), P(None, "space"), P(None, "space"), P(None, "space"))
    return jax.shard_map(local, mesh=mesh, in_specs=in_specs, out_specs=out_specs, check_vma=False)
```

profile of v0, /device:TPU:0, one launch (start us, length us, event | category | flops | bytes accessed | tf_op | source)
XLA Modules:
  0.0 62.6 jit_solution(4841851968787239390)
XLA Ops:
  1.3 3.4 %shard_map.111 = (f32[464,128]{1,0:T(8,128)}, f32[48,256]{1,0:T(8,128)}, f32[32,16,128]{2,1,0:T(8,128)}) custom-call(s32[8]{0:T(128)} %blocks.7, s32[1]{0:T(128)S(6)} %copy.12.live, s32[1]{0:T(128)} %bitcast.me_ref, f32[3,4096]{1,0:T(4,128)} %refs_0_.1, f32[3,4096]{1,0:T(4,128)} %refs_1_.1, f32[9,4096]{1,0:T(8,128)} %refs_2_.1, f32[9,4096]{1,0:T(8,128)} %refs_3_.1, ...), custom_call_target="tpu_custom_call" | custom-call | tf_op jit(solution)/shard_map/pallas_call | solution.py:502
  4.6 18.0 %all_to_all.15.refs_2_ = f32[32,16,128]{2,1,0:T(8,128)} all-to-all(f32[32,16,128]{2,1,0:T(8,128)} %get-tuple-element.15), channel_id=1, replica_groups=mesh['space'=32] {'space'}, dimensions={0} | all-to-all | bytes 524288 | tf_op jit(solution)/shard_map/all_to_all | solution.py:529
  22.6 4.5 %shard_map.112 = (f32[464,128]{1,0:T(8,128)}, f32[48,256]{1,0:T(8,128)}, f32[32,16,128]{2,1,0:T(8,128)}) custom-call(s32[8]{0:T(128)} %blocks.7, s32[1]{0:T(128)S(6)} %copy.12.live, s32[1]{0:T(128)} %bitcast.me_ref, f32[464,128]{1,0:T(8,128)} %get-tuple-element.13.refs_0_, f32[48,256]{1,0:T(8,128)} %get-tuple-element.14.refs_1_, ...), custom_call_target="tpu_custom_call" | custom-call | tf_op jit(solution)/shard_map/pallas_call | solution.py:502
  27.2 13.9 %all_to_all.16.refs_2_ = f32[32,16,128]{2,1,0:T(8,128)} all-to-all(f32[32,16,128]{2,1,0:T(8,128)} %get-tuple-element.18), channel_id=1, replica_groups=mesh['space'=32] {'space'}, dimensions={0} | all-to-all | bytes 524288 | tf_op jit(solution)/shard_map/all_to_all | solution.py:529
  41.0 4.5 %shard_map.113 = (f32[464,128]{1,0:T(8,128)}, f32[48,256]{1,0:T(8,128)}, f32[32,16,128]{2,1,0:T(8,128)}) custom-call(s32[8]{0:T(128)} %blocks.7, s32[1]{0:T(128)S(6)} %copy.12.live, s32[1]{0:T(128)} %bitcast.me_ref, f32[464,128]{1,0:T(8,128)} %get-tuple-element.16.refs_0_, f32[48,256]{1,0:T(8,128)} %get-tuple-element.17.refs_1_, ...), custom_call_target="tpu_custom_call" | custom-call | tf_op jit(solution)/shard_map/pallas_call | solution.py:502
  45.6 13.9 %all_to_all.17.refs_2_ = f32[32,16,128]{2,1,0:T(8,128)} all-to-all(f32[32,16,128]{2,1,0:T(8,128)} %get-tuple-element.21), channel_id=1, replica_groups=mesh['space'=32] {'space'}, dimensions={0} | all-to-all | bytes 524288 | tf_op jit(solution)/shard_map/all_to_all | solution.py:529
  59.4 3.2 %shard_map.114 = (f32[3,4096]{1,0:T(4,128)}, f32[3,4096]{1,0:T(4,128)}, f32[9,4096]{1,0:T(8,128)}, f32[9,4096]{1,0:T(8,128)}) custom-call(s32[8]{0:T(128)} %blocks.7, s32[1]{0:T(128)S(6)} %copy.12.live, s32[1]{0:T(128)} %bitcast.me_ref, f32[464,128]{1,0:T(8,128)} %get-tuple-element.19.refs_0_, f32[48,256]{1,0:T(8,128)} %get-tuple-element.20.refs_1_, ...), custom_call_target="tpu_custom_call" | custom-call | tf_op jit(solution)/shard_map/pallas_call | solution.py:502
where the time goes:
time: 63 us; the launch traced here: 62.6 us
  blocking collectives  45.7 us (73%)
  Pallas kernels  15.6 us (25%)
  between operations  1.29 us (2%)
    all_to_all x3, blocking collectives, local(): received = lax.all_to_all(message, 'space', 0, 0, tiled=True)  45.7 us
    pallas_call x4, Pallas kernels, call(): pl.pallas_call(kernel, in_specs=[smem, smem, smem] + in_specs, out_shape=...  15.6 us

commit v1 on v0

--- a/solution.py
+++ b/solution.py
@@ -1,5 +1,3 @@
-import functools
-
 import jax
 import jax.numpy as jnp
 from jax import lax
@@ -24,8 +22,8 @@
 TILE = 36
 PITCH = 40
 META = 112
-SPEED = 7
 BIG = 3.0e38
+GRANT = 8 * 2**20
 F32 = jnp.float32
 BF16 = jnp.bfloat16
 INTERPRET = False
@@ -67,11 +65,14 @@
     return jnp.concatenate(parts, axis=1)
 
 
-def bin_weights(local, bin_index, quarters, table):
+def bin_weights(local, bin_index, quarters, table, along):
     along_x, along_y, along_z = [spread(local[axis], bin_index, quarters) for axis in range(3)]
     width = along_x.shape[1]
     first = [spline(float(a) - along_x) for a in range(6)]
     first_moved = [first[a] * (float(a) - along_x) for a in range(6)]
+    for a in range(6):
+        along[pl.ds(16 * bin_index + a, 1), :] = first[a][0:1, :]
+        along[pl.ds(16 * bin_index + 8 + a, 1), :] = first_moved[a][0:1, :]
     third_node = iota((8, width), 0)
     third_offset = third_node.astype(F32) - along_z
     third = jnp.where(third_node < 6, spline(third_offset), 0.0)
@@ -114,16 +115,19 @@
     return stress
 
 
-def to_grid(state, local, blocks, device, bins, device_total, table, shuffle, tiles, message):
+def send_speed(velocity, mass, speeds):
+    speed = velocity[0] * velocity[0] + velocity[1] * velocity[1] + velocity[2] * velocity[2]
+    speed = jnp.max(jnp.where(mass > 0.0, speed, 0.0), axis=0, keepdims=True)
+    speed = jnp.max(speed, axis=1, keepdims=True)
+    speeds[...] = jnp.broadcast_to(speed, speeds.shape)
+
+
+def to_grid(state, device, bins, meta, tiles, near, far, highs, lows, along, table, shuffle):
     rows = state[0].shape[0]
     quarters = rows // bins
     deform = state[DEF : DEF + 9]
     mass, volume = state[MASS], state[VOL]
     velocity = state[VEL : VEL + 3]
-    speed = velocity[0] * velocity[0] + velocity[1] * velocity[1] + velocity[2] * velocity[2]
-    speed = jnp.max(jnp.where(mass > 0.0, speed, 0.0), axis=0, keepdims=True)
-    speed = jnp.max(speed, axis=1, keepdims=True)
-
     stress = kirchhoff(deform)
     scaled = 4.0 * volume
     span = 8 * rows
@@ -145,7 +149,9 @@
             put(1 + axis, 4 + c, scaled * stress[3 * c + axis])
 
     for b in range(bins):
-        first, first_moved = bin_weights(local, b, quarters, table)
+        first, first_moved = bin_weights(state[0:3], b, quarters, table, along)
+        factors = split(table[...])
+        highs[b], lows[b] = factors
 
         def channel(matrix):
             begin = matrix * span + 8 * b * quarters
@@ -171,10 +177,6 @@
             total = product if total is None else total + product
         tiles[:, TILE * b : TILE * (b + 1)] = total[:, 0:TILE]
 
-    lane = iota((1, LANES), 1)
-    meta = jnp.where(lane == SPEED, speed, 0.0)
-    for b in range(bins):
-        meta = jnp.where(lane == b, blocks[b].astype(F32), meta)
     row = iota((8, LANES), 0)
     lanes = iota((8, LANES), 1)
     extra = bins * TILE - LANES
@@ -187,20 +189,11 @@
         folded = jnp.sum(rest, axis=0, keepdims=True)
         return jnp.where(row == 7, jnp.broadcast_to(folded, (8, LANES)), body)
 
-    low = [packed(0), packed(1)]
-    high = [packed(4), packed(5)]
-
-    def send(index, carry):
-        message[index, 0:8, :] = low[0]
-        message[index, 8:16, :] = low[1]
-        return carry
-
-    lax.fori_loop(0, device_total, send, 0)
-
-    @pl.when(device + 1 < device_total)
-    def _():
-        message[device + 1, 0:8, :] = high[0]
-        message[device + 1, 8:16, :] = high[1]
+    odd = device % 2 == 1
+    for half in range(2):
+        low, high = packed(half), packed(4 + half)
+        near[pl.ds(8 * half, 8), :] = jnp.where(odd, low, high)
+        far[pl.ds(8 * half, 8), :] = jnp.where(odd, high, low)
 
 
 def unpacked(block, bins):
@@ -224,89 +217,74 @@
     return 4.0 * block_y + node_y, 4.0 * block_z + node_z
 
 
-def to_particles(state, local, blocks, device, bins, device_total, tiles, received, table, shuffle, live):
+def placing(source_block, column_key, bins):
+    nodes = bins * TILE
+    source = iota((nodes, 1), 0).astype(F32)
+    source_bin = jnp.floor((source + 0.5) * (1.0 / TILE))
+    source_node = source - TILE * source_bin
+    block = jnp.zeros((nodes, 1), F32)
+    for b in range(bins):
+        block = jnp.where(source_bin == float(b), source_block[b], block)
+    row_y, row_z = node_key(block, source_node)
+    return jnp.where(LANES * row_y + row_z == column_key, 1.0, 0.0).astype(BF16)
+
+
+def placed(values, selector):
+    count = values.shape[0]
+    high, low = split(values)
+    result = dot_nn(jnp.concatenate([high, low], axis=0), selector)
+    return result[0:count] + result[count : 2 * count]
+
+
+def halos(near, far, device, device_total):
+    odd = device % 2 == 1
+    near_block, far_block = near[...], far[...]
+    left_block = jnp.where(odd, near_block, far_block)
+    right_block = jnp.where(odd, far_block, near_block)
+    left_block = jnp.where(device > 0, left_block, 0.0)
+    right_block = jnp.where(device + 1 < device_total, right_block, 0.0)
+    return left_block, right_block
+
+
+def halo_blocks(block, bins):
+    lane = iota((1, LANES), 1)
+    return [
+        jnp.max(jnp.where(lane == META + b, block[7:8, :], 0.0), axis=1, keepdims=True)
+        for b in range(bins)
+    ]
+
+
+def to_particles(
+    state, device, bins, device_total, geometry, own, sides, speeds, blocks_around,
+    highs, lows, along, shuffle,
+):
     rows = state[0].shape[0]
     quarters = rows // bins
     width = bins * LANES
     nodes = bins * TILE
-    speeds = jnp.max(received[:, 7, :], axis=0, keepdims=True)
-    lane = iota((1, LANES), 1)
-    fastest = jnp.max(jnp.where(lane == META + SPEED, speeds, 0.0), axis=1, keepdims=True)
+    fastest = jnp.max(speeds[...], axis=0, keepdims=True)
+    fastest = jnp.max(fastest, axis=1, keepdims=True)
     time_step = courant / (jnp.sqrt(fastest) + sound_speed)
 
-    left_index = jnp.maximum(device - 1, 0)
-    right_index = jnp.minimum(device + 1, device_total - 1)
-    left_live = jnp.where(device > 0, 1.0, 0.0)
-    right_live = jnp.where(device + 1 < device_total, 1.0, 0.0)
-    left_block = received[left_index]
-    right_block = received[right_index]
-    left_meta = left_block[7:8, :]
-    right_meta = right_block[7:8, :]
-
-    position = iota((1, width), 1)
-    column_bin = position // LANES
-    column_slot = position - LANES * column_bin
-    column_part = jnp.where(column_slot >= 2 * PITCH, 2, jnp.where(column_slot >= PITCH, 1, 0))
-    column_node = column_slot - PITCH * column_part
-    column_valid = (column_node < TILE) & (column_slot < 3 * PITCH)
-    column_block = jnp.zeros((1, width), F32)
-    for b in range(bins):
-        column_block = jnp.where(column_bin == b, blocks[b].astype(F32), column_block)
-    column_y, column_z = node_key(column_block, column_node.astype(F32))
-    column_key = jnp.where(column_valid, LANES * column_y + column_z, -1.0)
-
-    source = iota((nodes, 1), 0).astype(F32)
-    source_bin = jnp.floor((source + 0.5) * (1.0 / TILE))
-    source_node = source - TILE * source_bin
-
-    def placing(values):
-        source_block = jnp.zeros((nodes, 1), F32)
-        for b in range(bins):
-            source_block = jnp.where(source_bin == float(b), values[b], source_block)
-        row_y, row_z = node_key(source_block, source_node)
-        return jnp.where(LANES * row_y + row_z == column_key, 1.0, 0.0).astype(BF16)
-
-    def meta_values(meta):
-        return [
-            jnp.max(jnp.where(lane == META + b, meta, 0.0), axis=1, keepdims=True)
-            for b in range(bins)
-        ]
-
-    def placed(values, selector):
-        count = values.shape[0]
-        high, low = split(values)
-        result = dot_nn(jnp.concatenate([high, low], axis=0), selector)
-        return result[0:count] + result[count : 2 * count]
-
-    own = placed(tiles[:, 0:nodes], placing([blocks[b].astype(F32) for b in range(bins)]))
-    left_values = jnp.concatenate(
-        [unpacked(left_block[0:8, :], bins), unpacked(left_block[8:16, :], bins)], axis=0
-    )
-    right_values = jnp.concatenate(
-        [unpacked(right_block[0:8, :], bins), unpacked(right_block[8:16, :], bins)], axis=0
-    )
-    left = placed(left_values[:, 0:nodes] * left_live, placing(meta_values(left_meta)))
-    right = placed(right_values[:, 0:nodes] * right_live, placing(meta_values(right_meta)))
+    around = []
+    for side, block in enumerate(blocks_around):
+        values = jnp.concatenate(
+            [unpacked(block[0:8, :], bins), unpacked(block[8:16, :], bins)], axis=0
+        )
+        around.append(placed(values[:, 0:nodes], sides[side]))
+    left, right = around
 
     sub = iota((8, width), 0)
-    wide_y = jnp.broadcast_to(column_y, (8, width))
-    wide_z = jnp.broadcast_to(column_z, (8, width))
-    wide_valid = jnp.broadcast_to(column_key, (8, width)) >= 0.0
+    wide_valid = geometry[0:8, :] >= 0.0
     component = (sub >= 1) & (sub <= 3) & wide_valid
-    floor_of = jnp.where(
-        ((sub == 2) & (wide_y < 2.0)) | ((sub == 3) & (wide_z < 2.0)), 0.0, -BIG
-    )
-    roof_of = jnp.where(
-        ((sub == 2) & (wide_y >= NGY - 2.0)) | ((sub == 3) & (wide_z >= NGZ - 2.0)), 0.0, BIG
-    )
-    pull = time_step * jnp.where(
-        sub == 1, gravity_x, jnp.where(sub == 3, gravity_z, 0.0)
-    )
+    floor_of = geometry[8:16, :]
+    roof_of = geometry[16:24, :]
+    pull = time_step * jnp.where(sub == 1, gravity_x, jnp.where(sub == 3, gravity_z, 0.0))
     plane_total = 4 * device_total
     slot = iota((8, LANES), 1)
     lower_half, upper_half = [], []
     for a in range(6):
-        sums = own[8 * a : 8 * a + 8]
+        sums = own[8 * a : 8 * a + 8, :]
         if a < 2:
             sums = sums + left[8 * a : 8 * a + 8]
         if a >= 4:
@@ -332,20 +310,20 @@
 
     span = 8 * rows
     for b in range(bins):
-        first, first_moved = bin_weights(local, b, quarters, table)
         motions = jnp.concatenate(
             [half[bins * a + b] for a in range(6) for half in (lower_half, upper_half)], axis=0
         )[:, 0 : 3 * PITCH]
         count = motions.shape[0]
         high, low = split(motions)
-        right_high, right_low = split(table[pl.ds(0, 3 * PITCH), :])
-        product = dot_nn(jnp.concatenate([high, low], axis=0), right_high)
-        product = product[0:count] + product[count : 2 * count] + dot_nn(high, right_low)
+        product = dot_nn(jnp.concatenate([high, low], axis=0), highs[b])
+        product = product[0:count] + product[count : 2 * count] + dot_nn(high, lows[b])
         sums = [None, None, None]
         for a in range(6):
             top = product[16 * a : 16 * a + 8]
             bottom = product[16 * a + 8 : 16 * a + 16]
-            terms = (first[a] * top, first[a] * bottom, first_moved[a] * top)
+            weight = jnp.broadcast_to(along[pl.ds(16 * b + a, 1), :], top.shape)
+            weight_moved = jnp.broadcast_to(along[pl.ds(16 * b + 8 + a, 1), :], top.shape)
+            terms = (weight * top, weight * bottom, weight_moved * top)
             sums = [t if s is None else s + t for s, t in zip(sums, terms)]
         for kind in range(3):
             for q in range(quarters):
@@ -370,7 +348,7 @@
             )
             deform.append(old[3 * r + c] + time_step * change)
     steps = [time_step * velocity[c] for c in range(3)]
-    moved = [local[c] + steps[c] for c in range(3)]
+    moved = [state[c] + steps[c] for c in range(3)]
     travelled = [state[TRAV + c] + steps[c] for c in range(3)]
     return moved + velocity + deform + affine + [state[MASS], state[VOL]] + travelled
 
@@ -386,10 +364,9 @@
 
 
 def first_kernel(
-    bins, device_total, blocks, live, x_ref, v_ref, f_ref, c_ref, m_ref, vol_ref,
-    state_ref, tiles, message, table, shuffle, device_of,
+    bins, device_total, blocks, live, device, x_ref, v_ref, f_ref, c_ref, m_ref, vol_ref,
+    state_ref, speeds, tiles, near, far, highs, lows, along, table, shuffle,
 ):
-    device = device_of()
     rows = state_ref.shape[0] // ROWS
     quarters = rows // bins
     begin = 0
@@ -424,42 +401,111 @@
         state_ref[pl.ds(rows * (TRAV + axis), rows), :] = home
     clear_pads(table)
     state = read_state(state_ref, rows)
+    send_speed(state[VEL : VEL + 3], state[MASS], speeds)
+    lane = iota((1, LANES), 1)
+    meta = jnp.zeros((1, LANES), F32)
+    for b in range(bins):
+        meta = jnp.where(lane == b, blocks[b].astype(F32), meta)
     to_grid(
-        state, state[0:3], blocks, device, bins, device_total, table, shuffle, tiles, message
-    )
-
-
-def middle_kernel(
-    bins, device_total, blocks, live, old_ref, old_tiles, received,
-    state_ref, tiles, message, table, shuffle, device_of,
+        state, device, bins, meta, tiles, near, far, highs, lows, along, table, shuffle
+    )
+
+
+def first_own_kernel(bins, device_total, blocks, live, device, tiles, own, geometry, home):
+    width = bins * LANES
+    nodes = bins * TILE
+    position = iota((1, width), 1)
+    column_bin = position // LANES
+    column_slot = position - LANES * column_bin
+    column_part = jnp.where(column_slot >= 2 * PITCH, 2, jnp.where(column_slot >= PITCH, 1, 0))
+    column_node = column_slot - PITCH * column_part
+    column_valid = (column_node < TILE) & (column_slot < 3 * PITCH)
+    own_blocks = [blocks[b].astype(F32) for b in range(bins)]
+    column_block = jnp.zeros((1, width), F32)
+    for b in range(bins):
+        column_block = jnp.where(column_bin == b, own_blocks[b], column_block)
+    column_y, column_z = node_key(column_block, column_node.astype(F32))
+    column_key = jnp.where(column_valid, LANES * column_y + column_z, -1.0)
+    selector = placing(own_blocks, column_key, bins)
+    home[...] = selector
+    own[...] = placed(tiles[:, 0:nodes], selector)
+    sub = iota((8, width), 0)
+    wide_y = jnp.broadcast_to(column_y, (8, width))
+    wide_z = jnp.broadcast_to(column_z, (8, width))
+    geometry[0:8, :] = jnp.broadcast_to(column_key, (8, width))
+    geometry[8:16, :] = jnp.where(
+        ((sub == 2) & (wide_y < 2.0)) | ((sub == 3) & (wide_z < 2.0)), 0.0, -BIG
+    )
+    geometry[16:24, :] = jnp.where(
+        ((sub == 2) & (wide_y >= NGY - 2.0)) | ((sub == 3) & (wide_z >= NGZ - 2.0)), 0.0, BIG
+    )
+
+
+def own_kernel(bins, device_total, live, device, tiles, home, own):
+    own[...] = placed(tiles[:, 0 : bins * TILE], home[...])
+
+
+def second_kernel(
+    bins, device_total, live, device, old_ref, speeds, own, geometry, old_highs, old_lows,
+    old_along, near, far, state_ref, new_speeds, tiles, new_near, new_far, highs, lows, along,
+    sides_ref, table, shuffle,
 ):
-    device = device_of()
+    around = halos(near, far, device, device_total)
+    key = geometry[0:1, :]
+    sides = [placing(halo_blocks(block, bins), key, bins) for block in around]
+    for side in range(2):
+        sides_ref[side] = sides[side]
+    advance(
+        bins, device_total, device, old_ref, speeds, own, geometry, old_highs, old_lows,
+        old_along, around, sides, state_ref, new_speeds, tiles, new_near, new_far, highs, lows,
+        along, table, shuffle,
+    )
+
+
+def later_kernel(
+    bins, device_total, live, device, old_ref, speeds, own, geometry, old_highs, old_lows,
+    old_along, near, far, sides_ref, state_ref, new_speeds, tiles, new_near, new_far, highs, lows,
+    along, table, shuffle,
+):
+    around = halos(near, far, device, device_total)
+    sides = [sides_ref[0], sides_ref[1]]
+    advance(
+        bins, device_total, device, old_ref, speeds, own, geometry, old_highs, old_lows,
+        old_along, around, sides, state_ref, new_speeds, tiles, new_near, new_far, highs, lows,
+        along, table, shuffle,
+    )
+
+
+def advance(
+    bins, device_total, device, old_ref, speeds, own, geometry, old_highs, old_lows,
+    old_along, around, sides, state_ref, new_speeds, tiles, near, far, highs, lows, along,
+    table, shuffle,
+):
     rows = state_ref.shape[0] // ROWS
     clear_pads(table)
     state = read_state(old_ref, rows)
     state = to_particles(
-        state, state[0:3], blocks, device, bins, device_total, old_tiles, received, table,
-        shuffle, live,
+        state, device, bins, device_total, geometry, own, sides, speeds, around, old_highs,
+        old_lows, old_along, shuffle,
     )
     write_state(state_ref, state)
-    state = read_state(state_ref, rows)
+    send_speed(state[VEL : VEL + 3], state[MASS], new_speeds)
     to_grid(
-        state, state[0:3], blocks, device, bins, device_total, table, shuffle, tiles, message
+        state, device, bins, jnp.zeros((1, LANES), F32), tiles, near, far, highs, lows, along,
+        table, shuffle,
     )
 
 
 def last_kernel(
-    bins, device_total, blocks, live, old_ref, old_tiles, received,
-    d_out, v_out, f_out, c_out, table, shuffle, device_of,
+    bins, device_total, live, device, old_ref, speeds, own, geometry, highs, lows, along,
+    near, far, sides_ref, d_out, v_out, f_out, c_out, shuffle,
 ):
-    device = device_of()
     rows = old_ref.shape[0] // ROWS
     quarters = rows // bins
-    clear_pads(table)
     state = read_state(old_ref, rows)
     state = to_particles(
-        state, state[0:3], blocks, device, bins, device_total, old_tiles, received, table,
-        shuffle, live,
+        state, device, bins, device_total, geometry, own, [sides_ref[0], sides_ref[1]], speeds,
+        halos(near, far, device, device_total), highs, lows, along, shuffle,
     )
     row_bin = iota((rows, LANES), 0) // quarters
     alive = row_bin < live[0]
@@ -481,63 +527,115 @@
     rows = bins * per_bin // LANES
     half = rows * LANES
     nodes = bins * TILE
-    state_shape = jax.ShapeDtypeStruct((ROWS * rows, LANES), F32)
-    tiles_shape = jax.ShapeDtypeStruct((48, 2 * LANES), F32)
-    message_shape = jax.ShapeDtypeStruct((device_total, 16, LANES), F32)
+    width = bins * LANES
+    nodes = bins * TILE
+    held = [
+        ((ROWS * rows, LANES), F32),
+        ((device_total, LANES), F32),
+        ((48, 2 * LANES), F32),
+        ((16, LANES), F32),
+        ((16, LANES), F32),
+        ((bins, 3 * PITCH, per_bin), BF16),
+        ((bins, 3 * PITCH, per_bin), BF16),
+        ((16 * bins, per_bin), F32),
+    ]
+    own_shape = ((48, width), F32)
+    geometry_shape = ((24, width), F32)
+    home_shape = ((nodes, width), BF16)
+    sides_shape = ((2, nodes, width), BF16)
     smem = pl.BlockSpec(memory_space=pltpu.SMEM)
     vmem = pl.BlockSpec(memory_space=pltpu.VMEM)
-    scratch = [
-        pltpu.VMEM((3 * PITCH, per_bin), F32),
-        pltpu.VMEM((4 * 8 * rows, LANES), F32),
-    ]
+    table = pltpu.VMEM((3 * PITCH, per_bin), F32)
+    shuffle = pltpu.VMEM((4 * 8 * rows, LANES), F32)
+    bin_block = bin_block if INTERPRET else pltpu.with_memory_space_constraint(bin_block, pltpu.HBM)
     me = lax.axis_index("space").astype(jnp.int32).reshape(1)
 
-    def call(body, in_specs, out_shape, out_specs, arguments, grid=None):
-        def kernel(blocks, live, me_ref, *refs):
-            functools.partial(body, bins, device_total, blocks, live)(
-                *refs, device_of=lambda: me_ref[0]
+    def stay(array, space=pltpu.VMEM):
+        return array if INTERPRET else pltpu.with_memory_space_constraint(array, space)
+
+    def call(body, scalars, arguments, outputs, scratch, in_specs=None, final=False):
+        def kernel(*refs):
+            count = len(scalars)
+            body(bins, device_total, *refs[: count - 1], refs[count - 1][0], *refs[count:])
+
+        extra = {}
+        out_specs = tuple(vmem for _ in outputs)
+        if in_specs is None:
+            in_specs = [vmem] * len(arguments)
+            arguments = [stay(argument) for argument in arguments]
+        else:
+            arguments = [stay(argument, pltpu.HBM) for argument in arguments]
+            out_specs = tuple(
+                pl.BlockSpec(shape, lambda i, rank=len(shape): (0,) * rank)
+                for shape, _ in outputs
             )
-
-        extra = {} if grid is None else {"grid": grid}
+            extra = {"grid": (1,)}
+        make = jax.ShapeDtypeStruct if final or INTERPRET else pltpu.VMEM
         return pl.pallas_call(
             kernel,
-            in_specs=[smem, smem, smem] + in_specs,
-            out_shape=out_shape,
+            in_specs=[smem] * len(scalars) + in_specs,
+            out_shape=tuple(make(shape, kind) for shape, kind in outputs),
             out_specs=out_specs,
             scratch_shapes=scratch,
             interpret=INTERPRET,
+            compiler_params=pltpu.CompilerParams(vmem_limit_bytes=GRANT),
             **extra,
-        )(bin_block, live_count, me, *arguments)
+        )(*scalars, *arguments)
 
     def first_half(count):
         return pl.BlockSpec((count, half), lambda i: (0, 0))
 
     flat_half = pl.BlockSpec((half,), lambda i: (0,))
-    middle_shapes = (state_shape, tiles_shape, message_shape)
-    state, tiles, message = call(
+    length = device_total
+    swap_pairs = [(i, i ^ 1) for i in range(length)]
+    cross_pairs = [(i, i + 1) for i in range(1, length - 1, 2)]
+    cross_pairs = cross_pairs + [(j, i) for i, j in cross_pairs]
+
+    def exchange(speeds, near, far):
+        far = lax.ppermute(far, "space", cross_pairs)
+        speeds = lax.all_to_all(speeds, "space", 0, 0, tiled=True)
+        near = lax.ppermute(near, "space", swap_pairs)
+        return speeds, near, far
+
+    state, speeds, tiles, near, far, highs, lows, along = call(
         first_kernel,
+        (bin_block, live_count, me),
+        (positions, velocity, deformation, affine, particle_mass, volume),
+        held,
+        [table, shuffle],
         [first_half(3), first_half(3), first_half(9), first_half(9), flat_half, flat_half],
-        middle_shapes,
-        tuple(
-            pl.BlockSpec(shape.shape, lambda i, rank=len(shape.shape): (0,) * rank)
-            for shape in middle_shapes
-        ),
-        (positions, velocity, deformation, affine, particle_mass, volume),
-        grid=(1,),
-    )
-    for step in range(STEPS):
-        received = lax.all_to_all(message, "space", 0, 0, tiled=True)
-        if step < STEPS - 1:
-            state, tiles, message = call(
-                middle_kernel, [vmem, vmem, vmem], middle_shapes, (vmem, vmem, vmem),
-                (state, tiles, received),
-            )
-        else:
-            total = positions.shape[1]
-            out_shape = tuple(jax.ShapeDtypeStruct((count, total), F32) for count in (3, 3, 9, 9))
-            return call(
-                last_kernel, [vmem, vmem, vmem], out_shape, (vmem,) * 4, (state, tiles, received)
-            )
+    )
+    speeds, near, far = exchange(speeds, near, far)
+    own, geometry, home = call(
+        first_own_kernel,
+        (bin_block, live_count, me),
+        (tiles,),
+        [own_shape, geometry_shape, home_shape],
+        [],
+    )
+    sides = ()
+    for step in range(STEPS - 1):
+        results = call(
+            second_kernel if step == 0 else later_kernel,
+            (live_count, me),
+            (state, speeds, own, geometry, highs, lows, along, near, far, *sides),
+            held + ([sides_shape] if step == 0 else []),
+            [table, shuffle],
+        )
+        state, speeds, tiles, near, far, highs, lows, along = results[:8]
+        if step == 0:
+            sides = results[8:]
+        speeds, near, far = exchange(speeds, near, far)
+        (own,) = call(own_kernel, (live_count, me), (tiles, home), [own_shape], [])
+    total = positions.shape[1]
+    return call(
+        last_kernel,
+        (live_count, me),
+        (state, speeds, own, geometry, highs, lows, along, near, far, *sides),
+        [((count, total), F32) for count in (3, 3, 9, 9)],
+        [shuffle],
+        final=True,
+    )
 
 
 def solution(mesh):

time: 63 us -> 50 us (0.79)
  blocking collectives: 45.7 us -> 0 us
  starting transfers between devices: 0 us -> 19.6 us
  waiting for transfers between devices: 0 us -> 17.1 us
  Pallas kernels: 15.6 us -> 11.6 us
    all_to_all x3 -> x0, blocking collectives: 45.7 us -> none  [local(): received = lax.all_to_all(message, 'space', 0, 0, tiled=True)]
    all_to_all x0 -> x3, waiting for transfers between devices: none -> 16.9 us  [exchange(): speeds = lax.all_to_all(speeds, 'space', 0, 0, tiled=True)]
    all_to_all x0 -> x3, starting transfers between devices: none -> 16.7 us  [exchange(): speeds = lax.all_to_all(speeds, 'space', 0, 0, tiled=True)]
    pallas_call x4 -> x7, Pallas kernels: 15.6 us -> 11.6 us  [call(): pl.pallas_call(kernel, in_specs=[smem] * len(scalars) + in_specs, out_sha...]
    ppermute x0 -> x6, starting transfers between devices: none -> 2.9 us  [the longest x3 1.95 us: exchange(): far = lax.ppermute(far, 'space', cross_pairs)]
  transfers between devices with their start and end apart: 0 -> 9, of which waited for: 0 -> 5; matrix products, arithmetic and copies ran while one was open for 0% -> 0% of each run, Pallas kernels for 0% -> 2%
where the time goes in v1:
time: 50 us; the launch traced here: 49.7 us
  starting transfers between devices  19.6 us (39%)
  waiting for transfers between devices  17.1 us (34%)
  Pallas kernels  11.6 us (23%)
  between operations  1.36 us (3%)
    all_to_all x3, waiting for transfers between devices, exchange(): speeds = lax.all_to_all(speeds, 'space', 0, 0, tiled=True)  16.9 us
    all_to_all x3, starting transfers between devices, exchange(): speeds = lax.all_to_all(speeds, 'space', 0, 0, tiled=True)  16.7 us
    pallas_call x7, Pallas kernels, call(): pl.pallas_call(kernel, in_specs=[smem] * len(scalars) + in_specs, out_sha...  11.6 us
    ppermute x3, starting transfers between devices, exchange(): far = lax.ppermute(far, 'space', cross_pairs)  1.95 us
  transfers between devices with their start and end apart: 9, of which 5 were waited for; matrix products, arithmetic and copies ran while one was open for 0% of the time, Pallas kernels for 2%

profile of v1, /device:TPU:0, one launch (start us, length us, event | category | flops | bytes accessed | tf_op | source)
XLA Modules:
  0.0 49.7 jit_solution(15079399146408455881)
XLA Ops:
  1.3 3.1 %shard_map.111 = (f32[464,128]{1,0:T(8,128)S(1)}, f32[32,128]{1,0:T(8,128)}, f32[48,256]{1,0:T(8,128)S(1)}, f32[16,128]{1,0:T(8,128)S(1)}, f32[16,128]{1,0:T(8,1...) custom-call(s32[8]{0:T(128)} %refs_0_.8, ...), custom_call_target="tpu_custom_call" | custom-call | tf_op jit(solution)/shard_map/pallas_call | solution.py:574
  4.4 7.3 %all-to-all-start = ((f32[32,1,128]{2,1,0:T(1,128)}), f32[32,1,128]{2,1,0:T(1,128)S(1)}, u32[]{:S(2)}, u32[]{:S(2)}) async-start(f32[32,1,128]{2,1,0:T(1,128)} %bitcast.2), calls=%async_computation | async-start | bytes 32768 | tf_op jit(solution)/shard_map/all_to_all | solution.py:596
  11.8 0.3 collective-permute-start
  12.1 0.6 %collective-permute-start.1 = (f32[16,128]{1,0:T(8,128)S(1)}, f32[16,128]{1,0:T(8,128)S(1)}, u32[]{:S(2)}, u32[]{:S(2)}) collective-permute-start(f32[16,128]{1,0:T(8,128)S(1)} %get-tuple-element.41), channel_id=1, source_target_pairs={{1,2},{3,4},{5,6},{7,8},{9,10},{11,12},{13,14},{15,16},{17,18},{19... | collective-permute-start | bytes 24584 | tf_op jit(solution)/shard_map/ppermute | solution.py:595
  12.7 0.9 %shard_map.112 = (f32[48,512]{1,0:T(8,128)S(1)}, f32[24,512]{1,0:T(8,128)S(1)}, bf16[144,512]{1,0:T(8,128)(2,1)S(1)}) custom-call(s32[8]{0:T(128)} %refs_0_.8, s32[1]{0:T(128)S(6)} %copy.15.refs_1_.refs_0_, s32[1]{0:T(128)} %bitcast.refs_2_.refs_1_, f32[48,256]{1,0:T(8,128)S(1)} %get-tuple-element.34.refs_3_), custom_call_target="tpu_custom_call" | custom-call | tf_op jit(solution)/shard_map/pallas_call | solution.py:574
  13.7 0.0 collective-permute-done.refs_9_
  13.7 0.0 collective-permute-done.1.refs_10_
  13.7 5.2 %all-to-all-done = f32[32,1,128]{2,1,0:T(1,128)S(1)} async-done(((f32[32,1,128]{2,1,0:T(1,128)}), f32[32,1,128]{2,1,0:T(1,128)S(1)}, u32[]{:S(2)}, u32[]{:S(2)}) %all-to-all-start) | async-done | bytes 16416 | tf_op jit(solution)/shard_map/all_to_all | solution.py:596
  18.9 2.8 %shard_map.113 = (f32[464,128]{1,0:T(8,128)S(1)}, f32[32,128]{1,0:T(8,128)}, f32[48,256]{1,0:T(8,128)S(1)}, f32[16,128]{1,0:T(8,128)S(1)}, f32[16,128]{1,0:T(8,1...) custom-call(s32[1]{0:T(128)S(6)} %copy.15.refs_1_.refs_0_, ...), custom_call_target="tpu_custom_call" | custom-call | tf_op jit(solution)/shard_map/pallas_call | solution.py:574
  21.7 4.7 %all-to-all-start.1 = ((f32[32,1,128]{2,1,0:T(1,128)}), f32[32,1,128]{2,1,0:T(1,128)S(1)}, u32[]{:S(2)}, u32[]{:S(2)}) async-start(f32[32,1,128]{2,1,0:T(1,128)} %bitcast.5), calls=%async_computation.1 | async-start | bytes 32768 | tf_op jit(solution)/shard_map/all_to_all | solution.py:596
  26.4 0.3 collective-permute-start.2
  26.7 0.6 %collective-permute-start.3 = (f32[16,128]{1,0:T(8,128)S(1)}, f32[16,128]{1,0:T(8,128)S(1)}, u32[]{:S(2)}, u32[]{:S(2)}) collective-permute-start(f32[16,128]{1,0:T(8,128)S(1)} %get-tuple-element.50), channel_id=1, source_target_pairs={{1,2},{3,4},{5,6},{7,8},{9,10},{11,12},{13,14},{15,16},{17,18},{19... | collective-permute-start | bytes 24584 | tf_op jit(solution)/shard_map/ppermute | solution.py:595
  27.3 0.1 shard_map.114.refs_4_
  27.5 0.1 collective-permute-done.2.refs_9_
  27.6 0.0 collective-permute-done.3.refs_10_
  27.6 5.9 %all-to-all-done.1 = f32[32,1,128]{2,1,0:T(1,128)S(1)} async-done(((f32[32,1,128]{2,1,0:T(1,128)}), f32[32,1,128]{2,1,0:T(1,128)S(1)}, u32[]{:S(2)}, u32[]{:S(2)}) %all-to-all-start.1) | async-done | bytes 16416 | tf_op jit(solution)/shard_map/all_to_all | solution.py:596
  33.5 2.8 %shard_map.115 = (f32[464,128]{1,0:T(8,128)S(1)}, f32[32,128]{1,0:T(8,128)}, f32[48,256]{1,0:T(8,128)S(1)}, f32[16,128]{1,0:T(8,128)S(1)}, f32[16,128]{1,0:T(8,1...) custom-call(s32[1]{0:T(128)S(6)} %copy.15.refs_1_.refs_0_, ...), custom_call_target="tpu_custom_call" | custom-call | tf_op jit(solution)/shard_map/pallas_call | solution.py:574
  36.2 4.7 %all-to-all-start.2 = ((f32[32,1,128]{2,1,0:T(1,128)}), f32[32,1,128]{2,1,0:T(1,128)S(1)}, u32[]{:S(2)}, u32[]{:S(2)}) async-start(f32[32,1,128]{2,1,0:T(1,128)} %bitcast.8), calls=%async_computation.2 | async-start | bytes 32768 | tf_op jit(solution)/shard_map/all_to_all | solution.py:596
  40.9 0.3 collective-permute-start.4
  41.3 0.6 %collective-permute-start.5 = (f32[16,128]{1,0:T(8,128)S(1)}, f32[16,128]{1,0:T(8,128)S(1)}, u32[]{:S(2)}, u32[]{:S(2)}) collective-permute-start(f32[16,128]{1,0:T(8,128)S(1)} %get-tuple-element.59), channel_id=1, source_target_pairs={{1,2},{3,4},{5,6},{7,8},{9,10},{11,12},{13,14},{15,16},{17,18},{19... | collective-permute-start | bytes 24584 | tf_op jit(solution)/shard_map/ppermute | solution.py:595
  41.9 0.1 shard_map.116.refs_4_
  42.1 0.1 collective-permute-done.4.refs_9_
  42.2 0.0 collective-permute-done.5.refs_10_
  42.2 5.9 %all-to-all-done.2 = f32[32,1,128]{2,1,0:T(1,128)S(1)} async-done(((f32[32,1,128]{2,1,0:T(1,128)}), f32[32,1,128]{2,1,0:T(1,128)S(1)}, u32[]{:S(2)}, u32[]{:S(2)}) %all-to-all-start.2) | async-done | bytes 16416 | tf_op jit(solution)/shard_map/all_to_all | solution.py:596
  48.0 1.7 %shard_map.117 = (f32[3,4096]{1,0:T(4,128)}, f32[3,4096]{1,0:T(4,128)}, f32[9,4096]{1,0:T(8,128)}, f32[9,4096]{1,0:T(8,128)}) custom-call(s32[1]{0:T(128)S(6)} %copy.15.refs_1_.refs_0_, s32[1]{0:T(128)} %bitcast.refs_2_.refs_1_, f32[464,128]{1,0:T(8,128)S(1)} %get-tuple-element.52.refs_2_, f32[32,128]{1,0:T(8,128)S(1)} %bitcast.15, ...), custom_call_target="tpu_custom_call" | custom-call | tf_op jit(solution)/shard_map/pallas_call | solution.py:574
Async XLA Ops:
  4.4 14.4 %all-to-all-start = ((f32[32,1,128]{2,1,0:T(1,128)}), f32[32,1,128]{2,1,0:T(1,128)S(1)}, u32[]{:S(2)}, u32[]{:S(2)}) async-start(f32[32,1,128]{2,1,0:T(1,128)} %bitcast.2), calls=%async_computation | async-start | bytes 32768 | tf_op jit(solution)/shard_map/all_to_all | solution.py:596
  11.8 1.9 %collective-permute-start = (f32[16,128]{1,0:T(8,128)S(1)}, f32[16,128]{1,0:T(8,128)S(1)}, u32[]{:S(2)}, u32[]{:S(2)}) collective-permute-start(f32[16,128]{1,0:T(8,128)S(1)} %get-tuple-element.40), channel_id=1, source_target_pairs={{0,1},{1,0},{2,3},{3,2},{4,5},{5,4},{6,7},{7,6},{8,9},{9,8},{10,11... | collective-permute-start | bytes 24584 | tf_op jit(solution)/shard_map/ppermute | solution.py:597
  12.1 1.6 %collective-permute-start.1 = (f32[16,128]{1,0:T(8,128)S(1)}, f32[16,128]{1,0:T(8,128)S(1)}, u32[]{:S(2)}, u32[]{:S(2)}) collective-permute-start(f32[16,128]{1,0:T(8,128)S(1)} %get-tuple-element.41), channel_id=1, source_target_pairs={{1,2},{3,4},{5,6},{7,8},{9,10},{11,12},{13,14},{15,16},{17,18},{19... | collective-permute-start | bytes 24584 | tf_op jit(solution)/shard_map/ppermute | solution.py:595
  21.7 11.8 %all-to-all-start.1 = ((f32[32,1,128]{2,1,0:T(1,128)}), f32[32,1,128]{2,1,0:T(1,128)S(1)}, u32[]{:S(2)}, u32[]{:S(2)}) async-start(f32[32,1,128]{2,1,0:T(1,128)} %bitcast.5), calls=%async_computation.1 | async-start | bytes 32768 | tf_op jit(solution)/shard_map/all_to_all | solution.py:596
  26.4 1.2 %collective-permute-start.2 = (f32[16,128]{1,0:T(8,128)S(1)}, f32[16,128]{1,0:T(8,128)S(1)}, u32[]{:S(2)}, u32[]{:S(2)}) collective-permute-start(f32[16,128]{1,0:T(8,128)S(1)} %get-tuple-element.49), channel_id=1, source_target_pairs={{0,1},{1,0},{2,3},{3,2},{4,5},{5,4},{6,7},{7,6},{8,9},{9,8},{10,11... | collective-permute-start | bytes 24584 | tf_op jit(solution)/shard_map/ppermute | solution.py:597
  26.7 0.9 %collective-permute-start.3 = (f32[16,128]{1,0:T(8,128)S(1)}, f32[16,128]{1,0:T(8,128)S(1)}, u32[]{:S(2)}, u32[]{:S(2)}) collective-permute-start(f32[16,128]{1,0:T(8,128)S(1)} %get-tuple-element.50), channel_id=1, source_target_pairs={{1,2},{3,4},{5,6},{7,8},{9,10},{11,12},{13,14},{15,16},{17,18},{19... | collective-permute-start | bytes 24584 | tf_op jit(solution)/shard_map/ppermute | solution.py:595
  36.2 11.8 %all-to-all-start.2 = ((f32[32,1,128]{2,1,0:T(1,128)}), f32[32,1,128]{2,1,0:T(1,128)S(1)}, u32[]{:S(2)}, u32[]{:S(2)}) async-start(f32[32,1,128]{2,1,0:T(1,128)} %bitcast.8), calls=%async_computation.2 | async-start | bytes 32768 | tf_op jit(solution)/shard_map/all_to_all | solution.py:596
  40.9 1.2 %collective-permute-start.4 = (f32[16,128]{1,0:T(8,128)S(1)}, f32[16,128]{1,0:T(8,128)S(1)}, u32[]{:S(2)}, u32[]{:S(2)}) collective-permute-start(f32[16,128]{1,0:T(8,128)S(1)} %get-tuple-element.58), channel_id=1, source_target_pairs={{0,1},{1,0},{2,3},{3,2},{4,5},{5,4},{6,7},{7,6},{8,9},{9,8},{10,11... | collective-permute-start | bytes 24584 | tf_op jit(solution)/shard_map/ppermute | solution.py:597
  41.3 0.9 %collective-permute-start.5 = (f32[16,128]{1,0:T(8,128)S(1)}, f32[16,128]{1,0:T(8,128)S(1)}, u32[]{:S(2)}, u32[]{:S(2)}) collective-permute-start(f32[16,128]{1,0:T(8,128)S(1)} %get-tuple-element.59), channel_id=1, source_target_pairs={{1,2},{3,4},{5,6},{7,8},{9,10},{11,12},{13,14},{15,16},{17,18},{19... | collective-permute-start | bytes 24584 | tf_op jit(solution)/shard_map/ppermute | solution.py:595

commit v2 on v1

v2 whole, which is shorter than its diff:
```python
import jax
import jax.numpy as jnp
from jax import lax
from jax.experimental import pallas as pl
from jax.experimental.pallas import tpu as pltpu
from jax.sharding import PartitionSpec as P


BZ = 16
STEPS = 3
NGY = 66
NGZ = 66

mu_shear = 4.0
lame_first = 6.0
courant = 0.15
sound_speed = 3.7416573867739413
mass_floor = 0.05
gravity_x = 3.0
gravity_z = -9.0

LANES = 128
TILE = 48
SLOT = 64
META = 64
BIG = 3.0e38
GRANT = 8 * 2**20
F32 = jnp.float32
BF16 = jnp.bfloat16
INTERPRET = False

POS, DEF, MASS, VOL, TRAV = 0, 3, 12, 13, 14
ROWS = 17


def iota(shape, dim):
    return lax.broadcasted_iota(jnp.int32, shape, dim)


def split(value):
    high = value.astype(BF16)
    low = (value - high.astype(F32)).astype(BF16)
    return high, low


def dot_nt(a, b):
    return lax.dot_general(a, b, (((1,), (1,)), ((), ())), preferred_element_type=F32)


def dot_nn(a, b):
    return lax.dot_general(a, b, (((1,), (0,)), ((), ())), preferred_element_type=F32)


def spline(distance):
    magnitude = jnp.abs(distance)
    outer = jnp.maximum(1.5 - magnitude, 0.0)
    inner = jnp.maximum(0.5 - magnitude, 0.0)
    return 0.5 * outer * outer - 1.5 * inner * inner


def spread(ref, row, quarters):
    return jnp.concatenate(
        [ref[pl.ds(row + q, 8, stride=0), :] for q in range(quarters)], axis=1
    )


def dense_weights(position, ref):
    rows = position.shape[0]
    for a in range(6):
        offset = float(a) - position
        weight = spline(offset)
        ref[pl.ds(rows * a, rows), :] = weight
        ref[pl.ds(rows * (6 + a), rows), :] = weight * offset


def pair_weights(state_ref, across, row, span):
    rows = across.shape[0] // 12
    along_z = spread(state_ref, 2 * rows + row, span)
    third_node = iota(along_z.shape, 0)
    third_offset = third_node.astype(F32) - along_z
    third = jnp.where(third_node < 6, spline(third_offset), 0.0)
    third_moved = third * third_offset
    plain, moved_y, moved_z = [], [], []
    for a in range(6):
        second = spread(across, rows * a + row, span)
        second_moved = spread(across, rows * (6 + a) + row, span)
        plain.append(second * third)
        moved_y.append(second_moved * third)
        moved_z.append(second * third_moved)
    return [jnp.concatenate(part, axis=0) for part in (plain, moved_y, moved_z)]


def kirchhoff(deform):
    determinant = (
        deform[0] * (deform[4] * deform[8] - deform[5] * deform[7])
        - deform[1] * (deform[3] * deform[8] - deform[5] * deform[6])
        + deform[2] * (deform[3] * deform[7] - deform[4] * deform[6])
    )
    pressure = lame_first * (determinant - 1.0) * determinant
    stress = [None] * 9
    for r in range(3):
        for c in range(r, 3):
            product = (
                deform[3 * r] * deform[3 * c]
                + deform[3 * r + 1] * deform[3 * c + 1]
                + deform[3 * r + 2] * deform[3 * c + 2]
            )
            if r == c:
                stress[3 * r + c] = mu_shear * (product - 1.0) + pressure
            else:
                stress[3 * r + c] = mu_shear * product
                stress[3 * c + r] = stress[3 * r + c]
    return stress


def send_speed(velocity, mass, speeds, outbox, sem):
    speed = velocity[0] * velocity[0] + velocity[1] * velocity[1] + velocity[2] * velocity[2]
    speed = jnp.max(jnp.where(mass > 0.0, speed, 0.0), axis=0, keepdims=True)
    speed = jnp.max(speed, axis=1, keepdims=True)
    outbox[...] = jnp.broadcast_to(speed, outbox.shape)
    copy = pltpu.make_async_copy(outbox, speeds, sem)
    copy.start()
    return copy


def halves(quarters):
    parts = 2 if quarters % 2 == 0 else 1
    span = quarters // parts
    return [(part * span, span, pl.ds(part * span * LANES, span * LANES)) for part in range(parts)]


def plane_sums(planes, row, span, channels, along, tables):
    rows = along.shape[0] // 12

    def channel(matrix):
        begin = 8 * (matrix * rows + row)
        return jnp.concatenate(
            [channels[pl.ds(begin + 8 * q, 8), :] for q in range(span)], axis=1
        )

    base, slope_x, slope_y, slope_z = [channel(matrix) for matrix in range(4)]
    pieces = ([], [], [])
    for a in planes:
        first = spread(along, rows * a + row, span)
        first_moved = spread(along, rows * (6 + a) + row, span)
        pieces[0].append(first * base + first_moved * slope_x)
        pieces[1].append(first * slope_y)
        pieces[2].append(first * slope_z)
    count = 8 * len(planes)
    total = None
    for piece, (right_high, right_low) in zip(pieces, tables):
        left_high, left_low = split(jnp.concatenate(piece, axis=0))
        both = dot_nt(jnp.concatenate([left_high, left_low], axis=0), right_high)
        product = both[0:count] + both[count : 2 * count] + dot_nt(left_high, right_low)
        total = product if total is None else total + product
    return total


def far_planes(device):
    return 4 * (device % 2)


def to_grid(
    state, velocity, affine, state_ref, device, bins, meta, far, highs, lows, along, channels, across
):
    rows = state[0].shape[0]
    quarters = rows // bins
    deform = state[DEF : DEF + 9]
    mass, volume = state[MASS], state[VOL]
    stress = kirchhoff(deform)
    scaled = 4.0 * volume
    span = 8 * rows
    zero = jnp.zeros((rows, LANES), F32)

    def put(matrix, row, value):
        channels[pl.ds(matrix * span + row, rows, stride=8), :] = value

    put(0, 0, mass)
    for c in range(3):
        put(0, 1 + c, mass * velocity[c])
        put(0, 4 + c, zero)
    put(0, 7, zero)
    for axis in range(3):
        put(1 + axis, 0, zero)
        put(1 + axis, 7, zero)
        for c in range(3):
            put(1 + axis, 1 + c, mass * affine[3 * c + axis])
            put(1 + axis, 4 + c, scaled * stress[3 * c + axis])
    dense_weights(state[0], along)
    dense_weights(state[1], across)
    base = far_planes(device)
    for b in range(bins):
        total = None
        for begin, width, lanes in halves(quarters):
            row = b * quarters + begin
            tables = []
            for kind, values in enumerate(pair_weights(state_ref, across, row, width)):
                high, low = split(values)
                highs[b, pl.ds(kind * TILE, TILE), lanes] = high
                lows[b, pl.ds(kind * TILE, TILE), lanes] = low
                tables.append((high, low))
            sums = plane_sums((base, base + 1), row, width, channels, along, tables)
            total = sums if total is None else total + sums
        far[:, TILE * b : TILE * (b + 1)] = total
    nodes = bins * TILE
    width = far.shape[1]
    if meta is None:
        meta = jnp.zeros((1, width), F32)
    far[:, nodes:width] = jnp.broadcast_to(meta, (16, width))[:, nodes:width]


def rest_of_grid(device, bins, meta, far, highs, lows, along, channels, near):
    rows = along.shape[0] // 12
    quarters = rows // bins
    odd = device % 2 == 1
    base = 4 - far_planes(device)
    middle = []
    for b in range(bins):
        total = None
        for begin, width, lanes in halves(quarters):
            row = b * quarters + begin
            tables = [
                (highs[b, pl.ds(kind * TILE, TILE), lanes], lows[b, pl.ds(kind * TILE, TILE), lanes])
                for kind in range(3)
            ]
            sums = plane_sums((base, base + 1, 2, 3), row, width, channels, along, tables)
            total = sums if total is None else total + sums
        near[:, TILE * b : TILE * (b + 1)] = total[0:16]
        middle.append(total[16:32])
    nodes = bins * TILE
    width = near.shape[1]
    if meta is None:
        meta = jnp.zeros((1, width), F32)
    near[:, nodes:width] = jnp.broadcast_to(meta, (16, width))[:, nodes:width]
    near_part, far_part = near[:, 0:nodes], far[:, 0:nodes]
    low = jnp.where(odd, near_part, far_part)
    high = jnp.where(odd, far_part, near_part)
    return low, middle, high


def node_key(block, node):
    block_y = jnp.floor((block + 0.5) * (1.0 / BZ))
    block_z = block - BZ * block_y
    node_y = jnp.floor((node + 0.5) * (1.0 / 8.0))
    node_z = node - 8.0 * node_y
    return 4.0 * block_y + node_y, 4.0 * block_z + node_z


def placing(source_block, column_key, bins):
    nodes = bins * TILE
    source = iota((nodes, 1), 0).astype(F32)
    source_bin = jnp.floor((source + 0.5) * (1.0 / TILE))
    source_node = source - TILE * source_bin
    block = jnp.zeros((nodes, 1), F32)
    for b in range(bins):
        block = jnp.where(source_bin == float(b), source_block[b], block)
    row_y, row_z = node_key(block, source_node)
    row_key = LANES * row_y + row_z
    used = source_node - 8.0 * jnp.floor((source_node + 0.5) * (1.0 / 8.0)) < 6.0
    row_key = jnp.where(used, row_key, -2.0)
    return jnp.where(row_key == column_key, 1.0, 0.0).astype(BF16)


def placed(values, selector):
    count = values.shape[0]
    high, low = split(values)
    result = dot_nn(jnp.concatenate([high, low], axis=0), selector)
    return result[0:count] + result[count : 2 * count]


def halos(near, far, device, device_total):
    odd = device % 2 == 1
    near_block, far_block = near[...], far[...]
    left_block = jnp.where(odd, near_block, far_block)
    right_block = jnp.where(odd, far_block, near_block)
    left_block = jnp.where(device > 0, left_block, 0.0)
    right_block = jnp.where(device + 1 < device_total, right_block, 0.0)
    return left_block, right_block


def halo_blocks(block, bins):
    lane = iota((1, LANES), 1)
    return [
        jnp.max(jnp.where(lane == META + b, block[7:8, LANES : 2 * LANES], 0.0), axis=1, keepdims=True)
        for b in range(bins)
    ]


def to_particles(
    state, device, bins, device_total, geometry, own, sides, speeds, blocks_around,
    highs, lows, along, shuffle,
):
    rows = state[0].shape[0]
    quarters = rows // bins
    width = bins * SLOT
    nodes = bins * TILE
    fastest = jnp.max(speeds[...], axis=0, keepdims=True)
    fastest = jnp.max(fastest, axis=1, keepdims=True)
    time_step = courant / (jnp.sqrt(fastest) + sound_speed)

    around = []
    for side, block in enumerate(blocks_around):
        around.append(placed(block[:, 0:nodes], sides[side]))
    left, right = around

    sub = iota((8, width), 0)
    wide_valid = geometry[0:8, :] >= 0.0
    component = (sub >= 1) & (sub <= 3) & wide_valid
    floor_of = geometry[8:16, :]
    roof_of = geometry[16:24, :]
    pull = time_step * jnp.where(sub == 1, gravity_x, jnp.where(sub == 3, gravity_z, 0.0))
    plane_total = 4 * device_total
    motions = []
    for a in range(6):
        sums = own[8 * a : 8 * a + 8, :]
        if a < 2:
            sums = sums + left[8 * a : 8 * a + 8]
        if a >= 4:
            sums = sums + right[8 * a - 32 : 8 * a - 24]
        plane = 4 * device + a
        node_mass = jnp.maximum(jnp.broadcast_to(sums[0:1, :], (8, width)), mass_floor)
        per_step = pltpu.roll(sums, 5, 0)
        motion = (sums - time_step * per_step) / node_mass + pull
        lowest = jnp.where(plane < 2, 0.0, -BIG)
        highest = jnp.where(plane >= plane_total - 2, 0.0, BIG)
        motion = jnp.maximum(motion, jnp.where(sub == 1, lowest, floor_of))
        motion = jnp.minimum(motion, jnp.where(sub == 1, highest, roof_of))
        inside = jnp.where(plane < plane_total, 1, 0)
        motion = jnp.where(component & (inside > 0), motion, 0.0)
        motions.append(motion)
    paired = jnp.concatenate(
        [motions[2 * g] + pltpu.roll(motions[2 * g + 1], 4, 0) for g in range(3)], axis=0
    )

    span = 8 * rows
    for b in range(bins):
        begin = (b * SLOT) // LANES * LANES
        block = paired[:, begin : begin + LANES]
        if b * SLOT > begin:
            block = pltpu.roll(block, LANES - (b * SLOT - begin), 1)
        block = block[:, 0:TILE]
        count = block.shape[0]
        high = block.astype(BF16)
        kept = high.astype(F32)
        stacked = jnp.concatenate([kept, block - kept], axis=0).astype(BF16)
        for first_quarter, wide, lanes in halves(quarters):
            row = b * quarters + first_quarter
            shape = (8, wide * LANES)
            even = iota(shape, 0) < 4
            weights, weights_moved = [
                [
                    jnp.where(
                        even,
                        spread(along, rows * (begin + 2 * g) + row, wide),
                        spread(along, rows * (begin + 2 * g + 1) + row, wide),
                    )
                    for g in range(3)
                ]
                for begin in (0, 6)
            ]
            sums = []
            for kind in range(3):
                right_high = highs[b, pl.ds(kind * TILE, TILE), lanes]
                right_low = lows[b, pl.ds(kind * TILE, TILE), lanes]
                product = dot_nn(stacked, right_high)
                product = product[0:count] + product[count : 2 * count] + dot_nn(high, right_low)
                groups = [product[8 * g : 8 * g + 8] for g in range(3)]
                sums.append(sum(w * group for w, group in zip(weights, groups)))
                if kind == 0:
                    moved_sum = sum(w * group for w, group in zip(weights_moved, groups))
            sums.append(moved_sum)
            for kind in range(4):
                for q in range(wide):
                    target = kind * span + 8 * (row + q)
                    shuffle[pl.ds(target, 8), :] = sums[kind][:, LANES * q : LANES * (q + 1)]

    def take(kind, c):
        return (
            shuffle[pl.ds(kind * span + 1 + c, rows, stride=8), :]
            + shuffle[pl.ds(kind * span + 5 + c, rows, stride=8), :]
        )

    velocity = [take(0, c) for c in range(3)]
    affine = [None] * 9
    for c in range(3):
        affine[3 * c] = 4.0 * take(3, c)
        affine[3 * c + 1] = 4.0 * take(1, c)
        affine[3 * c + 2] = 4.0 * take(2, c)
    old = state[DEF : DEF + 9]
    deform = []
    for r in range(3):
        for c in range(3):
            change = (
                affine[3 * r] * old[c] + affine[3 * r + 1] * old[3 + c] + affine[3 * r + 2] * old[6 + c]
            )
            deform.append(old[3 * r + c] + time_step * change)
    steps = [time_step * velocity[c] for c in range(3)]
    moved = [state[c] + steps[c] for c in range(3)]
    travelled = [state[TRAV + c] + steps[c] for c in range(3)]
    return moved + deform + [state[MASS], state[VOL]] + travelled, velocity, affine


def read_state(ref, rows):
    return [ref[pl.ds(rows * number, rows), :] for number in range(ROWS)]


def write_state(ref, state):
    rows = state[0].shape[0]
    for number in range(ROWS):
        ref[pl.ds(rows * number, rows), :] = state[number]


def block_row(blocks, bins, width):
    lane = iota((1, width), 1)
    meta = jnp.zeros((1, width), F32)
    for b in range(bins):
        meta = jnp.where(lane == LANES + META + b, blocks[b].astype(F32), meta)
    return meta


def first_kernel(
    bins, device_total, blocks, live, device, x_ref, v_ref, f_ref, c_ref, m_ref, vol_ref,
    state_ref, speeds, far, highs, lows, along, channels, across, outbox, sem, motion_ref,
):
    rows = state_ref.shape[0] // ROWS
    quarters = rows // bins
    for ref, count, kept, begin in (
        (x_ref, 3, state_ref, POS),
        (f_ref, 9, state_ref, DEF),
        (v_ref, 3, motion_ref, 0),
        (c_ref, 9, motion_ref, 3),
    ):
        for number in range(count):
            for s in range(rows):
                target = rows * (begin + number) + s
                kept[pl.ds(target, 1), :] = ref[pl.ds(number, 1), pl.ds(LANES * s, LANES)]
    for ref, number in ((m_ref, MASS), (vol_ref, VOL)):
        for b in range(bins):
            alive = jnp.where(b < live[0], 1.0, 0.0)
            for q in range(quarters):
                s = quarters * b + q
                piece = ref[pl.ds(LANES * s, LANES)].reshape(1, LANES)
                state_ref[pl.ds(rows * number + s, 1), :] = piece * alive
    home = jnp.zeros((rows, LANES), F32)
    home_y, home_z = home, home
    row_bin = iota((rows, LANES), 0) // quarters
    for b in range(bins):
        block = blocks[b]
        block_y = block // BZ
        block_z = block - BZ * block_y
        home_y = jnp.where(row_bin == b, (4 * block_y).astype(F32), home_y)
        home_z = jnp.where(row_bin == b, (4 * block_z).astype(F32), home_z)
    anchors = (home + (4 * device).astype(F32), home_y, home_z)
    for axis in range(3):
        place = pl.ds(rows * axis, rows)
        state_ref[place, :] = state_ref[place, :] - anchors[axis]
        state_ref[pl.ds(rows * (TRAV + axis), rows), :] = home
    state = read_state(state_ref, rows)
    motion = [motion_ref[pl.ds(rows * number, rows), :] for number in range(12)]
    copy = send_speed(motion[0:3], state[MASS], speeds, outbox, sem)
    to_grid(
        state, motion[0:3], motion[3:12], state_ref, device, bins, block_row(blocks, bins, far.shape[1]), far, highs, lows,
        along, channels, across,
    )
    copy.wait()


def place_own(own, low, middle, high, selector):
    own[0:16, :] = placed(low, selector)
    own[16:32, :] = placed(jnp.concatenate(middle, axis=1), selector)
    own[32:48, :] = placed(high, selector)


def first_rest_kernel(
    bins, device_total, blocks, live, device, far, highs, lows, along, channels,
    near, own, geometry, home,
):
    low, middle, high = rest_of_grid(
        device, bins, block_row(blocks, bins, near.shape[1]), far, highs, lows, along, channels,
        near,
    )
    width = bins * SLOT
    position = iota((1, width), 1)
    column_bin = position // SLOT
    column_node = position - SLOT * column_bin
    column_valid = (column_node < TILE) & (column_node % 8 < 6)
    own_blocks = [blocks[b].astype(F32) for b in range(bins)]
    column_block = jnp.zeros((1, width), F32)
    for b in range(bins):
        column_block = jnp.where(column_bin == b, own_blocks[b], column_block)
    column_y, column_z = node_key(column_block, column_node.astype(F32))
    column_key = jnp.where(column_valid, LANES * column_y + column_z, -1.0)
    selector = placing(own_blocks, column_key, bins)
    home[...] = selector
    place_own(own, low, middle, high, selector)
    sub = iota((8, width), 0)
    wide_y = jnp.broadcast_to(column_y, (8, width))
    wide_z = jnp.broadcast_to(column_z, (8, width))
    geometry[0:8, :] = jnp.broadcast_to(column_key, (8, width))
    geometry[8:16, :] = jnp.where(
        ((sub == 2) & (wide_y < 2.0)) | ((sub == 3) & (wide_z < 2.0)), 0.0, -BIG
    )
    geometry[16:24, :] = jnp.where(
        ((sub == 2) & (wide_y >= NGY - 2.0)) | ((sub == 3) & (wide_z >= NGZ - 2.0)), 0.0, BIG
    )


def rest_kernel(
    bins, device_total, live, device, far, highs, lows, along, channels, home, near, own
):
    low, middle, high = rest_of_grid(
        device, bins, None, far, highs, lows, along, channels, near
    )
    place_own(own, low, middle, high, home[...])


def second_kernel(
    bins, device_total, live, device, old_ref, speeds, own, geometry, old_highs, old_lows,
    old_along, near, far, state_ref, new_speeds, new_far, highs, lows, along, channels,
    sides_ref, across, outbox, sem,
):
    around = halos(near, far, device, device_total)
    key = geometry[0:1, :]
    sides = [placing(halo_blocks(block, bins), key, bins) for block in around]
    for side in range(2):
        sides_ref[side] = sides[side]
    advance(
        bins, device_total, device, old_ref, speeds, own, geometry, old_highs, old_lows,
        old_along, around, sides, state_ref, new_speeds, new_far, highs, lows, along, channels,
        across, outbox, sem,
    )


def later_kernel(
    bins, device_total, live, device, old_ref, speeds, own, geometry, old_highs, old_lows,
    old_along, near, far, sides_ref, state_ref, new_speeds, new_far, highs, lows, along, channels,
    across, outbox, sem,
):
    around = halos(near, far, device, device_total)
    sides = [sides_ref[0], sides_ref[1]]
    advance(
        bins, device_total, device, old_ref, speeds, own, geometry, old_highs, old_lows,
        old_along, around, sides, state_ref, new_speeds, new_far, highs, lows, along, channels,
        across, outbox, sem,
    )


def advance(
    bins, device_total, device, old_ref, speeds, own, geometry, old_highs, old_lows,
    old_along, around, sides, state_ref, new_speeds, far, highs, lows, along, channels,
    across, outbox, sem,
):
    rows = state_ref.shape[0] // ROWS
    state = read_state(old_ref, rows)
    state, velocity, affine = to_particles(
        state, device, bins, device_total, geometry, own, sides, speeds, around, old_highs,
        old_lows, old_along, channels,
    )
    write_state(state_ref, state)
    copy = send_speed(velocity, state[MASS], new_speeds, outbox, sem)
    to_grid(
        state, velocity, affine, state_ref, device, bins, None, far, highs, lows, along, channels, across
    )
    copy.wait()


def last_kernel(
    bins, device_total, live, device, old_ref, speeds, own, geometry, highs, lows, along,
    near, far, sides_ref, d_out, v_out, f_out, c_out, shuffle,
):
    rows = old_ref.shape[0] // ROWS
    quarters = rows // bins
    state = read_state(old_ref, rows)
    state, velocity, affine = to_particles(
        state, device, bins, device_total, geometry, own, [sides_ref[0], sides_ref[1]], speeds,
        halos(near, far, device, device_total), highs, lows, along, shuffle,
    )
    row_bin = iota((rows, LANES), 0) // quarters
    alive = row_bin < live[0]
    half = rows * LANES
    results = (
        (d_out, state[TRAV : TRAV + 3]),
        (v_out, velocity),
        (f_out, state[DEF : DEF + 9]),
        (c_out, affine),
    )
    for ref, values in results:
        count = len(values)
        for number in range(count):
            value = jnp.where(alive, values[number], 0.0)
            for s in range(rows):
                ref[pl.ds(number, 1), pl.ds(LANES * s, LANES)] = value[s : s + 1, :]
        total = ref.shape[1]
        ref[:, pl.ds(half, total - half)] = jnp.zeros((count, total - half), F32)


def local(positions, velocity, deformation, affine, particle_mass, volume, bin_block, live_count):
    slot_total = bin_block.shape[0]
    per_bin = positions.shape[1] // slot_total
    bins = slot_total // 2
    device_total = lax.axis_size("space")
    rows = bins * per_bin // LANES
    half = rows * LANES
    nodes = bins * TILE
    width = bins * SLOT
    message = ((16, -(-(nodes + LANES // 2) // LANES) * LANES), F32)
    held = [
        ((ROWS * rows, LANES), F32),
        ((device_total, LANES), F32),
        message,
        ((bins, 3 * TILE, per_bin), BF16),
        ((bins, 3 * TILE, per_bin), BF16),
        ((12 * rows, LANES), F32),
        ((4 * 8 * rows, LANES), F32),
    ]
    speeds_shape = held[1]
    own_shape = ((48, width), F32)
    geometry_shape = ((24, width), F32)
    home_shape = ((nodes, width), BF16)
    sides_shape = ((2, nodes, width), BF16)
    smem = pl.BlockSpec(memory_space=pltpu.SMEM)
    vmem = pl.BlockSpec(memory_space=pltpu.VMEM)
    anywhere = pl.BlockSpec(memory_space=pl.ANY)
    working = [
        pltpu.VMEM((12 * rows, LANES), F32),
        pltpu.VMEM((device_total, LANES), F32),
        pltpu.SemaphoreType.DMA,
    ]
    bin_block = bin_block if INTERPRET else pltpu.with_memory_space_constraint(bin_block, pltpu.HBM)
    me = lax.axis_index("space").astype(jnp.int32).reshape(1)

    def stay(array, space=pltpu.VMEM):
        return array if INTERPRET else pltpu.with_memory_space_constraint(array, space)

    def call(body, scalars, arguments, outputs, scratch, in_specs=None, final=False):
        def kernel(*refs):
            count = len(scalars)
            body(bins, device_total, *refs[: count - 1], refs[count - 1][0], *refs[count:])

        extra = {}
        out_specs = tuple(anywhere if output == speeds_shape else vmem for output in outputs)
        if in_specs is None:
            in_specs = [vmem] * len(arguments)
            arguments = [stay(argument) for argument in arguments]
        else:
            arguments = [stay(argument, pltpu.HBM) for argument in arguments]
            out_specs = tuple(
                anywhere
                if output == speeds_shape
                else pl.BlockSpec(output[0], lambda i, rank=len(output[0]): (0,) * rank)
                for output in outputs
            )
            extra = {"grid": (1,)}
        make = jax.ShapeDtypeStruct if final or INTERPRET else pltpu.VMEM
        return pl.pallas_call(
            kernel,
            in_specs=[smem] * len(scalars) + in_specs,
            out_shape=tuple(
                pltpu.HBM(*output) if output == speeds_shape and not INTERPRET else make(*output)
                for output in outputs
            ),
            out_specs=out_specs,
            scratch_shapes=scratch,
            interpret=INTERPRET,
            compiler_params=pltpu.CompilerParams(vmem_limit_bytes=GRANT),
            **extra,
        )(*scalars, *arguments)

    def first_half(count):
        return pl.BlockSpec((count, half), lambda i: (0, 0))

    flat_half = pl.BlockSpec((half,), lambda i: (0,))
    length = device_total
    swap_pairs = [(i, i ^ 1) for i in range(length)]
    cross_pairs = [(i, i + 1) for i in range(1, length - 1, 2)]
    cross_pairs = cross_pairs + [(j, i) for i, j in cross_pairs]

    results = call(
        first_kernel,
        (bin_block, live_count, me),
        (positions, velocity, deformation, affine, particle_mass, volume),
        held,
        working + [pltpu.VMEM((12 * rows, LANES), F32)],
        [first_half(3), first_half(3), first_half(9), first_half(9), flat_half, flat_half],
    )
    sides = ()
    for step in range(STEPS):
        state, speeds, far, highs, lows, along, channels = results[:7]
        sides = sides + tuple(results[7:])
        speeds = lax.all_to_all(speeds, "space", 0, 0, tiled=True)
        from_far = lax.ppermute(far, "space", cross_pairs)
        arguments = (far, highs, lows, along, channels)
        if step == 0:
            near, own, geometry, home = call(
                first_rest_kernel,
                (bin_block, live_count, me),
                arguments,
                [message, own_shape, geometry_shape, home_shape],
                [],
            )
        else:
            near, own = call(
                rest_kernel, (live_count, me), arguments + (home,), [message, own_shape], []
            )
        from_near = lax.ppermute(near, "space", swap_pairs)
        arguments = (state, speeds, own, geometry, highs, lows, along, from_near, from_far, *sides)
        if step < STEPS - 1:
            results = call(
                second_kernel if step == 0 else later_kernel,
                (live_count, me),
                arguments,
                held + ([sides_shape] if step == 0 else []),
                working,
            )
    total = positions.shape[1]
    return call(
        last_kernel,
        (live_count, me),
        arguments,
        [((count, total), F32) for count in (3, 3, 9, 9)],
        [pltpu.VMEM((4 * 8 * rows, LANES), F32)],
        final=True,
    )


def solution(mesh):
    in_specs = (
        P(None, "space"),
        P(None, "space"),
        P(None, "space"),
        P(None, "space"),
        P("space"),
        P("space"),
        P("space"),
        P("space"),
    )
    out_specs = (P(None, "space"), P(None, "space"), P(None, "space"), P(None, "space"))
    return jax.shard_map(local, mesh=mesh, in_specs=in_specs, out_specs=out_specs, check_vma=False)
```

time: 50 us -> 45.9 us (0.918)
  waiting for transfers between devices: 17.1 us -> 9.67 us
  starting transfers between devices: 19.6 us -> 24.6 us
  Pallas kernels: 11.6 us -> 9.98 us
    all_to_all x3, waiting for transfers between devices: 16.9 us -> 7.71 us  [local(): speeds = lax.all_to_all(speeds, 'space', 0, 0, tiled=True)]
    ppermute x6, starting transfers between devices: 2.9 us -> 8.56 us  [the longest x3 6.58 us: local(): from_near = lax.ppermute(near, 'space', swap_pairs)]
    ppermute x6, waiting for transfers between devices: 0.26 us -> 1.96 us  [the longest x3 1.95 us: local(): from_near = lax.ppermute(near, 'space', swap_pairs)]
    pallas_call x7, Pallas kernels: 11.6 us -> 9.98 us  [call(): pl.pallas_call(kernel, in_specs=[smem] * len(scalars) + in_specs, out_sha...]
    all_to_all x3, starting transfers between devices: 16.7 us -> 16.1 us  [local(): speeds = lax.all_to_all(speeds, 'space', 0, 0, tiled=True)]
  transfers between devices with their start and end apart: 9 -> 9, of which waited for: 5 -> 6; matrix products, arithmetic and copies ran while one was open for 0% -> 0% of each run, Pallas kernels for 2% -> 7%
where the time goes in v2:
time: 45.9 us; the launch traced here: 45.6 us
  starting transfers between devices  24.6 us (54%)
  Pallas kernels  9.98 us (22%)
  waiting for transfers between devices  9.67 us (21%)
  between operations  1.36 us (3%)
    all_to_all x3, starting transfers between devices, local(): speeds = lax.all_to_all(speeds, 'space', 0, 0, tiled=True)  16.1 us
    pallas_call x7, Pallas kernels, call(): pl.pallas_call(kernel, in_specs=[smem] * len(scalars) + in_specs, out_sha...  9.98 us
    all_to_all x3, waiting for transfers between devices, local(): speeds = lax.all_to_all(speeds, 'space', 0, 0, tiled=True)  7.71 us
    ppermute x3, starting transfers between devices, local(): from_near = lax.ppermute(near, 'space', swap_pairs)  6.58 us
    ppermute x3, starting transfers between devices, local(): from_far = lax.ppermute(far, 'space', cross_pairs)  1.97 us
    ppermute x3, waiting for transfers between devices, local(): from_near = lax.ppermute(near, 'space', swap_pairs)  1.95 us
  transfers between devices with their start and end apart: 9, of which 6 were waited for; matrix products, arithmetic and copies ran while one was open for 0% of the time, Pallas kernels for 7%

profile of v2, /device:TPU:0, one launch (start us, length us, event | category | flops | bytes accessed | tf_op | source)
XLA Modules:
  0.0 45.6 jit_solution(10192388030540421840)
XLA Ops:
  1.3 2.3 %shard_map.111 = (f32[272,128]{1,0:T(8,128)S(1)}, f32[32,128]{1,0:T(8,128)}, f32[16,256]{1,0:T(8,128)S(1)}, bf16[4,144,512]{2,1,0:T(8,128)(2,1)S(1)}, bf16[4,144...) custom-call(s32[8]{0:T(128)} %refs_0_.8, s32[1]{0:T(128)S(6)} %copy.15.refs_1_.refs_0_, ...), custom_call_target="tpu_custom_call" | custom-call | tf_op jit(solution)/shard_map/pallas_call | solution.py:655
  3.6 7.3 %all-to-all-start = ((f32[32,1,128]{2,1,0:T(1,128)}), f32[32,1,128]{2,1,0:T(1,128)S(1)}, u32[]{:S(2)}, u32[]{:S(2)}) async-start(f32[32,1,128]{2,1,0:T(1,128)} %bitcast.18), calls=%async_computation | async-start | bytes 32768 | tf_op jit(solution)/shard_map/all_to_all | solution.py:690
  10.9 0.7 %collective-permute-start.1 = (f32[16,256]{1,0:T(8,128)S(1)}, f32[16,256]{1,0:T(8,128)S(1)}, u32[]{:S(2)}, u32[]{:S(2)}) collective-permute-start(f32[16,256]{1,0:T(8,128)S(1)} %get-tuple-element.36.refs_3_), channel_id=1, source_target_pairs={{1,2},{3,4},{5,6},{7,8},{9,10},{11,12},{13,14},{15,16},{17,18},{19... | collective-permute-start | bytes 49160 | tf_op jit(solution)/shard_map/ppermute | solution.py:691
  11.6 1.5 %shard_map.112 = (f32[16,256]{1,0:T(8,128)S(1)}, f32[48,256]{1,0:T(8,128)S(1)}, f32[24,256]{1,0:T(8,128)S(1)}, bf16[192,256]{1,0:T(8,128)(2,1)S(1)}) custom-call(s32[8]{0:T(128)} %refs_0_.8, s32[1]{0:T(128)S(6)} %copy.15.refs_1_.refs_0_, s32[1]{0:T(128)} %bitcast.refs_2_.refs_1_, f32[16,256]{1,0:T(8,128)S(1)} %get-tuple-element.36.refs_3_, ...), custom_call_target="tpu_custom_call" | custom-call | tf_op jit(solution)/shard_map/pallas_call | solution.py:655
  13.1 3.2 %collective-permute-start = (f32[16,256]{1,0:T(8,128)S(1)}, f32[16,256]{1,0:T(8,128)S(1)}, u32[]{:S(2)}, u32[]{:S(2)}) collective-permute-start(f32[16,256]{1,0:T(8,128)S(1)} %get-tuple-element.43), channel_id=1, source_target_pairs={{0,1},{1,0},{2,3},{3,2},{4,5},{5,4},{6,7},{7,6},{8,9},{9,8},{10,11... | collective-permute-start | bytes 49160 | tf_op jit(solution)/shard_map/ppermute | solution.py:705
  16.2 0.0 collective-permute-done.1.refs_10_
  16.2 0.8 %collective-permute-done.refs_9_ = f32[16,256]{1,0:T(8,128)S(1)} collective-permute-done((f32[16,256]{1,0:T(8,128)S(1)}, f32[16,256]{1,0:T(8,128)S(1)}, u32[]{:S(2)}, u32[]{:S(2)}) %collective-permute-start) | collective-permute-done | bytes 16416 | tf_op jit(solution)/shard_map/ppermute | solution.py:705
  17.1 1.0 %all-to-all-done = f32[32,1,128]{2,1,0:T(1,128)S(1)} async-done(((f32[32,1,128]{2,1,0:T(1,128)}), f32[32,1,128]{2,1,0:T(1,128)S(1)}, u32[]{:S(2)}, u32[]{:S(2)}) %all-to-all-start) | async-done | bytes 16416 | tf_op jit(solution)/shard_map/all_to_all | solution.py:690
  18.0 1.8 %shard_map.113 = (f32[272,128]{1,0:T(8,128)S(1)}, f32[32,128]{1,0:T(8,128)}, f32[16,256]{1,0:T(8,128)S(1)}, bf16[4,144,512]{2,1,0:T(8,128)(2,1)S(1)}, bf16[4,144...) custom-call(s32[1]{0:T(128)S(6)} %copy.15.refs_1_.refs_0_, ...), custom_call_target="tpu_custom_call" | custom-call | tf_op jit(solution)/shard_map/pallas_call | solution.py:655
  19.8 4.4 %all-to-all-start.1 = ((f32[32,1,128]{2,1,0:T(1,128)}), f32[32,1,128]{2,1,0:T(1,128)S(1)}, u32[]{:S(2)}, u32[]{:S(2)}) async-start(f32[32,1,128]{2,1,0:T(1,128)} %bitcast.16), calls=%async_computation.1 | async-start | bytes 32768 | tf_op jit(solution)/shard_map/all_to_all | solution.py:690
  24.2 0.7 %collective-permute-start.3 = (f32[16,256]{1,0:T(8,128)S(1)}, f32[16,256]{1,0:T(8,128)S(1)}, u32[]{:S(2)}, u32[]{:S(2)}) collective-permute-start(f32[16,256]{1,0:T(8,128)S(1)} %get-tuple-element.46.refs_2_), channel_id=1, source_target_pairs={{1,2},{3,4},{5,6},{7,8},{9,10},{11,12},{13,14},{15,16},{17,18},{19... | collective-permute-start | bytes 49160 | tf_op jit(solution)/shard_map/ppermute | solution.py:691
  24.8 0.8 %shard_map.114 = (f32[16,256]{1,0:T(8,128)S(1)}, f32[48,256]{1,0:T(8,128)S(1)}) custom-call(s32[1]{0:T(128)S(6)} %copy.15.refs_1_.refs_0_, s32[1]{0:T(128)} %bitcast.refs_2_.refs_1_, f32[16,256]{1,0:T(8,128)S(1)} %get-tuple-element.46.refs_2_, bf16[4,144,512]{2,1,0:T(8,128)(2,1)S(1)} %get-tuple-element.47.refs_3_.refs_6_, ...), custom_call_target="tpu_custom_call" | custom-call | tf_op jit(solution)/shard_map/pallas_call | solution.py:655
  25.6 3.2 %collective-permute-start.2 = (f32[16,256]{1,0:T(8,128)S(1)}, f32[16,256]{1,0:T(8,128)S(1)}, u32[]{:S(2)}, u32[]{:S(2)}) collective-permute-start(f32[16,256]{1,0:T(8,128)S(1)} %get-tuple-element.53), channel_id=1, source_target_pairs={{0,1},{1,0},{2,3},{3,2},{4,5},{5,4},{6,7},{7,6},{8,9},{9,8},{10,11... | collective-permute-start | bytes 49160 | tf_op jit(solution)/shard_map/ppermute | solution.py:705
  28.8 0.0 collective-permute-done.3.refs_10_
  28.8 0.8 %collective-permute-done.2.refs_9_ = f32[16,256]{1,0:T(8,128)S(1)} collective-permute-done((f32[16,256]{1,0:T(8,128)S(1)}, f32[16,256]{1,0:T(8,128)S(1)}, u32[]{:S(2)}, u32[]{:S(2)}) %collective-permute-start.2) | collective-permute-done | bytes 16416 | tf_op jit(solution)/shard_map/ppermute | solution.py:705
  29.6 1.7 %all-to-all-done.1 = f32[32,1,128]{2,1,0:T(1,128)S(1)} async-done(((f32[32,1,128]{2,1,0:T(1,128)}), f32[32,1,128]{2,1,0:T(1,128)S(1)}, u32[]{:S(2)}, u32[]{:S(2)}) %all-to-all-start.1) | async-done | bytes 16416 | tf_op jit(solution)/shard_map/all_to_all | solution.py:690
  31.3 1.4 %shard_map.115 = (f32[272,128]{1,0:T(8,128)S(1)}, f32[32,128]{1,0:T(8,128)}, f32[16,256]{1,0:T(8,128)S(1)}, bf16[4,144,512]{2,1,0:T(8,128)(2,1)S(1)}, bf16[4,144...) custom-call(s32[1]{0:T(128)S(6)} %copy.15.refs_1_.refs_0_, s32[1]{0:T(128)} %bitcast.refs_2_.refs_1_, ...), custom_call_target="tpu_custom_call" | custom-call | tf_op jit(solution)/shard_map/pallas_call | solution.py:655
  32.7 4.4 %all-to-all-start.2 = ((f32[32,1,128]{2,1,0:T(1,128)}), f32[32,1,128]{2,1,0:T(1,128)S(1)}, u32[]{:S(2)}, u32[]{:S(2)}) async-start(f32[32,1,128]{2,1,0:T(1,128)} %bitcast.17), calls=%async_computation.2 | async-start | bytes 32768 | tf_op jit(solution)/shard_map/all_to_all | solution.py:690
  37.1 0.8 %shard_map.116 = (f32[16,256]{1,0:T(8,128)S(1)}, f32[48,256]{1,0:T(8,128)S(1)}) custom-call(s32[1]{0:T(128)S(6)} %copy.15.refs_1_.refs_0_, s32[1]{0:T(128)} %bitcast.refs_2_.refs_1_, f32[16,256]{1,0:T(8,128)S(1)} %get-tuple-element.57.refs_2_, bf16[4,144,512]{2,1,0:T(8,128)(2,1)S(1)} %get-tuple-element.58.refs_3_.refs_6_, ...), custom_call_target="tpu_custom_call" | custom-call | tf_op jit(solution)/shard_map/pallas_call | solution.py:655
  37.9 0.3 collective-permute-start.4
  38.2 0.7 %collective-permute-start.5 = (f32[16,256]{1,0:T(8,128)S(1)}, f32[16,256]{1,0:T(8,128)S(1)}, u32[]{:S(2)}, u32[]{:S(2)}) collective-permute-start(f32[16,256]{1,0:T(8,128)S(1)} %get-tuple-element.57.refs_2_), channel_id=1, source_target_pairs={{1,2},{3,4},{5,6},{7,8},{9,10},{11,12},{13,14},{15,16},{17,18},{19... | collective-permute-start | bytes 49160 | tf_op jit(solution)/shard_map/ppermute | solution.py:691
  38.8 0.3 collective-permute-done.4.refs_9_
  39.1 0.0 collective-permute-done.5.refs_10_
  39.1 5.1 %all-to-all-done.2 = f32[32,1,128]{2,1,0:T(1,128)S(1)} async-done(((f32[32,1,128]{2,1,0:T(1,128)}), f32[32,1,128]{2,1,0:T(1,128)S(1)}, u32[]{:S(2)}, u32[]{:S(2)}) %all-to-all-start.2) | async-done | bytes 16416 | tf_op jit(solution)/shard_map/all_to_all | solution.py:690
  44.2 1.4 %shard_map.117 = (f32[3,4096]{1,0:T(4,128)}, f32[3,4096]{1,0:T(4,128)}, f32[9,4096]{1,0:T(8,128)}, f32[9,4096]{1,0:T(8,128)}) custom-call(s32[1]{0:T(128)S(6)} %copy.15.refs_1_.refs_0_, s32[1]{0:T(128)} %bitcast.refs_2_.refs_1_, f32[272,128]{1,0:T(8,128)S(1)} %get-tuple-element.55.refs_2_, f32[32,128]{1,0:T(8,128)S(1)} %bitcast.14, ...), custom_call_target="tpu_custom_call" | custom-call | tf_op jit(solution)/shard_map/pallas_call | solution.py:655
Async XLA Ops:
  3.6 14.4 %all-to-all-start = ((f32[32,1,128]{2,1,0:T(1,128)}), f32[32,1,128]{2,1,0:T(1,128)S(1)}, u32[]{:S(2)}, u32[]{:S(2)}) async-start(f32[32,1,128]{2,1,0:T(1,128)} %bitcast.18), calls=%async_computation | async-start | bytes 32768 | tf_op jit(solution)/shard_map/all_to_all | solution.py:690
  10.9 5.3 %collective-permute-start.1 = (f32[16,256]{1,0:T(8,128)S(1)}, f32[16,256]{1,0:T(8,128)S(1)}, u32[]{:S(2)}, u32[]{:S(2)}) collective-permute-start(f32[16,256]{1,0:T(8,128)S(1)} %get-tuple-element.36.refs_3_), channel_id=1, source_target_pairs={{1,2},{3,4},{5,6},{7,8},{9,10},{11,12},{13,14},{15,16},{17,18},{19... | collective-permute-start | bytes 49160 | tf_op jit(solution)/shard_map/ppermute | solution.py:691
  13.1 4.0 %collective-permute-start = (f32[16,256]{1,0:T(8,128)S(1)}, f32[16,256]{1,0:T(8,128)S(1)}, u32[]{:S(2)}, u32[]{:S(2)}) collective-permute-start(f32[16,256]{1,0:T(8,128)S(1)} %get-tuple-element.43), channel_id=1, source_target_pairs={{0,1},{1,0},{2,3},{3,2},{4,5},{5,4},{6,7},{7,6},{8,9},{9,8},{10,11... | collective-permute-start | bytes 49160 | tf_op jit(solution)/shard_map/ppermute | solution.py:705
  19.8 11.5 %all-to-all-start.1 = ((f32[32,1,128]{2,1,0:T(1,128)}), f32[32,1,128]{2,1,0:T(1,128)S(1)}, u32[]{:S(2)}, u32[]{:S(2)}) async-start(f32[32,1,128]{2,1,0:T(1,128)} %bitcast.16), calls=%async_computation.1 | async-start | bytes 32768 | tf_op jit(solution)/shard_map/all_to_all | solution.py:690
  24.2 4.6 %collective-permute-start.3 = (f32[16,256]{1,0:T(8,128)S(1)}, f32[16,256]{1,0:T(8,128)S(1)}, u32[]{:S(2)}, u32[]{:S(2)}) collective-permute-start(f32[16,256]{1,0:T(8,128)S(1)} %get-tuple-element.46.refs_2_), channel_id=1, source_target_pairs={{1,2},{3,4},{5,6},{7,8},{9,10},{11,12},{13,14},{15,16},{17,18},{19... | collective-permute-start | bytes 49160 | tf_op jit(solution)/shard_map/ppermute | solution.py:691
  25.6 4.0 %collective-permute-start.2 = (f32[16,256]{1,0:T(8,128)S(1)}, f32[16,256]{1,0:T(8,128)S(1)}, u32[]{:S(2)}, u32[]{:S(2)}) collective-permute-start(f32[16,256]{1,0:T(8,128)S(1)} %get-tuple-element.53), channel_id=1, source_target_pairs={{0,1},{1,0},{2,3},{3,2},{4,5},{5,4},{6,7},{7,6},{8,9},{9,8},{10,11... | collective-permute-start | bytes 49160 | tf_op jit(solution)/shard_map/ppermute | solution.py:705
  32.7 11.5 %all-to-all-start.2 = ((f32[32,1,128]{2,1,0:T(1,128)}), f32[32,1,128]{2,1,0:T(1,128)S(1)}, u32[]{:S(2)}, u32[]{:S(2)}) async-start(f32[32,1,128]{2,1,0:T(1,128)} %bitcast.17), calls=%async_computation.2 | async-start | bytes 32768 | tf_op jit(solution)/shard_map/all_to_all | solution.py:690
  37.9 1.2 %collective-permute-start.4 = (f32[16,256]{1,0:T(8,128)S(1)}, f32[16,256]{1,0:T(8,128)S(1)}, u32[]{:S(2)}, u32[]{:S(2)}) collective-permute-start(f32[16,256]{1,0:T(8,128)S(1)} %get-tuple-element.63), channel_id=1, source_target_pairs={{0,1},{1,0},{2,3},{3,2},{4,5},{5,4},{6,7},{7,6},{8,9},{9,8},{10,11... | collective-permute-start | bytes 49160 | tf_op jit(solution)/shard_map/ppermute | solution.py:705
  38.2 0.9 %collective-permute-start.5 = (f32[16,256]{1,0:T(8,128)S(1)}, f32[16,256]{1,0:T(8,128)S(1)}, u32[]{:S(2)}, u32[]{:S(2)}) collective-permute-start(f32[16,256]{1,0:T(8,128)S(1)} %get-tuple-element.57.refs_2_), channel_id=1, source_target_pairs={{1,2},{3,4},{5,6},{7,8},{9,10},{11,12},{13,14},{15,16},{17,18},{19... | collective-permute-start | bytes 49160 | tf_op jit(solution)/shard_map/ppermute | solution.py:691

commit v3 on v2

--- a/solution.py
+++ b/solution.py
@@ -268,9 +268,11 @@
     return result[0:count] + result[count : 2 * count]
 
 
-def halos(near, far, device, device_total):
+def halos(near, outer, inner, device, device_total):
     odd = device % 2 == 1
-    near_block, far_block = near[...], far[...]
+    middle = (device + 1) % 4 >= 2
+    near_block = near[...]
+    far_block = jnp.where(middle, inner[...], outer[...])
     left_block = jnp.where(odd, near_block, far_block)
     right_block = jnp.where(odd, far_block, near_block)
     left_block = jnp.where(device > 0, left_block, 0.0)
@@ -516,10 +518,10 @@
 
 def second_kernel(
     bins, device_total, live, device, old_ref, speeds, own, geometry, old_highs, old_lows,
-    old_along, near, far, state_ref, new_speeds, new_far, highs, lows, along, channels,
+    old_along, near, outer, inner, state_ref, new_speeds, new_far, highs, lows, along, channels,
     sides_ref, across, outbox, sem,
 ):
-    around = halos(near, far, device, device_total)
+    around = halos(near, outer, inner, device, device_total)
     key = geometry[0:1, :]
     sides = [placing(halo_blocks(block, bins), key, bins) for block in around]
     for side in range(2):
@@ -533,10 +535,10 @@
 
 def later_kernel(
     bins, device_total, live, device, old_ref, speeds, own, geometry, old_highs, old_lows,
-    old_along, near, far, sides_ref, state_ref, new_speeds, new_far, highs, lows, along, channels,
+    old_along, near, outer, inner, sides_ref, state_ref, new_speeds, new_far, highs, lows, along, channels,
     across, outbox, sem,
 ):
-    around = halos(near, far, device, device_total)
+    around = halos(near, outer, inner, device, device_total)
     sides = [sides_ref[0], sides_ref[1]]
     advance(
         bins, device_total, device, old_ref, speeds, own, geometry, old_highs, old_lows,
@@ -566,14 +568,14 @@
 
 def last_kernel(
     bins, device_total, live, device, old_ref, speeds, own, geometry, highs, lows, along,
-    near, far, sides_ref, d_out, v_out, f_out, c_out, shuffle,
+    near, outer, inner, sides_ref, d_out, v_out, f_out, c_out, shuffle,
 ):
     rows = old_ref.shape[0] // ROWS
     quarters = rows // bins
     state = read_state(old_ref, rows)
     state, velocity, affine = to_particles(
         state, device, bins, device_total, geometry, own, [sides_ref[0], sides_ref[1]], speeds,
-        halos(near, far, device, device_total), highs, lows, along, shuffle,
+        halos(near, outer, inner, device, device_total), highs, lows, along, shuffle,
     )
     row_bin = iota((rows, LANES), 0) // quarters
     alive = row_bin < live[0]
@@ -672,8 +674,11 @@
     flat_half = pl.BlockSpec((half,), lambda i: (0,))
     length = device_total
     swap_pairs = [(i, i ^ 1) for i in range(length)]
-    cross_pairs = [(i, i + 1) for i in range(1, length - 1, 2)]
-    cross_pairs = cross_pairs + [(j, i) for i, j in cross_pairs]
+    inner_pairs = [(i, i ^ 3) for i in range(length)]
+    outer_pairs = [(i, i + 1) for i in range(3, length - 1, 4)]
+    outer_pairs = outer_pairs + [(i, i + 3) for i in range(2, length - 3, 4)]
+    outer_pairs = outer_pairs + [(0, 1), (length - 2, length - 1)]
+    outer_pairs = outer_pairs + [(j, i) for i, j in outer_pairs]
 
     results = call(
         first_kernel,
@@ -688,7 +693,8 @@
         state, speeds, far, highs, lows, along, channels = results[:7]
         sides = sides + tuple(results[7:])
         speeds = lax.all_to_all(speeds, "space", 0, 0, tiled=True)
-        from_far = lax.ppermute(far, "space", cross_pairs)
+        from_outer = lax.ppermute(far, "space", outer_pairs)
+        from_inner = lax.ppermute(far, "space", inner_pairs)
         arguments = (far, highs, lows, along, channels)
         if step == 0:
             near, own, geometry, home = call(
@@ -703,7 +709,7 @@
                 rest_kernel, (live_count, me), arguments + (home,), [message, own_shape], []
             )
         from_near = lax.ppermute(near, "space", swap_pairs)
-        arguments = (state, speeds, own, geometry, highs, lows, along, from_near, from_far, *sides)
+        arguments = (state, speeds, own, geometry, highs, lows, along, from_near, from_outer, from_inner, *sides)
         if step < STEPS - 1:
             results = call(
                 second_kernel if step == 0 else later_kernel,

time: 45.9 us -> 45 us (0.980)
  starting transfers between devices: 24.6 us -> 20.6 us
  waiting for transfers between devices: 9.67 us -> 11.4 us
  local copies, waits for them, and re-layouts: 0 us -> 1.32 us
    ppermute x3, starting transfers between devices: 6.58 us -> 0.56 us  [local(): from_near = lax.ppermute(near, 'space', swap_pairs)]
    ppermute x3 -> x6, starting transfers between devices: 1.97 us -> 5.64 us  [the longest x3 4.74 us: local(): from_inner = lax.ppermute(far, 'space', inner_pairs)]
    ppermute x3 -> x6, waiting for transfers between devices: 0.01 us -> 1.78 us  [the longest x3 1.77 us: local(): from_inner = lax.ppermute(far, 'space', inner_pairs)]
    all_to_all x3, starting transfers between devices: 16.1 us -> 14.4 us  [local(): speeds = lax.all_to_all(speeds, 'space', 0, 0, tiled=True)]
    unnamed x0 -> x4, local copies, waits for them, and re-layouts: none -> 1.32 us
  transfers between devices with their start and end apart: 9 -> 12, of which waited for: 6 -> 7; matrix products, arithmetic and copies ran while one was open for 0% -> 0% of each run, Pallas kernels for 7% -> 7%
where the time goes in v3:
time: 45 us; the launch traced here: 44.6 us
  starting transfers between devices  20.6 us (46%)
  waiting for transfers between devices  11.4 us (25%)
  Pallas kernels  9.97 us (22%)
  between operations  1.34 us (3%)
  local copies, waits for them, and re-layouts  1.32 us (3%)
    all_to_all x3, starting transfers between devices, local(): speeds = lax.all_to_all(speeds, 'space', 0, 0, tiled=True)  14.4 us
    pallas_call x7, Pallas kernels, call(): pl.pallas_call(kernel, in_specs=[smem] * len(scalars) + in_specs, out_sha...  9.97 us
    all_to_all x3, waiting for transfers between devices, local(): speeds = lax.all_to_all(speeds, 'space', 0, 0, tiled=True)  7.89 us
    ppermute x3, starting transfers between devices, local(): from_inner = lax.ppermute(far, 'space', inner_pairs)  4.74 us
    ppermute x3, waiting for transfers between devices, local(): from_inner = lax.ppermute(far, 'space', inner_pairs)  1.77 us
    ppermute x3, waiting for transfers between devices, local(): from_near = lax.ppermute(near, 'space', swap_pairs)  1.77 us
    unnamed x4, local copies, waits for them, and re-layouts  1.32 us
    ppermute x3, starting transfers between devices, local(): from_outer = lax.ppermute(far, 'space', outer_pairs)  0.91 us
  transfers between devices with their start and end apart: 12, of which 7 were waited for; matrix products, arithmetic and copies ran while one was open for 0% of the time, Pallas kernels for 7%

profile of v3, /device:TPU:0, one launch (start us, length us, event | category | flops | bytes accessed | tf_op | source)
XLA Modules:
  0.0 44.6 jit_solution(7557713442074715564)
XLA Ops:
  1.3 2.3 %shard_map.111 = (f32[272,128]{1,0:T(8,128)S(1)}, f32[32,128]{1,0:T(8,128)}, f32[16,256]{1,0:T(8,128)S(1)}, bf16[4,144,512]{2,1,0:T(8,128)(2,1)S(1)}, bf16[4,144...) custom-call(s32[8]{0:T(128)} %refs_0_.8, s32[1]{0:T(128)S(6)} %copy.15.refs_1_.refs_0_, ...), custom_call_target="tpu_custom_call" | custom-call | tf_op jit(solution)/shard_map/pallas_call | solution.py:657
  3.6 7.3 %all-to-all-start = ((f32[32,1,128]{2,1,0:T(1,128)}), f32[32,1,128]{2,1,0:T(1,128)S(1)}, u32[]{:S(2)}, u32[]{:S(2)}) async-start(f32[32,1,128]{2,1,0:T(1,128)} %bitcast.18), calls=%async_computation | async-start | bytes 32768 | tf_op jit(solution)/shard_map/all_to_all | solution.py:695
  10.9 1.6 %collective-permute-start.2 = (f32[16,256]{1,0:T(8,128)S(1)}, f32[16,256]{1,0:T(8,128)S(1)}, u32[]{:S(2)}, u32[]{:S(2)}) collective-permute-start(f32[16,256]{1,0:T(8,128)S(1)} %get-tuple-element.36.refs_3_), channel_id=1, source_target_pairs={{0,3},{1,2},{2,1},{3,0},{4,7},{5,6},{6,5},{7,4},{8,11},{9,10},{10,... | collective-permute-start | bytes 49160 | tf_op jit(solution)/shard_map/ppermute | solution.py:697
  12.5 0.4 collective-permute-start.1
  12.9 1.5 %shard_map.112 = (f32[16,256]{1,0:T(8,128)S(1)}, f32[48,256]{1,0:T(8,128)S(1)}, f32[24,256]{1,0:T(8,128)S(1)}, bf16[192,256]{1,0:T(8,128)(2,1)S(1)}) custom-call(s32[8]{0:T(128)} %refs_0_.8, s32[1]{0:T(128)S(6)} %copy.15.refs_1_.refs_0_, s32[1]{0:T(128)} %bitcast.refs_2_.refs_1_, f32[16,256]{1,0:T(8,128)S(1)} %get-tuple-element.36.refs_3_, ...), custom_call_target="tpu_custom_call" | custom-call | tf_op jit(solution)/shard_map/pallas_call | solution.py:657
  14.3 0.1 collective-permute-start
  14.5 0.0 collective-permute-done.2.refs_11_
  14.5 0.0 collective-permute-done.1.refs_10_
  14.5 1.1 %collective-permute-done.refs_9_ = f32[16,256]{1,0:T(8,128)S(1)} collective-permute-done((f32[16,256]{1,0:T(8,128)S(1)}, f32[16,256]{1,0:T(8,128)S(1)}, u32[]{:S(2)}, u32[]{:S(2)}) %collective-permute-start) | collective-permute-done | bytes 16416 | tf_op jit(solution)/shard_map/ppermute | solution.py:711
  15.6 2.5 %all-to-all-done = f32[32,1,128]{2,1,0:T(1,128)S(1)} async-done(((f32[32,1,128]{2,1,0:T(1,128)}), f32[32,1,128]{2,1,0:T(1,128)S(1)}, u32[]{:S(2)}, u32[]{:S(2)}) %all-to-all-start) | async-done | bytes 16416 | tf_op jit(solution)/shard_map/all_to_all | solution.py:695
  18.0 1.8 %shard_map.113 = (f32[272,128]{1,0:T(8,128)S(1)}, f32[32,128]{1,0:T(8,128)}, f32[16,256]{1,0:T(8,128)S(1)}, bf16[4,144,512]{2,1,0:T(8,128)(2,1)S(1)}, bf16[4,144...) custom-call(s32[1]{0:T(128)S(6)} %copy.15.refs_1_.refs_0_, ...), custom_call_target="tpu_custom_call" | custom-call | tf_op jit(solution)/shard_map/pallas_call | solution.py:657
  19.8 3.2 %all-to-all-start.1 = ((f32[32,1,128]{2,1,0:T(1,128)}), f32[32,1,128]{2,1,0:T(1,128)S(1)}, u32[]{:S(2)}, u32[]{:S(2)}) async-start(f32[32,1,128]{2,1,0:T(1,128)} %bitcast.16), calls=%async_computation.1 | async-start | bytes 32768 | tf_op jit(solution)/shard_map/all_to_all | solution.py:695
  23.1 1.6 %collective-permute-start.5 = (f32[16,256]{1,0:T(8,128)S(1)}, f32[16,256]{1,0:T(8,128)S(1)}, u32[]{:S(2)}, u32[]{:S(2)}) collective-permute-start(f32[16,256]{1,0:T(8,128)S(1)} %get-tuple-element.46.refs_2_), channel_id=1, source_target_pairs={{0,3},{1,2},{2,1},{3,0},{4,7},{5,6},{6,5},{7,4},{8,11},{9,10},{10,... | collective-permute-start | bytes 49160 | tf_op jit(solution)/shard_map/ppermute | solution.py:697
  24.6 0.4 collective-permute-start.4
  25.0 0.8 %shard_map.114 = (f32[16,256]{1,0:T(8,128)S(1)}, f32[48,256]{1,0:T(8,128)S(1)}) custom-call(s32[1]{0:T(128)S(6)} %copy.15.refs_1_.refs_0_, s32[1]{0:T(128)} %bitcast.refs_2_.refs_1_, f32[16,256]{1,0:T(8,128)S(1)} %get-tuple-element.46.refs_2_, bf16[4,144,512]{2,1,0:T(8,128)(2,1)S(1)} %get-tuple-element.47.refs_3_.refs_6_, ...), custom_call_target="tpu_custom_call" | custom-call | tf_op jit(solution)/shard_map/pallas_call | solution.py:657
  25.8 0.1 collective-permute-start.3
  25.9 0.4 collective-permute-done.5.refs_11_
  26.3 0.0 collective-permute-done.4.refs_10_
  26.3 0.7 %collective-permute-done.3.refs_9_ = f32[16,256]{1,0:T(8,128)S(1)} collective-permute-done((f32[16,256]{1,0:T(8,128)S(1)}, f32[16,256]{1,0:T(8,128)S(1)}, u32[]{:S(2)}, u32[]{:S(2)}) %collective-permute-start.3) | collective-permute-done | bytes 16416 | tf_op jit(solution)/shard_map/ppermute | solution.py:711
  27.0 0.0 copy-start
  27.0 0.6 %copy-done = f32[16,256]{1,0:T(8,128)} copy-done((f32[16,256]{1,0:T(8,128)}, f32[16,256]{1,0:T(8,128)S(1)}, u32[]{:S(2)}) %copy-start) | copy-done | bytes 16408
  27.6 2.6 %all-to-all-done.1 = f32[32,1,128]{2,1,0:T(1,128)S(1)} async-done(((f32[32,1,128]{2,1,0:T(1,128)}), f32[32,1,128]{2,1,0:T(1,128)S(1)}, u32[]{:S(2)}, u32[]{:S(2)}) %all-to-all-start.1) | async-done | bytes 16416 | tf_op jit(solution)/shard_map/all_to_all | solution.py:695
  30.2 0.0 copy-start.1
  30.2 0.7 %copy-done.1 = f32[16,256]{1,0:T(8,128)S(1)} copy-done((f32[16,256]{1,0:T(8,128)S(1)}, f32[16,256]{1,0:T(8,128)}, u32[]{:S(2)}) %copy-start.1) | copy-done | bytes 16408
  30.9 1.4 %shard_map.115 = (f32[272,128]{1,0:T(8,128)S(1)}, f32[32,128]{1,0:T(8,128)}, f32[16,256]{1,0:T(8,128)S(1)}, bf16[4,144,512]{2,1,0:T(8,128)(2,1)S(1)}, bf16[4,144...) custom-call(s32[1]{0:T(128)S(6)} %copy.15.refs_1_.refs_0_, s32[1]{0:T(128)} %bitcast.refs_2_.refs_1_, ...), custom_call_target="tpu_custom_call" | custom-call | tf_op jit(solution)/shard_map/pallas_call | solution.py:657
  32.3 3.8 %all-to-all-start.2 = ((f32[32,1,128]{2,1,0:T(1,128)}), f32[32,1,128]{2,1,0:T(1,128)S(1)}, u32[]{:S(2)}, u32[]{:S(2)}) async-start(f32[32,1,128]{2,1,0:T(1,128)} %bitcast.17), calls=%async_computation.2 | async-start | bytes 32768 | tf_op jit(solution)/shard_map/all_to_all | solution.py:695
  36.1 0.8 %shard_map.116 = (f32[16,256]{1,0:T(8,128)S(1)}, f32[48,256]{1,0:T(8,128)S(1)}) custom-call(s32[1]{0:T(128)S(6)} %copy.15.refs_1_.refs_0_, s32[1]{0:T(128)} %bitcast.refs_2_.refs_1_, f32[16,256]{1,0:T(8,128)S(1)} %get-tuple-element.57.refs_2_, bf16[4,144,512]{2,1,0:T(8,128)(2,1)S(1)} %get-tuple-element.58.refs_3_.refs_6_, ...), custom_call_target="tpu_custom_call" | custom-call | tf_op jit(solution)/shard_map/pallas_call | solution.py:657
  36.9 0.3 collective-permute-start.6
  37.2 1.6 %collective-permute-start.8 = (f32[16,256]{1,0:T(8,128)S(1)}, f32[16,256]{1,0:T(8,128)S(1)}, u32[]{:S(2)}, u32[]{:S(2)}) collective-permute-start(f32[16,256]{1,0:T(8,128)S(1)} %get-tuple-element.57.refs_2_), channel_id=1, source_target_pairs={{0,3},{1,2},{2,1},{3,0},{4,7},{5,6},{6,5},{7,4},{8,11},{9,10},{10,... | collective-permute-start | bytes 49160 | tf_op jit(solution)/shard_map/ppermute | solution.py:697
  38.8 0.1 collective-permute-start.7
  38.9 0.0 collective-permute-done.6.refs_9_
  38.9 1.4 %collective-permute-done.8.refs_11_ = f32[16,256]{1,0:T(8,128)S(1)} collective-permute-done((f32[16,256]{1,0:T(8,128)S(1)}, f32[16,256]{1,0:T(8,128)S(1)}, u32[]{:S(2)}, u32[]{:S(2)}) %collective-permute-start.8) | collective-permute-done | bytes 16416 | tf_op jit(solution)/shard_map/ppermute | solution.py:697
  40.3 0.0 collective-permute-done.7.refs_10_
  40.3 2.9 %all-to-all-done.2 = f32[32,1,128]{2,1,0:T(1,128)S(1)} async-done(((f32[32,1,128]{2,1,0:T(1,128)}), f32[32,1,128]{2,1,0:T(1,128)S(1)}, u32[]{:S(2)}, u32[]{:S(2)}) %all-to-all-start.2) | async-done | bytes 16416 | tf_op jit(solution)/shard_map/all_to_all | solution.py:695
  43.2 1.4 %shard_map.117 = (f32[3,4096]{1,0:T(4,128)}, f32[3,4096]{1,0:T(4,128)}, f32[9,4096]{1,0:T(8,128)}, f32[9,4096]{1,0:T(8,128)}) custom-call(s32[1]{0:T(128)S(6)} %copy.15.refs_1_.refs_0_, s32[1]{0:T(128)} %bitcast.refs_2_.refs_1_, f32[272,128]{1,0:T(8,128)S(1)} %get-tuple-element.55.refs_2_, f32[32,128]{1,0:T(8,128)S(1)} %bitcast.14, ...), custom_call_target="tpu_custom_call" | custom-call | tf_op jit(solution)/shard_map/pallas_call | solution.py:657
Async XLA Ops:
  3.6 14.4 %all-to-all-start = ((f32[32,1,128]{2,1,0:T(1,128)}), f32[32,1,128]{2,1,0:T(1,128)S(1)}, u32[]{:S(2)}, u32[]{:S(2)}) async-start(f32[32,1,128]{2,1,0:T(1,128)} %bitcast.18), calls=%async_computation | async-start | bytes 32768 | tf_op jit(solution)/shard_map/all_to_all | solution.py:695
  10.9 3.6 %collective-permute-start.2 = (f32[16,256]{1,0:T(8,128)S(1)}, f32[16,256]{1,0:T(8,128)S(1)}, u32[]{:S(2)}, u32[]{:S(2)}) collective-permute-start(f32[16,256]{1,0:T(8,128)S(1)} %get-tuple-element.36.refs_3_), channel_id=1, source_target_pairs={{0,3},{1,2},{2,1},{3,0},{4,7},{5,6},{6,5},{7,4},{8,11},{9,10},{10,... | collective-permute-start | bytes 49160 | tf_op jit(solution)/shard_map/ppermute | solution.py:697
  12.5 2.0 %collective-permute-start.1 = (f32[16,256]{1,0:T(8,128)S(1)}, f32[16,256]{1,0:T(8,128)S(1)}, u32[]{:S(2)}, u32[]{:S(2)}) collective-permute-start(f32[16,256]{1,0:T(8,128)S(1)} %get-tuple-element.36.refs_3_), channel_id=1, source_target_pairs={{3,4},{7,8},{11,12},{15,16},{19,20},{23,24},{27,28},{2,5},{6,9},{1... | collective-permute-start | bytes 49160 | tf_op jit(solution)/shard_map/ppermute | solution.py:696
  14.3 1.2 %collective-permute-start = (f32[16,256]{1,0:T(8,128)S(1)}, f32[16,256]{1,0:T(8,128)S(1)}, u32[]{:S(2)}, u32[]{:S(2)}) collective-permute-start(f32[16,256]{1,0:T(8,128)S(1)} %get-tuple-element.43), channel_id=1, source_target_pairs={{0,1},{1,0},{2,3},{3,2},{4,5},{5,4},{6,7},{7,6},{8,9},{9,8},{10,11... | collective-permute-start | bytes 49160 | tf_op jit(solution)/shard_map/ppermute | solution.py:711
  19.8 10.4 %all-to-all-start.1 = ((f32[32,1,128]{2,1,0:T(1,128)}), f32[32,1,128]{2,1,0:T(1,128)S(1)}, u32[]{:S(2)}, u32[]{:S(2)}) async-start(f32[32,1,128]{2,1,0:T(1,128)} %bitcast.16), calls=%async_computation.1 | async-start | bytes 32768 | tf_op jit(solution)/shard_map/all_to_all | solution.py:695
  23.1 3.2 %collective-permute-start.5 = (f32[16,256]{1,0:T(8,128)S(1)}, f32[16,256]{1,0:T(8,128)S(1)}, u32[]{:S(2)}, u32[]{:S(2)}) collective-permute-start(f32[16,256]{1,0:T(8,128)S(1)} %get-tuple-element.46.refs_2_), channel_id=1, source_target_pairs={{0,3},{1,2},{2,1},{3,0},{4,7},{5,6},{6,5},{7,4},{8,11},{9,10},{10,... | collective-permute-start | bytes 49160 | tf_op jit(solution)/shard_map/ppermute | solution.py:697
  24.6 1.7 %collective-permute-start.4 = (f32[16,256]{1,0:T(8,128)S(1)}, f32[16,256]{1,0:T(8,128)S(1)}, u32[]{:S(2)}, u32[]{:S(2)}) collective-permute-start(f32[16,256]{1,0:T(8,128)S(1)} %get-tuple-element.46.refs_2_), channel_id=1, source_target_pairs={{3,4},{7,8},{11,12},{15,16},{19,20},{23,24},{27,28},{2,5},{6,9},{1... | collective-permute-start | bytes 49160 | tf_op jit(solution)/shard_map/ppermute | solution.py:696
  25.8 1.2 %collective-permute-start.3 = (f32[16,256]{1,0:T(8,128)S(1)}, f32[16,256]{1,0:T(8,128)S(1)}, u32[]{:S(2)}, u32[]{:S(2)}) collective-permute-start(f32[16,256]{1,0:T(8,128)S(1)} %get-tuple-element.53), channel_id=1, source_target_pairs={{0,1},{1,0},{2,3},{3,2},{4,5},{5,4},{6,7},{7,6},{8,9},{9,8},{10,11... | collective-permute-start | bytes 49160 | tf_op jit(solution)/shard_map/ppermute | solution.py:711
  27.0 0.6 %copy-start = (f32[16,256]{1,0:T(8,128)}, f32[16,256]{1,0:T(8,128)S(1)}, u32[]{:S(2)}) copy-start(f32[16,256]{1,0:T(8,128)S(1)} %collective-permute-done.3.refs_9_) | copy-start | bytes 49156
  30.2 0.7 %copy-start.1 = (f32[16,256]{1,0:T(8,128)S(1)}, f32[16,256]{1,0:T(8,128)}, u32[]{:S(2)}) copy-start(f32[16,256]{1,0:T(8,128)} %copy-done) | copy-start | bytes 49156
  32.3 10.9 %all-to-all-start.2 = ((f32[32,1,128]{2,1,0:T(1,128)}), f32[32,1,128]{2,1,0:T(1,128)S(1)}, u32[]{:S(2)}, u32[]{:S(2)}) async-start(f32[32,1,128]{2,1,0:T(1,128)} %bitcast.17), calls=%async_computation.2 | async-start | bytes 32768 | tf_op jit(solution)/shard_map/all_to_all | solution.py:695
  36.9 2.0 %collective-permute-start.6 = (f32[16,256]{1,0:T(8,128)S(1)}, f32[16,256]{1,0:T(8,128)S(1)}, u32[]{:S(2)}, u32[]{:S(2)}) collective-permute-start(f32[16,256]{1,0:T(8,128)S(1)} %get-tuple-element.63), channel_id=1, source_target_pairs={{0,1},{1,0},{2,3},{3,2},{4,5},{5,4},{6,7},{7,6},{8,9},{9,8},{10,11... | collective-permute-start | bytes 49160 | tf_op jit(solution)/shard_map/ppermute | solution.py:711
  37.2 3.2 %collective-permute-start.8 = (f32[16,256]{1,0:T(8,128)S(1)}, f32[16,256]{1,0:T(8,128)S(1)}, u32[]{:S(2)}, u32[]{:S(2)}) collective-permute-start(f32[16,256]{1,0:T(8,128)S(1)} %get-tuple-element.57.refs_2_), channel_id=1, source_target_pairs={{0,3},{1,2},{2,1},{3,0},{4,7},{5,6},{6,5},{7,4},{8,11},{9,10},{10,... | collective-permute-start | bytes 49160 | tf_op jit(solution)/shard_map/ppermute | solution.py:697
  38.8 1.5 %collective-permute-start.7 = (f32[16,256]{1,0:T(8,128)S(1)}, f32[16,256]{1,0:T(8,128)S(1)}, u32[]{:S(2)}, u32[]{:S(2)}) collective-permute-start(f32[16,256]{1,0:T(8,128)S(1)} %get-tuple-element.57.refs_2_), channel_id=1, source_target_pairs={{3,4},{7,8},{11,12},{15,16},{19,20},{23,24},{27,28},{2,5},{6,9},{1... | collective-permute-start | bytes 49160 | tf_op jit(solution)/shard_map/ppermute | solution.py:696

commit v4 on v3

--- a/solution.py
+++ b/solution.py
@@ -118,9 +118,7 @@
     speed = jnp.max(jnp.where(mass > 0.0, speed, 0.0), axis=0, keepdims=True)
     speed = jnp.max(speed, axis=1, keepdims=True)
     outbox[...] = jnp.broadcast_to(speed, outbox.shape)
-    copy = pltpu.make_async_copy(outbox, speeds, sem)
-    copy.start()
-    return copy
+    pltpu.make_async_copy(outbox, speeds, sem).start()
 
 
 def halves(quarters):
@@ -204,9 +202,7 @@
         far[:, TILE * b : TILE * (b + 1)] = total
     nodes = bins * TILE
     width = far.shape[1]
-    if meta is None:
-        meta = jnp.zeros((1, width), F32)
-    far[:, nodes:width] = jnp.broadcast_to(meta, (16, width))[:, nodes:width]
+    far[:, nodes:width] = jnp.broadcast_to(meta[0:1, nodes:width], (16, width - nodes))
 
 
 def rest_of_grid(device, bins, meta, far, highs, lows, along, channels, near):
@@ -229,9 +225,7 @@
         middle.append(total[16:32])
     nodes = bins * TILE
     width = near.shape[1]
-    if meta is None:
-        meta = jnp.zeros((1, width), F32)
-    near[:, nodes:width] = jnp.broadcast_to(meta, (16, width))[:, nodes:width]
+    near[:, nodes:width] = jnp.broadcast_to(meta[0:1, nodes:width], (16, width - nodes))
     near_part, far_part = near[:, 0:nodes], far[:, 0:nodes]
     low = jnp.where(odd, near_part, far_part)
     high = jnp.where(odd, far_part, near_part)
@@ -280,20 +274,21 @@
     return left_block, right_block
 
 
-def halo_blocks(block, bins):
+def block_numbers(row, bins):
     lane = iota((1, LANES), 1)
     return [
-        jnp.max(jnp.where(lane == META + b, block[7:8, LANES : 2 * LANES], 0.0), axis=1, keepdims=True)
+        jnp.max(jnp.where(lane == META + b, row[:, LANES : 2 * LANES], 0.0), axis=1, keepdims=True)
         for b in range(bins)
     ]
 
 
 def to_particles(
-    state, device, bins, device_total, geometry, own, sides, speeds, blocks_around,
-    highs, lows, along, shuffle,
-):
-    rows = state[0].shape[0]
+    live, old_ref, device, bins, device_total, geometry, own, sides, speeds, blocks_around,
+    highs, lows, along, shuffle, started, finish,
+):
+    rows = old_ref.shape[0] // ROWS
     quarters = rows // bins
+    state = read_state(old_ref, rows)
     width = bins * SLOT
     nodes = bins * TILE
     fastest = jnp.max(speeds[...], axis=0, keepdims=True)
@@ -335,46 +330,51 @@
     )
 
     span = 8 * rows
+    blocks = []
     for b in range(bins):
         begin = (b * SLOT) // LANES * LANES
         block = paired[:, begin : begin + LANES]
         if b * SLOT > begin:
             block = pltpu.roll(block, LANES - (b * SLOT - begin), 1)
         block = block[:, 0:TILE]
-        count = block.shape[0]
         high = block.astype(BF16)
         kept = high.astype(F32)
-        stacked = jnp.concatenate([kept, block - kept], axis=0).astype(BF16)
-        for first_quarter, wide, lanes in halves(quarters):
-            row = b * quarters + first_quarter
-            shape = (8, wide * LANES)
-            even = iota(shape, 0) < 4
-            weights, weights_moved = [
-                [
-                    jnp.where(
-                        even,
-                        spread(along, rows * (begin + 2 * g) + row, wide),
-                        spread(along, rows * (begin + 2 * g + 1) + row, wide),
-                    )
-                    for g in range(3)
-                ]
-                for begin in (0, 6)
-            ]
-            sums = []
-            for kind in range(3):
-                right_high = highs[b, pl.ds(kind * TILE, TILE), lanes]
-                right_low = lows[b, pl.ds(kind * TILE, TILE), lanes]
-                product = dot_nn(stacked, right_high)
-                product = product[0:count] + product[count : 2 * count] + dot_nn(high, right_low)
-                groups = [product[8 * g : 8 * g + 8] for g in range(3)]
-                sums.append(sum(w * group for w, group in zip(weights, groups)))
-                if kind == 0:
-                    moved_sum = sum(w * group for w, group in zip(weights_moved, groups))
-            sums.append(moved_sum)
-            for kind in range(4):
-                for q in range(wide):
-                    target = kind * span + 8 * (row + q)
-                    shuffle[pl.ds(target, 8), :] = sums[kind][:, LANES * q : LANES * (q + 1)]
+        blocks.append((jnp.concatenate([kept, block - kept], axis=0).astype(BF16), high))
+
+    def gather(kinds):
+        for b in range(bins):
+            stacked, high = blocks[b]
+            count = high.shape[0]
+            for first_quarter, wide, lanes in halves(quarters):
+                row = b * quarters + first_quarter
+                even = iota((8, wide * LANES), 0) < 4
+
+                def pair_weights_of(begin):
+                    return [
+                        jnp.where(
+                            even,
+                            spread(along, rows * (begin + 2 * g) + row, wide),
+                            spread(along, rows * (begin + 2 * g + 1) + row, wide),
+                        )
+                        for g in range(3)
+                    ]
+
+                weights = pair_weights_of(0)
+                for kind in kinds:
+                    right_high = highs[b, pl.ds(kind * TILE, TILE), lanes]
+                    right_low = lows[b, pl.ds(kind * TILE, TILE), lanes]
+                    product = dot_nn(stacked, right_high)
+                    product = product[0:count] + product[count : 2 * count]
+                    product = product + dot_nn(high, right_low)
+                    groups = [product[8 * g : 8 * g + 8] for g in range(3)]
+                    sums = [(kind, sum(w * group for w, group in zip(weights, groups)))]
+                    if kind == 0:
+                        moved = zip(pair_weights_of(6), groups)
+                        sums.append((3, sum(w * group for w, group in moved)))
+                    for target, value in sums:
+                        for q in range(wide):
+                            place = target * span + 8 * (row + q)
+                            shuffle[pl.ds(place, 8), :] = value[:, LANES * q : LANES * (q + 1)]
 
     def take(kind, c):
         return (
@@ -382,24 +382,37 @@
             + shuffle[pl.ds(kind * span + 5 + c, rows, stride=8), :]
         )
 
-    velocity = [take(0, c) for c in range(3)]
-    affine = [None] * 9
-    for c in range(3):
-        affine[3 * c] = 4.0 * take(3, c)
-        affine[3 * c + 1] = 4.0 * take(1, c)
-        affine[3 * c + 2] = 4.0 * take(2, c)
-    old = state[DEF : DEF + 9]
-    deform = []
-    for r in range(3):
+    gather((0, 1, 2) if live is None else (0,))
+    started([take(0, c) for c in range(3)])
+
+    def rest():
+        if live is not None:
+            gather((1, 2))
+        velocity = [take(0, c) for c in range(3)]
+        affine = [None] * 9
         for c in range(3):
-            change = (
-                affine[3 * r] * old[c] + affine[3 * r + 1] * old[3 + c] + affine[3 * r + 2] * old[6 + c]
-            )
-            deform.append(old[3 * r + c] + time_step * change)
-    steps = [time_step * velocity[c] for c in range(3)]
-    moved = [state[c] + steps[c] for c in range(3)]
-    travelled = [state[TRAV + c] + steps[c] for c in range(3)]
-    return moved + deform + [state[MASS], state[VOL]] + travelled, velocity, affine
+            affine[3 * c] = 4.0 * take(3, c)
+            affine[3 * c + 1] = 4.0 * take(1, c)
+            affine[3 * c + 2] = 4.0 * take(2, c)
+        old = state[DEF : DEF + 9]
+        deform = []
+        for r in range(3):
+            for c in range(3):
+                change = (
+                    affine[3 * r] * old[c]
+                    + affine[3 * r + 1] * old[3 + c]
+                    + affine[3 * r + 2] * old[6 + c]
+                )
+                deform.append(old[3 * r + c] + time_step * change)
+        steps = [time_step * velocity[c] for c in range(3)]
+        moved = [state[c] + steps[c] for c in range(3)]
+        travelled = [state[TRAV + c] + steps[c] for c in range(3)]
+        finish(moved + deform + [state[MASS], state[VOL]] + travelled, velocity, affine)
+
+    if live is None:
+        rest()
+    else:
+        pl.when(live[0] >= 0)(rest)
 
 
 def read_state(ref, rows):
@@ -422,49 +435,65 @@
 
 def first_kernel(
     bins, device_total, blocks, live, device, x_ref, v_ref, f_ref, c_ref, m_ref, vol_ref,
-    state_ref, speeds, far, highs, lows, along, channels, across, outbox, sem, motion_ref,
+    state_ref, motion_ref, speeds, meta, outbox, sem,
 ):
     rows = state_ref.shape[0] // ROWS
     quarters = rows // bins
-    for ref, count, kept, begin in (
-        (x_ref, 3, state_ref, POS),
-        (f_ref, 9, state_ref, DEF),
-        (v_ref, 3, motion_ref, 0),
-        (c_ref, 9, motion_ref, 3),
-    ):
+
+    def relay(ref, count, kept, begin):
         for number in range(count):
             for s in range(rows):
                 target = rows * (begin + number) + s
                 kept[pl.ds(target, 1), :] = ref[pl.ds(number, 1), pl.ds(LANES * s, LANES)]
-    for ref, number in ((m_ref, MASS), (vol_ref, VOL)):
+
+    def relay_flat(ref, number):
         for b in range(bins):
             alive = jnp.where(b < live[0], 1.0, 0.0)
             for q in range(quarters):
                 s = quarters * b + q
                 piece = ref[pl.ds(LANES * s, LANES)].reshape(1, LANES)
                 state_ref[pl.ds(rows * number + s, 1), :] = piece * alive
-    home = jnp.zeros((rows, LANES), F32)
-    home_y, home_z = home, home
-    row_bin = iota((rows, LANES), 0) // quarters
-    for b in range(bins):
-        block = blocks[b]
-        block_y = block // BZ
-        block_z = block - BZ * block_y
-        home_y = jnp.where(row_bin == b, (4 * block_y).astype(F32), home_y)
-        home_z = jnp.where(row_bin == b, (4 * block_z).astype(F32), home_z)
-    anchors = (home + (4 * device).astype(F32), home_y, home_z)
-    for axis in range(3):
-        place = pl.ds(rows * axis, rows)
-        state_ref[place, :] = state_ref[place, :] - anchors[axis]
-        state_ref[pl.ds(rows * (TRAV + axis), rows), :] = home
-    state = read_state(state_ref, rows)
+
+    relay(v_ref, 3, motion_ref, 0)
+    relay_flat(m_ref, MASS)
+    motion = [motion_ref[pl.ds(rows * number, rows), :] for number in range(3)]
+    send_speed(motion, state_ref[pl.ds(rows * MASS, rows), :], speeds, outbox, sem)
+
+    @pl.when(live[0] >= 0)
+    def _():
+        relay(x_ref, 3, state_ref, POS)
+        relay(f_ref, 9, state_ref, DEF)
+        relay(c_ref, 9, motion_ref, 3)
+        relay_flat(vol_ref, VOL)
+        home = jnp.zeros((rows, LANES), F32)
+        home_y, home_z = home, home
+        row_bin = iota((rows, LANES), 0) // quarters
+        for b in range(bins):
+            block = blocks[b]
+            block_y = block // BZ
+            block_z = block - BZ * block_y
+            home_y = jnp.where(row_bin == b, (4 * block_y).astype(F32), home_y)
+            home_z = jnp.where(row_bin == b, (4 * block_z).astype(F32), home_z)
+        anchors = (home + (4 * device).astype(F32), home_y, home_z)
+        for axis in range(3):
+            place = pl.ds(rows * axis, rows)
+            state_ref[place, :] = state_ref[place, :] - anchors[axis]
+            state_ref[pl.ds(rows * (TRAV + axis), rows), :] = home
+        meta[...] = jnp.broadcast_to(block_row(blocks, bins, meta.shape[1]), meta.shape)
+
+    pltpu.make_async_copy(outbox, speeds, sem).wait()
+
+
+def scatter_kernel(
+    bins, device_total, live, device, state_ref, motion_ref, meta, far, highs, lows, along,
+    channels, across,
+):
+    rows = state_ref.shape[0] // ROWS
     motion = [motion_ref[pl.ds(rows * number, rows), :] for number in range(12)]
-    copy = send_speed(motion[0:3], state[MASS], speeds, outbox, sem)
     to_grid(
-        state, motion[0:3], motion[3:12], state_ref, device, bins, block_row(blocks, bins, far.shape[1]), far, highs, lows,
-        along, channels, across,
-    )
-    copy.wait()
+        read_state(state_ref, rows), motion[0:3], motion[3:12], state_ref, device, bins, meta, far,
+        highs, lows, along, channels, across,
+    )
 
 
 def place_own(own, low, middle, high, selector):
@@ -474,19 +503,18 @@
 
 
 def first_rest_kernel(
-    bins, device_total, blocks, live, device, far, highs, lows, along, channels,
+    bins, device_total, live, device, meta, far, highs, lows, along, channels,
     near, own, geometry, home,
 ):
     low, middle, high = rest_of_grid(
-        device, bins, block_row(blocks, bins, near.shape[1]), far, highs, lows, along, channels,
-        near,
+        device, bins, meta, far, highs, lows, along, channels, near
     )
     width = bins * SLOT
     position = iota((1, width), 1)
     column_bin = position // SLOT
     column_node = position - SLOT * column_bin
     column_valid = (column_node < TILE) & (column_node % 8 < 6)
-    own_blocks = [blocks[b].astype(F32) for b in range(bins)]
+    own_blocks = block_numbers(meta[0:1, :], bins)
     column_block = jnp.zeros((1, width), F32)
     for b in range(bins):
         column_block = jnp.where(column_bin == b, own_blocks[b], column_block)
@@ -508,62 +536,60 @@
 
 
 def rest_kernel(
-    bins, device_total, live, device, far, highs, lows, along, channels, home, near, own
+    bins, device_total, live, device, meta, far, highs, lows, along, channels, home, near, own
 ):
     low, middle, high = rest_of_grid(
-        device, bins, None, far, highs, lows, along, channels, near
+        device, bins, meta, far, highs, lows, along, channels, near
     )
     place_own(own, low, middle, high, home[...])
 
 
 def second_kernel(
-    bins, device_total, live, device, old_ref, speeds, own, geometry, old_highs, old_lows,
-    old_along, near, outer, inner, state_ref, new_speeds, new_far, highs, lows, along, channels,
-    sides_ref, across, outbox, sem,
+    bins, device_total, live, device, old_ref, speeds, own, geometry, highs, lows, along,
+    near, outer, inner, state_ref, motion_ref, new_speeds, sides_ref, shuffle, outbox, sem,
 ):
     around = halos(near, outer, inner, device, device_total)
     key = geometry[0:1, :]
-    sides = [placing(halo_blocks(block, bins), key, bins) for block in around]
+    sides = [placing(block_numbers(block[7:8, :], bins), key, bins) for block in around]
     for side in range(2):
         sides_ref[side] = sides[side]
     advance(
-        bins, device_total, device, old_ref, speeds, own, geometry, old_highs, old_lows,
-        old_along, around, sides, state_ref, new_speeds, new_far, highs, lows, along, channels,
-        across, outbox, sem,
+        live, bins, device_total, device, old_ref, speeds, own, geometry, highs, lows, along, around,
+        sides, state_ref, motion_ref, new_speeds, shuffle, outbox, sem,
     )
 
 
 def later_kernel(
-    bins, device_total, live, device, old_ref, speeds, own, geometry, old_highs, old_lows,
-    old_along, near, outer, inner, sides_ref, state_ref, new_speeds, new_far, highs, lows, along, channels,
-    across, outbox, sem,
+    bins, device_total, live, device, old_ref, speeds, own, geometry, highs, lows, along,
+    near, outer, inner, sides_ref, state_ref, motion_ref, new_speeds, shuffle, outbox, sem,
 ):
     around = halos(near, outer, inner, device, device_total)
     sides = [sides_ref[0], sides_ref[1]]
     advance(
-        bins, device_total, device, old_ref, speeds, own, geometry, old_highs, old_lows,
-        old_along, around, sides, state_ref, new_speeds, new_far, highs, lows, along, channels,
-        across, outbox, sem,
+        live, bins, device_total, device, old_ref, speeds, own, geometry, highs, lows, along, around,
+        sides, state_ref, motion_ref, new_speeds, shuffle, outbox, sem,
     )
 
 
 def advance(
-    bins, device_total, device, old_ref, speeds, own, geometry, old_highs, old_lows,
-    old_along, around, sides, state_ref, new_speeds, far, highs, lows, along, channels,
-    across, outbox, sem,
+    live, bins, device_total, device, old_ref, speeds, own, geometry, highs, lows, along, around,
+    sides, state_ref, motion_ref, new_speeds, shuffle, outbox, sem,
 ):
     rows = state_ref.shape[0] // ROWS
-    state = read_state(old_ref, rows)
-    state, velocity, affine = to_particles(
-        state, device, bins, device_total, geometry, own, sides, speeds, around, old_highs,
-        old_lows, old_along, channels,
-    )
-    write_state(state_ref, state)
-    copy = send_speed(velocity, state[MASS], new_speeds, outbox, sem)
-    to_grid(
-        state, velocity, affine, state_ref, device, bins, None, far, highs, lows, along, channels, across
-    )
-    copy.wait()
+
+    def started(velocity):
+        send_speed(velocity, old_ref[pl.ds(rows * MASS, rows), :], new_speeds, outbox, sem)
+
+    def finish(state, velocity, affine):
+        write_state(state_ref, state)
+        for number, value in enumerate(velocity + affine):
+            motion_ref[pl.ds(rows * number, rows), :] = value
+
+    to_particles(
+        live, old_ref, device, bins, device_total, geometry, own, sides, speeds, around, highs,
+        lows, along, shuffle, started, finish,
+    )
+    pltpu.make_async_copy(outbox, new_speeds, sem).wait()
 
 
 def last_kernel(
@@ -572,28 +598,31 @@
 ):
     rows = old_ref.shape[0] // ROWS
     quarters = rows // bins
-    state = read_state(old_ref, rows)
-    state, velocity, affine = to_particles(
-        state, device, bins, device_total, geometry, own, [sides_ref[0], sides_ref[1]], speeds,
-        halos(near, outer, inner, device, device_total), highs, lows, along, shuffle,
-    )
     row_bin = iota((rows, LANES), 0) // quarters
     alive = row_bin < live[0]
     half = rows * LANES
-    results = (
-        (d_out, state[TRAV : TRAV + 3]),
-        (v_out, velocity),
-        (f_out, state[DEF : DEF + 9]),
-        (c_out, affine),
-    )
-    for ref, values in results:
-        count = len(values)
-        for number in range(count):
-            value = jnp.where(alive, values[number], 0.0)
-            for s in range(rows):
-                ref[pl.ds(number, 1), pl.ds(LANES * s, LANES)] = value[s : s + 1, :]
-        total = ref.shape[1]
-        ref[:, pl.ds(half, total - half)] = jnp.zeros((count, total - half), F32)
+
+    def finish(state, velocity, affine):
+        results = (
+            (d_out, state[TRAV : TRAV + 3]),
+            (v_out, velocity),
+            (f_out, state[DEF : DEF + 9]),
+            (c_out, affine),
+        )
+        for ref, values in results:
+            count = len(values)
+            for number in range(count):
+                value = jnp.where(alive, values[number], 0.0)
+                for s in range(rows):
+                    ref[pl.ds(number, 1), pl.ds(LANES * s, LANES)] = value[s : s + 1, :]
+            total = ref.shape[1]
+            ref[:, pl.ds(half, total - half)] = jnp.zeros((count, total - half), F32)
+
+    to_particles(
+        None, old_ref, device, bins, device_total, geometry, own, [sides_ref[0], sides_ref[1]], speeds,
+        halos(near, outer, inner, device, device_total), highs, lows, along, shuffle,
+        lambda velocity: None, finish,
+    )
 
 
 def local(positions, velocity, deformation, affine, particle_mass, volume, bin_block, live_count):
@@ -606,16 +635,16 @@
     nodes = bins * TILE
     width = bins * SLOT
     message = ((16, -(-(nodes + LANES // 2) // LANES) * LANES), F32)
-    held = [
-        ((ROWS * rows, LANES), F32),
-        ((device_total, LANES), F32),
+    speeds_shape = ((device_total, LANES), F32)
+    held = [((ROWS * rows, LANES), F32), ((12 * rows, LANES), F32), speeds_shape]
+    grid_held = [
         message,
         ((bins, 3 * TILE, per_bin), BF16),
         ((bins, 3 * TILE, per_bin), BF16),
         ((12 * rows, LANES), F32),
         ((4 * 8 * rows, LANES), F32),
     ]
-    speeds_shape = held[1]
+    meta_shape = ((8, message[0][1]), F32)
     own_shape = ((48, width), F32)
     geometry_shape = ((24, width), F32)
     home_shape = ((nodes, width), BF16)
@@ -623,11 +652,8 @@
     smem = pl.BlockSpec(memory_space=pltpu.SMEM)
     vmem = pl.BlockSpec(memory_space=pltpu.VMEM)
     anywhere = pl.BlockSpec(memory_space=pl.ANY)
-    working = [
-        pltpu.VMEM((12 * rows, LANES), F32),
-        pltpu.VMEM((device_total, LANES), F32),
-        pltpu.SemaphoreType.DMA,
-    ]
+    shuffle = pltpu.VMEM((4 * 8 * rows, LANES), F32)
+    sending = [pltpu.VMEM((device_total, LANES), F32), pltpu.SemaphoreType.DMA]
     bin_block = bin_block if INTERPRET else pltpu.with_memory_space_constraint(bin_block, pltpu.HBM)
     me = lax.axis_index("space").astype(jnp.int32).reshape(1)
 
@@ -680,26 +706,33 @@
     outer_pairs = outer_pairs + [(0, 1), (length - 2, length - 1)]
     outer_pairs = outer_pairs + [(j, i) for i, j in outer_pairs]
 
-    results = call(
+    *results, meta = call(
         first_kernel,
         (bin_block, live_count, me),
         (positions, velocity, deformation, affine, particle_mass, volume),
-        held,
-        working + [pltpu.VMEM((12 * rows, LANES), F32)],
+        held + [meta_shape],
+        sending,
         [first_half(3), first_half(3), first_half(9), first_half(9), flat_half, flat_half],
     )
     sides = ()
     for step in range(STEPS):
-        state, speeds, far, highs, lows, along, channels = results[:7]
-        sides = sides + tuple(results[7:])
+        state, motion, speeds = results[:3]
+        sides = sides + tuple(results[3:])
         speeds = lax.all_to_all(speeds, "space", 0, 0, tiled=True)
+        far, highs, lows, along, channels = call(
+            scatter_kernel,
+            (live_count, me),
+            (state, motion, meta),
+            grid_held,
+            [pltpu.VMEM((12 * rows, LANES), F32)],
+        )
         from_outer = lax.ppermute(far, "space", outer_pairs)
         from_inner = lax.ppermute(far, "space", inner_pairs)
-        arguments = (far, highs, lows, along, channels)
+        arguments = (meta, far, highs, lows, along, channels)
         if step == 0:
             near, own, geometry, home = call(
                 first_rest_kernel,
-                (bin_block, live_count, me),
+                (live_count, me),
                 arguments,
                 [message, own_shape, geometry_shape, home_shape],
                 [],
@@ -709,14 +742,17 @@
                 rest_kernel, (live_count, me), arguments + (home,), [message, own_shape], []
             )
         from_near = lax.ppermute(near, "space", swap_pairs)
-        arguments = (state, speeds, own, geometry, highs, lows, along, from_near, from_outer, from_inner, *sides)
+        arguments = (
+            state, speeds, own, geometry, highs, lows, along, from_near, from_outer, from_inner,
+            *sides,
+        )
         if step < STEPS - 1:
             results = call(
                 second_kernel if step == 0 else later_kernel,
                 (live_count, me),
                 arguments,
                 held + ([sides_shape] if step == 0 else []),
-                working,
+                [shuffle] + sending,
             )
     total = positions.shape[1]
     return call(
@@ -724,7 +760,7 @@
         (live_count, me),
         arguments,
         [((count, total), F32) for count in (3, 3, 9, 9)],
-        [pltpu.VMEM((4 * 8 * rows, LANES), F32)],
+        [shuffle],
         final=True,
     )
 

time: 45 us -> 45.8 us (1.018)
  starting transfers between devices: 20.6 us -> 23.3 us
  local copies, waits for them, and re-layouts: 1.32 us -> 0 us
    all_to_all x3, starting transfers between devices: 14.4 us -> 17.2 us  [local(): speeds = lax.all_to_all(speeds, 'space', 0, 0, tiled=True)]
    ppermute x3, waiting for transfers between devices: 1.77 us -> 4.24 us  [local(): from_inner = lax.ppermute(far, 'space', inner_pairs)]
    ppermute x3, waiting for transfers between devices: 1.77 us -> 0.01 us  [local(): from_near = lax.ppermute(near, 'space', swap_pairs)]
    unnamed x4 -> x0, local copies, waits for them, and re-layouts: 1.32 us -> none
    all_to_all x3, waiting for transfers between devices: 7.89 us -> 6.7 us  [local(): speeds = lax.all_to_all(speeds, 'space', 0, 0, tiled=True)]
    ppermute x3, starting transfers between devices: 0.91 us -> 0.35 us  [local(): from_outer = lax.ppermute(far, 'space', outer_pairs)]
    pallas_call x7 -> x10, Pallas kernels: 9.97 us -> 9.95 us  [call(): pl.pallas_call(kernel, in_specs=[smem] * len(scalars) + in_specs, out_sha...]
  transfers between devices with their start and end apart: 12 -> 12, of which waited for: 7 -> 6; matrix products, arithmetic and copies ran while one was open for 0% -> 0% of each run, Pallas kernels for 7% -> 9%
where the time goes in v4:
time: 45.8 us; the launch traced here: 45.5 us
  starting transfers between devices  23.3 us (51%)
  waiting for transfers between devices  11 us (24%)
  Pallas kernels  9.95 us (22%)
  between operations  1.34 us (3%)
    all_to_all x3, starting transfers between devices, local(): speeds = lax.all_to_all(speeds, 'space', 0, 0, tiled=True)  17.2 us
    pallas_call x10, Pallas kernels, call(): pl.pallas_call(kernel, in_specs=[smem] * len(scalars) + in_specs, out_sha...  9.95 us
    all_to_all x3, waiting for transfers between devices, local(): speeds = lax.all_to_all(speeds, 'space', 0, 0, tiled=True)  6.7 us
    ppermute x3, starting transfers between devices, local(): from_inner = lax.ppermute(far, 'space', inner_pairs)  4.89 us
    ppermute x3, waiting for transfers between devices, local(): from_inner = lax.ppermute(far, 'space', inner_pairs)  4.24 us
  transfers between devices with their start and end apart: 12, of which 6 were waited for; matrix products, arithmetic and copies ran while one was open for 0% of the time, Pallas kernels for 9%

profile of v4, /device:TPU:0, one launch (start us, length us, event | category | flops | bytes accessed | tf_op | source)
XLA Modules:
  0.0 45.5 jit_solution(13590934244889213638)
XLA Ops:
  1.3 1.8 %shard_map.111 = (f32[272,128]{1,0:T(8,128)S(1)}, f32[192,128]{1,0:T(8,128)S(1)}, f32[32,128]{1,0:T(8,128)}, f32[8,256]{1,0:T(8,128)S(1)}) custom-call(s32[8]{0:T(128)} %refs_0_.10, s32[1]{0:T(128)S(6)} %copy.15.refs_1_.refs_0_, s32[1]{0:T(128)} %bitcast.refs_2_.refs_1_, f32[3,4096]{1,0:T(4,128)} %refs_3_.1, f32[3,4096]{1,0:T(4,128)} %refs_4_.1, ...), custom_call_target="tpu_custom_call" | custom-call | tf_op jit(solution)/shard_map/pallas_call | solution.py:683
  3.0 7.3 %all-to-all-start = ((f32[32,1,128]{2,1,0:T(1,128)}), f32[32,1,128]{2,1,0:T(1,128)S(1)}, u32[]{:S(2)}, u32[]{:S(2)}) async-start(f32[32,1,128]{2,1,0:T(1,128)} %bitcast.18), calls=%async_computation | async-start | bytes 32768 | tf_op jit(solution)/shard_map/all_to_all | solution.py:721
  10.4 0.6 %shard_map.112 = (f32[16,256]{1,0:T(8,128)S(1)}, bf16[4,144,512]{2,1,0:T(8,128)(2,1)S(1)}, bf16[4,144,512]{2,1,0:T(8,128)(2,1)S(1)}, f32[192,128]{1,0:T(8,128)S(1)}, f32[512,128]{1,0:T(8,128)S(1)}) custom-call(s32[1]{0:T(128)S(6)} %copy.15.refs_1_.refs_0_, s32[1]{0:T(128)} %bitcast.refs_2_.refs_1_, f32[272,128]{1,0:T(8,128)S(1)} %get-tuple-element.38.refs_2_, ...), custom_call_target="tpu_custom_call" | custom-call | tf_op jit(solution)/shard_map/pallas_call | solution.py:683
  11.0 0.8 %shard_map.113 = (f32[16,256]{1,0:T(8,128)S(1)}, f32[48,256]{1,0:T(8,128)S(1)}, f32[24,256]{1,0:T(8,128)S(1)}, bf16[192,256]{1,0:T(8,128)(2,1)S(1)}) custom-call(s32[1]{0:T(128)S(6)} %copy.15.refs_1_.refs_0_, s32[1]{0:T(128)} %bitcast.refs_2_.refs_1_, f32[8,256]{1,0:T(8,128)S(1)} %get-tuple-element.40.refs_4_.refs_2_, ...), custom_call_target="tpu_custom_call" | custom-call | tf_op jit(solution)/shard_map/pallas_call | solution.py:683
  11.8 0.3 collective-permute-start
  12.1 1.6 %collective-permute-start.2 = (f32[16,256]{1,0:T(8,128)S(1)}, f32[16,256]{1,0:T(8,128)S(1)}, u32[]{:S(2)}, u32[]{:S(2)}) collective-permute-start(f32[16,256]{1,0:T(8,128)S(1)} %get-tuple-element.42.refs_3_), channel_id=1, source_target_pairs={{0,3},{1,2},{2,1},{3,0},{4,7},{5,6},{6,5},{7,4},{8,11},{9,10},{10,... | collective-permute-start | bytes 49160 | tf_op jit(solution)/shard_map/ppermute | solution.py:730
  13.7 0.1 collective-permute-start.1
  13.8 0.0 collective-permute-done.refs_9_
  13.8 1.4 %collective-permute-done.2.refs_11_ = f32[16,256]{1,0:T(8,128)S(1)} collective-permute-done((f32[16,256]{1,0:T(8,128)S(1)}, f32[16,256]{1,0:T(8,128)S(1)}, u32[]{:S(2)}, u32[]{:S(2)}) %collective-permute-start.2) | collective-permute-done | bytes 16416 | tf_op jit(solution)/shard_map/ppermute | solution.py:730
  15.2 0.0 collective-permute-done.1.refs_10_
  15.2 2.2 %all-to-all-done = f32[32,1,128]{2,1,0:T(1,128)S(1)} async-done(((f32[32,1,128]{2,1,0:T(1,128)}), f32[32,1,128]{2,1,0:T(1,128)S(1)}, u32[]{:S(2)}, u32[]{:S(2)}) %all-to-all-start) | async-done | bytes 16416 | tf_op jit(solution)/shard_map/all_to_all | solution.py:721
  17.5 1.4 %shard_map.114 = (f32[272,128]{1,0:T(8,128)S(1)}, f32[192,128]{1,0:T(8,128)S(1)}, f32[32,128]{1,0:T(8,128)}, bf16[2,192,256]{2,1,0:T(8,128)(2,1)S(1)}) custom-call(s32[1]{0:T(128)S(6)} %copy.15.refs_1_.refs_0_, s32[1]{0:T(128)} %bitcast.refs_2_.refs_1_, f32[272,128]{1,0:T(8,128)S(1)} %get-tuple-element.38.refs_2_, f32[32,128]{1,0:T(8,128)S(1)} %bitcast.14, ...), custom_call_target="tpu_custom_call" | custom-call | tf_op jit(solution)/shard_map/pallas_call | solution.py:683
  18.9 4.9 %all-to-all-start.1 = ((f32[32,1,128]{2,1,0:T(1,128)}), f32[32,1,128]{2,1,0:T(1,128)S(1)}, u32[]{:S(2)}, u32[]{:S(2)}) async-start(f32[32,1,128]{2,1,0:T(1,128)} %bitcast.16), calls=%async_computation.1 | async-start | bytes 32768 | tf_op jit(solution)/shard_map/all_to_all | solution.py:721
  23.8 0.6 %shard_map.115 = (f32[16,256]{1,0:T(8,128)S(1)}, bf16[4,144,512]{2,1,0:T(8,128)(2,1)S(1)}, bf16[4,144,512]{2,1,0:T(8,128)(2,1)S(1)}, f32[192,128]{1,0:T(8,128)S(1)}, f32[512,128]{1,0:T(8,128)S(1)}) custom-call(s32[1]{0:T(128)S(6)} %copy.15.refs_1_.refs_0_, s32[1]{0:T(128)} %bitcast.refs_2_.refs_1_, f32[272,128]{1,0:T(8,128)S(1)} %get-tuple-element.50.refs_2_, ...), custom_call_target="tpu_custom_call" | custom-call | tf_op jit(solution)/shard_map/pallas_call | solution.py:683
  24.4 0.8 %shard_map.116 = (f32[16,256]{1,0:T(8,128)S(1)}, f32[48,256]{1,0:T(8,128)S(1)}) custom-call(s32[1]{0:T(128)S(6)} %copy.15.refs_1_.refs_0_, s32[1]{0:T(128)} %bitcast.refs_2_.refs_1_, f32[8,256]{1,0:T(8,128)S(1)} %get-tuple-element.40.refs_4_.refs_2_, f32[16,256]{1,0:T(8,128)S(1)} %get-tuple-element.53.refs_3_, ...), custom_call_target="tpu_custom_call" | custom-call | tf_op jit(solution)/shard_map/pallas_call | solution.py:683
  25.2 0.3 collective-permute-start.3
  25.5 1.6 %collective-permute-start.5 = (f32[16,256]{1,0:T(8,128)S(1)}, f32[16,256]{1,0:T(8,128)S(1)}, u32[]{:S(2)}, u32[]{:S(2)}) collective-permute-start(f32[16,256]{1,0:T(8,128)S(1)} %get-tuple-element.53.refs_3_), channel_id=1, source_target_pairs={{0,3},{1,2},{2,1},{3,0},{4,7},{5,6},{6,5},{7,4},{8,11},{9,10},{10,... | collective-permute-start | bytes 49160 | tf_op jit(solution)/shard_map/ppermute | solution.py:730
  27.1 0.1 collective-permute-start.4
  27.2 0.0 collective-permute-done.3.refs_9_
  27.2 1.4 %collective-permute-done.5.refs_11_ = f32[16,256]{1,0:T(8,128)S(1)} collective-permute-done((f32[16,256]{1,0:T(8,128)S(1)}, f32[16,256]{1,0:T(8,128)S(1)}, u32[]{:S(2)}, u32[]{:S(2)}) %collective-permute-start.5) | collective-permute-done | bytes 16416 | tf_op jit(solution)/shard_map/ppermute | solution.py:730
  28.7 0.0 collective-permute-done.4.refs_10_
  28.7 2.2 %all-to-all-done.1 = f32[32,1,128]{2,1,0:T(1,128)S(1)} async-done(((f32[32,1,128]{2,1,0:T(1,128)}), f32[32,1,128]{2,1,0:T(1,128)S(1)}, u32[]{:S(2)}, u32[]{:S(2)}) %all-to-all-start.1) | async-done | bytes 16416 | tf_op jit(solution)/shard_map/all_to_all | solution.py:721
  30.9 1.1 %shard_map.117 = (f32[272,128]{1,0:T(8,128)S(1)}, f32[192,128]{1,0:T(8,128)S(1)}, f32[32,128]{1,0:T(8,128)}) custom-call(s32[1]{0:T(128)S(6)} %copy.15.refs_1_.refs_0_, s32[1]{0:T(128)} %bitcast.refs_2_.refs_1_, f32[272,128]{1,0:T(8,128)S(1)} %get-tuple-element.50.refs_2_, f32[32,128]{1,0:T(8,128)S(1)} %bitcast.15, f32[48,256]{1,0:T(8,128)S(1)} %get-tuple-element.59.refs_4_, ...), custom_call_target="tpu_custom_call" | custom-call | tf_op jit(solution)/shard_map/pallas_call | solution.py:683
  32.1 4.9 %all-to-all-start.2 = ((f32[32,1,128]{2,1,0:T(1,128)}), f32[32,1,128]{2,1,0:T(1,128)S(1)}, u32[]{:S(2)}, u32[]{:S(2)}) async-start(f32[32,1,128]{2,1,0:T(1,128)} %bitcast.17), calls=%async_computation.2 | async-start | bytes 32768 | tf_op jit(solution)/shard_map/all_to_all | solution.py:721
  37.0 0.6 %shard_map.118 = (f32[16,256]{1,0:T(8,128)S(1)}, bf16[4,144,512]{2,1,0:T(8,128)(2,1)S(1)}, bf16[4,144,512]{2,1,0:T(8,128)(2,1)S(1)}, f32[192,128]{1,0:T(8,128)S(1)}, f32[512,128]{1,0:T(8,128)S(1)}) custom-call(s32[1]{0:T(128)S(6)} %copy.15.refs_1_.refs_0_, s32[1]{0:T(128)} %bitcast.refs_2_.refs_1_, f32[272,128]{1,0:T(8,128)S(1)} %get-tuple-element.62.refs_2_, ...), custom_call_target="tpu_custom_call" | custom-call | tf_op jit(solution)/shard_map/pallas_call | solution.py:683
  37.6 0.8 %shard_map.119 = (f32[16,256]{1,0:T(8,128)S(1)}, f32[48,256]{1,0:T(8,128)S(1)}) custom-call(s32[1]{0:T(128)S(6)} %copy.15.refs_1_.refs_0_, s32[1]{0:T(128)} %bitcast.refs_2_.refs_1_, f32[8,256]{1,0:T(8,128)S(1)} %get-tuple-element.40.refs_4_.refs_2_, f32[16,256]{1,0:T(8,128)S(1)} %get-tuple-element.65.refs_3_, ...), custom_call_target="tpu_custom_call" | custom-call | tf_op jit(solution)/shard_map/pallas_call | solution.py:683
  38.4 0.3 collective-permute-start.6
  38.7 1.6 %collective-permute-start.8 = (f32[16,256]{1,0:T(8,128)S(1)}, f32[16,256]{1,0:T(8,128)S(1)}, u32[]{:S(2)}, u32[]{:S(2)}) collective-permute-start(f32[16,256]{1,0:T(8,128)S(1)} %get-tuple-element.65.refs_3_), channel_id=1, source_target_pairs={{0,3},{1,2},{2,1},{3,0},{4,7},{5,6},{6,5},{7,4},{8,11},{9,10},{10,... | collective-permute-start | bytes 49160 | tf_op jit(solution)/shard_map/ppermute | solution.py:730
  40.3 0.1 collective-permute-start.7
  40.4 0.0 collective-permute-done.6.refs_9_
  40.5 1.4 %collective-permute-done.8.refs_11_ = f32[16,256]{1,0:T(8,128)S(1)} collective-permute-done((f32[16,256]{1,0:T(8,128)S(1)}, f32[16,256]{1,0:T(8,128)S(1)}, u32[]{:S(2)}, u32[]{:S(2)}) %collective-permute-start.8) | collective-permute-done | bytes 16416 | tf_op jit(solution)/shard_map/ppermute | solution.py:730
  41.9 0.0 collective-permute-done.7.refs_10_
  41.9 2.2 %all-to-all-done.2 = f32[32,1,128]{2,1,0:T(1,128)S(1)} async-done(((f32[32,1,128]{2,1,0:T(1,128)}), f32[32,1,128]{2,1,0:T(1,128)S(1)}, u32[]{:S(2)}, u32[]{:S(2)}) %all-to-all-start.2) | async-done | bytes 16416 | tf_op jit(solution)/shard_map/all_to_all | solution.py:721
  44.1 1.4 %shard_map.120 = (f32[3,4096]{1,0:T(4,128)}, f32[3,4096]{1,0:T(4,128)}, f32[9,4096]{1,0:T(8,128)}, f32[9,4096]{1,0:T(8,128)}) custom-call(s32[1]{0:T(128)S(6)} %copy.15.refs_1_.refs_0_, s32[1]{0:T(128)} %bitcast.refs_2_.refs_1_, f32[272,128]{1,0:T(8,128)S(1)} %get-tuple-element.62.refs_2_, f32[32,128]{1,0:T(8,128)S(1)} %bitcast.13, ...), custom_call_target="tpu_custom_call" | custom-call | tf_op jit(solution)/shard_map/pallas_call | solution.py:683
Async XLA Ops:
  3.0 14.4 %all-to-all-start = ((f32[32,1,128]{2,1,0:T(1,128)}), f32[32,1,128]{2,1,0:T(1,128)S(1)}, u32[]{:S(2)}, u32[]{:S(2)}) async-start(f32[32,1,128]{2,1,0:T(1,128)} %bitcast.18), calls=%async_computation | async-start | bytes 32768 | tf_op jit(solution)/shard_map/all_to_all | solution.py:721
  11.8 2.0 %collective-permute-start = (f32[16,256]{1,0:T(8,128)S(1)}, f32[16,256]{1,0:T(8,128)S(1)}, u32[]{:S(2)}, u32[]{:S(2)}) collective-permute-start(f32[16,256]{1,0:T(8,128)S(1)} %get-tuple-element.49), channel_id=1, source_target_pairs={{0,1},{1,0},{2,3},{3,2},{4,5},{5,4},{6,7},{7,6},{8,9},{9,8},{10,11... | collective-permute-start | bytes 49160 | tf_op jit(solution)/shard_map/ppermute | solution.py:744
  12.1 3.2 %collective-permute-start.2 = (f32[16,256]{1,0:T(8,128)S(1)}, f32[16,256]{1,0:T(8,128)S(1)}, u32[]{:S(2)}, u32[]{:S(2)}) collective-permute-start(f32[16,256]{1,0:T(8,128)S(1)} %get-tuple-element.42.refs_3_), channel_id=1, source_target_pairs={{0,3},{1,2},{2,1},{3,0},{4,7},{5,6},{6,5},{7,4},{8,11},{9,10},{10,... | collective-permute-start | bytes 49160 | tf_op jit(solution)/shard_map/ppermute | solution.py:730
  13.7 1.5 %collective-permute-start.1 = (f32[16,256]{1,0:T(8,128)S(1)}, f32[16,256]{1,0:T(8,128)S(1)}, u32[]{:S(2)}, u32[]{:S(2)}) collective-permute-start(f32[16,256]{1,0:T(8,128)S(1)} %get-tuple-element.42.refs_3_), channel_id=1, source_target_pairs={{3,4},{7,8},{11,12},{15,16},{19,20},{23,24},{27,28},{2,5},{6,9},{1... | collective-permute-start | bytes 49160 | tf_op jit(solution)/shard_map/ppermute | solution.py:729
  18.9 12.0 %all-to-all-start.1 = ((f32[32,1,128]{2,1,0:T(1,128)}), f32[32,1,128]{2,1,0:T(1,128)S(1)}, u32[]{:S(2)}, u32[]{:S(2)}) async-start(f32[32,1,128]{2,1,0:T(1,128)} %bitcast.16), calls=%async_computation.1 | async-start | bytes 32768 | tf_op jit(solution)/shard_map/all_to_all | solution.py:721
  25.2 2.0 %collective-permute-start.3 = (f32[16,256]{1,0:T(8,128)S(1)}, f32[16,256]{1,0:T(8,128)S(1)}, u32[]{:S(2)}, u32[]{:S(2)}) collective-permute-start(f32[16,256]{1,0:T(8,128)S(1)} %get-tuple-element.60), channel_id=1, source_target_pairs={{0,1},{1,0},{2,3},{3,2},{4,5},{5,4},{6,7},{7,6},{8,9},{9,8},{10,11... | collective-permute-start | bytes 49160 | tf_op jit(solution)/shard_map/ppermute | solution.py:744
  25.5 3.2 %collective-permute-start.5 = (f32[16,256]{1,0:T(8,128)S(1)}, f32[16,256]{1,0:T(8,128)S(1)}, u32[]{:S(2)}, u32[]{:S(2)}) collective-permute-start(f32[16,256]{1,0:T(8,128)S(1)} %get-tuple-element.53.refs_3_), channel_id=1, source_target_pairs={{0,3},{1,2},{2,1},{3,0},{4,7},{5,6},{6,5},{7,4},{8,11},{9,10},{10,... | collective-permute-start | bytes 49160 | tf_op jit(solution)/shard_map/ppermute | solution.py:730
  27.1 1.5 %collective-permute-start.4 = (f32[16,256]{1,0:T(8,128)S(1)}, f32[16,256]{1,0:T(8,128)S(1)}, u32[]{:S(2)}, u32[]{:S(2)}) collective-permute-start(f32[16,256]{1,0:T(8,128)S(1)} %get-tuple-element.53.refs_3_), channel_id=1, source_target_pairs={{3,4},{7,8},{11,12},{15,16},{19,20},{23,24},{27,28},{2,5},{6,9},{1... | collective-permute-start | bytes 49160 | tf_op jit(solution)/shard_map/ppermute | solution.py:729
  32.1 12.0 %all-to-all-start.2 = ((f32[32,1,128]{2,1,0:T(1,128)}), f32[32,1,128]{2,1,0:T(1,128)S(1)}, u32[]{:S(2)}, u32[]{:S(2)}) async-start(f32[32,1,128]{2,1,0:T(1,128)} %bitcast.17), calls=%async_computation.2 | async-start | bytes 32768 | tf_op jit(solution)/shard_map/all_to_all | solution.py:721
  38.4 2.0 %collective-permute-start.6 = (f32[16,256]{1,0:T(8,128)S(1)}, f32[16,256]{1,0:T(8,128)S(1)}, u32[]{:S(2)}, u32[]{:S(2)}) collective-permute-start(f32[16,256]{1,0:T(8,128)S(1)} %get-tuple-element.71), channel_id=1, source_target_pairs={{0,1},{1,0},{2,3},{3,2},{4,5},{5,4},{6,7},{7,6},{8,9},{9,8},{10,11... | collective-permute-start | bytes 49160 | tf_op jit(solution)/shard_map/ppermute | solution.py:744
  38.7 3.2 %collective-permute-start.8 = (f32[16,256]{1,0:T(8,128)S(1)}, f32[16,256]{1,0:T(8,128)S(1)}, u32[]{:S(2)}, u32[]{:S(2)}) collective-permute-start(f32[16,256]{1,0:T(8,128)S(1)} %get-tuple-element.65.refs_3_), channel_id=1, source_target_pairs={{0,3},{1,2},{2,1},{3,0},{4,7},{5,6},{6,5},{7,4},{8,11},{9,10},{10,... | collective-permute-start | bytes 49160 | tf_op jit(solution)/shard_map/ppermute | solution.py:730
  40.3 1.5 %collective-permute-start.7 = (f32[16,256]{1,0:T(8,128)S(1)}, f32[16,256]{1,0:T(8,128)S(1)}, u32[]{:S(2)}, u32[]{:S(2)}) collective-permute-start(f32[16,256]{1,0:T(8,128)S(1)} %get-tuple-element.65.refs_3_), channel_id=1, source_target_pairs={{3,4},{7,8},{11,12},{15,16},{19,20},{23,24},{27,28},{2,5},{6,9},{1... | collective-permute-start | bytes 49160 | tf_op jit(solution)/shard_map/ppermute | solution.py:729

commit v5 on v4

--- a/solution.py
+++ b/solution.py
@@ -425,6 +425,12 @@
         ref[pl.ds(rows * number, rows), :] = state[number]
 
 
+def rows_of(begin, count, s, rows):
+    if count == 1:
+        return pl.ds(rows * begin + s, 1)
+    return pl.ds(rows * begin + s, count, stride=rows)
+
+
 def block_row(blocks, bins, width):
     lane = iota((1, width), 1)
     meta = jnp.zeros((1, width), F32)
@@ -434,17 +440,35 @@
 
 
 def first_kernel(
-    bins, device_total, blocks, live, device, x_ref, v_ref, f_ref, c_ref, m_ref, vol_ref,
-    state_ref, motion_ref, speeds, meta, outbox, sem,
+    bins, device_total, live, device, blocks_in, x_in, v_in, f_in, c_in, m_in, vol_in,
+    state_ref, motion_ref, speeds, meta, outbox, sem, blocks, x_ref, v_ref, f_ref, c_ref, m_ref,
+    vol_ref, arrivals,
 ):
     rows = state_ref.shape[0] // ROWS
     quarters = rows // bins
+    half = rows * LANES
+    copies = []
+    moves = (
+        (v_in.at[:, pl.ds(0, half)], v_ref),
+        (m_in.at[pl.ds(0, half)], m_ref),
+        (blocks_in, blocks),
+        (x_in.at[:, pl.ds(0, half)], x_ref),
+        (f_in.at[:, pl.ds(0, half)], f_ref),
+        (c_in.at[:, pl.ds(0, half)], c_ref),
+        (vol_in.at[pl.ds(0, half)], vol_ref),
+    )
+    for number, (source, target) in enumerate(moves):
+        copies.append(pltpu.make_async_copy(source, target, arrivals.at[number]))
+        copies[number].start()
+    copies[0].wait()
+    copies[1].wait()
 
     def relay(ref, count, kept, begin):
-        for number in range(count):
-            for s in range(rows):
-                target = rows * (begin + number) + s
-                kept[pl.ds(target, 1), :] = ref[pl.ds(number, 1), pl.ds(LANES * s, LANES)]
+        for s in range(rows):
+            for start in range(0, count, 8):
+                size = min(8, count - start)
+                source = ref[pl.ds(start, size), pl.ds(LANES * s, LANES)]
+                kept[rows_of(begin + start, size, s, rows), :] = source
 
     def relay_flat(ref, number):
         for b in range(bins):
@@ -454,13 +478,23 @@
                 piece = ref[pl.ds(LANES * s, LANES)].reshape(1, LANES)
                 state_ref[pl.ds(rows * number + s, 1), :] = piece * alive
 
-    relay(v_ref, 3, motion_ref, 0)
-    relay_flat(m_ref, MASS)
-    motion = [motion_ref[pl.ds(rows * number, rows), :] for number in range(3)]
-    send_speed(motion, state_ref[pl.ds(rows * MASS, rows), :], speeds, outbox, sem)
+    fastest = jnp.zeros((1, LANES), F32)
+    for b in range(bins):
+        for s in range(quarters * b, quarters * (b + 1)):
+            part = v_ref[:, pl.ds(LANES * s, LANES)]
+            speed = jnp.sum(part * part, axis=0, keepdims=True)
+            mass = m_ref[pl.ds(LANES * s, LANES)].reshape(1, LANES)
+            counted = (mass > 0.0) & (b < live[0])
+            fastest = jnp.maximum(fastest, jnp.where(counted, speed, 0.0))
+    outbox[...] = jnp.broadcast_to(jnp.max(fastest, axis=1, keepdims=True), outbox.shape)
+    pltpu.make_async_copy(outbox, speeds, sem).start()
 
     @pl.when(live[0] >= 0)
     def _():
+        for copy in copies[2:]:
+            copy.wait()
+        relay(v_ref, 3, motion_ref, 0)
+        relay_flat(m_ref, MASS)
         relay(x_ref, 3, state_ref, POS)
         relay(f_ref, 9, state_ref, DEF)
         relay(c_ref, 9, motion_ref, 3)
@@ -594,7 +628,8 @@
 
 def last_kernel(
     bins, device_total, live, device, old_ref, speeds, own, geometry, highs, lows, along,
-    near, outer, inner, sides_ref, d_out, v_out, f_out, c_out, shuffle,
+    near, outer, inner, sides_ref, d_out, v_out, f_out, c_out, shuffle, d_rows,
+    v_rows, f_rows, c_rows,
 ):
     rows = old_ref.shape[0] // ROWS
     quarters = rows // bins
@@ -604,17 +639,20 @@
 
     def finish(state, velocity, affine):
         results = (
-            (d_out, state[TRAV : TRAV + 3]),
-            (v_out, velocity),
-            (f_out, state[DEF : DEF + 9]),
-            (c_out, affine),
+            (d_out, state[TRAV : TRAV + 3], d_rows),
+            (v_out, velocity, v_rows),
+            (f_out, state[DEF : DEF + 9], f_rows),
+            (c_out, affine, c_rows),
         )
-        for ref, values in results:
+        for ref, values, finished in results:
             count = len(values)
             for number in range(count):
-                value = jnp.where(alive, values[number], 0.0)
-                for s in range(rows):
-                    ref[pl.ds(number, 1), pl.ds(LANES * s, LANES)] = value[s : s + 1, :]
+                finished[pl.ds(rows * number, rows), :] = jnp.where(alive, values[number], 0.0)
+            for s in range(rows):
+                for start in range(0, count, 8):
+                    size = min(8, count - start)
+                    value = finished[rows_of(start, size, s, rows), :]
+                    ref[pl.ds(start, size), pl.ds(LANES * s, LANES)] = value
             total = ref.shape[1]
             ref[:, pl.ds(half, total - half)] = jnp.zeros((count, total - half), F32)
 
@@ -654,7 +692,6 @@
     anywhere = pl.BlockSpec(memory_space=pl.ANY)
     shuffle = pltpu.VMEM((4 * 8 * rows, LANES), F32)
     sending = [pltpu.VMEM((device_total, LANES), F32), pltpu.SemaphoreType.DMA]
-    bin_block = bin_block if INTERPRET else pltpu.with_memory_space_constraint(bin_block, pltpu.HBM)
     me = lax.axis_index("space").astype(jnp.int32).reshape(1)
 
     def stay(array, space=pltpu.VMEM):
@@ -665,20 +702,12 @@
             count = len(scalars)
             body(bins, device_total, *refs[: count - 1], refs[count - 1][0], *refs[count:])
 
-        extra = {}
         out_specs = tuple(anywhere if output == speeds_shape else vmem for output in outputs)
         if in_specs is None:
             in_specs = [vmem] * len(arguments)
             arguments = [stay(argument) for argument in arguments]
         else:
             arguments = [stay(argument, pltpu.HBM) for argument in arguments]
-            out_specs = tuple(
-                anywhere
-                if output == speeds_shape
-                else pl.BlockSpec(output[0], lambda i, rank=len(output[0]): (0,) * rank)
-                for output in outputs
-            )
-            extra = {"grid": (1,)}
         make = jax.ShapeDtypeStruct if final or INTERPRET else pltpu.VMEM
         return pl.pallas_call(
             kernel,
@@ -691,13 +720,8 @@
             scratch_shapes=scratch,
             interpret=INTERPRET,
             compiler_params=pltpu.CompilerParams(vmem_limit_bytes=GRANT),
-            **extra,
         )(*scalars, *arguments)
 
-    def first_half(count):
-        return pl.BlockSpec((count, half), lambda i: (0, 0))
-
-    flat_half = pl.BlockSpec((half,), lambda i: (0,))
     length = device_total
     swap_pairs = [(i, i ^ 1) for i in range(length)]
     inner_pairs = [(i, i ^ 3) for i in range(length)]
@@ -706,13 +730,17 @@
     outer_pairs = outer_pairs + [(0, 1), (length - 2, length - 1)]
     outer_pairs = outer_pairs + [(j, i) for i, j in outer_pairs]
 
+    slot_rows = [pltpu.VMEM((count, half), F32) for count in (3, 3, 9, 9)]
     *results, meta = call(
         first_kernel,
-        (bin_block, live_count, me),
-        (positions, velocity, deformation, affine, particle_mass, volume),
-        held + [meta_shape],
-        sending,
-        [first_half(3), first_half(3), first_half(9), first_half(9), flat_half, flat_half],
+        (live_count, me),
+        (bin_block, positions, velocity, deformation, affine, particle_mass, volume),
+        [*held, meta_shape],
+        sending
+        + [pltpu.SMEM((slot_total,), jnp.int32)]
+        + slot_rows
+        + [pltpu.VMEM((half,), F32), pltpu.VMEM((half,), F32), pltpu.SemaphoreType.DMA((7,))],
+        [anywhere] * 7,
     )
     sides = ()
     for step in range(STEPS):
@@ -760,7 +788,7 @@
         (live_count, me),
         arguments,
         [((count, total), F32) for count in (3, 3, 9, 9)],
-        [shuffle],
+        [shuffle] + [pltpu.VMEM((count * rows, LANES), F32) for count in (3, 3, 9, 9)],
         final=True,
     )
 

time: 45.8 us -> 45.6 us (level)
  no operation moved by 1% of the time
where the time goes in v5:
time: 45.6 us; the launch traced here: 45.3 us
  starting transfers between devices  23.3 us (51%)
  waiting for transfers between devices  10.9 us (24%)
  Pallas kernels  9.75 us (21%)
  between operations  1.34 us (3%)
    all_to_all x3, starting transfers between devices, local(): speeds = lax.all_to_all(speeds, 'space', 0, 0, tiled=True)  17.2 us
    pallas_call x10, Pallas kernels, call(): pl.pallas_call(kernel, in_specs=[smem] * len(scalars) + in_specs, out_sha...  9.75 us
    all_to_all x3, waiting for transfers between devices, local(): speeds = lax.all_to_all(speeds, 'space', 0, 0, tiled=True)  6.69 us
    ppermute x3, starting transfers between devices, local(): from_inner = lax.ppermute(far, 'space', inner_pairs)  4.89 us
    ppermute x3, waiting for transfers between devices, local(): from_inner = lax.ppermute(far, 'space', inner_pairs)  4.24 us
  transfers between devices with their start and end apart: 12, of which 6 were waited for; matrix products, arithmetic and copies ran while one was open for 0% of the time, Pallas kernels for 9%

profile of v5, /device:TPU:0, one launch (start us, length us, event | category | flops | bytes accessed | tf_op | source)
XLA Modules:
  0.0 45.3 jit_solution(11470656022520034038)
XLA Ops:
  1.3 1.5 %shard_map.111 = (f32[272,128]{1,0:T(8,128)S(1)}, f32[192,128]{1,0:T(8,128)S(1)}, f32[32,128]{1,0:T(8,128)}, f32[8,256]{1,0:T(8,128)S(1)}) custom-call(s32[1]{0:T(128)S(6)} %copy.15.refs_0_, s32[1]{0:T(128)} %bitcast.refs_1_, s32[8]{0:T(128)} %refs_2_.1, f32[3,4096]{1,0:T(4,128)} %refs_3_.1, f32[3,4096]{1,0:T(4,128)} %refs_4_.1, f32[9,4096]{1,0:T(8,128)} %refs_5_.1, ...), custom_call_target="tpu_custom_call" | custom-call | tf_op jit(solution)/shard_map/pallas_call | solution.py:712
  2.8 7.3 %all-to-all-start = ((f32[32,1,128]{2,1,0:T(1,128)}), f32[32,1,128]{2,1,0:T(1,128)S(1)}, u32[]{:S(2)}, u32[]{:S(2)}) async-start(f32[32,1,128]{2,1,0:T(1,128)} %bitcast.18), calls=%async_computation | async-start | bytes 32768 | tf_op jit(solution)/shard_map/all_to_all | solution.py:749
  10.2 0.6 %shard_map.112 = (f32[16,256]{1,0:T(8,128)S(1)}, bf16[4,144,512]{2,1,0:T(8,128)(2,1)S(1)}, bf16[4,144,512]{2,1,0:T(8,128)(2,1)S(1)}, f32[192,128]{1,0:T(8,128)S(1)}, f32[512,128]{1,0:T(8,128)S(1)}) custom-call(s32[1]{0:T(128)S(6)} %copy.15.refs_0_, s32[1]{0:T(128)} %bitcast.refs_1_, f32[272,128]{1,0:T(8,128)S(1)} %get-tuple-element.38.refs_2_, ...), custom_call_target="tpu_custom_call" | custom-call | tf_op jit(solution)/shard_map/pallas_call | solution.py:712
  10.8 0.8 %shard_map.113 = (f32[16,256]{1,0:T(8,128)S(1)}, f32[48,256]{1,0:T(8,128)S(1)}, f32[24,256]{1,0:T(8,128)S(1)}, bf16[192,256]{1,0:T(8,128)(2,1)S(1)}) custom-call(s32[1]{0:T(128)S(6)} %copy.15.refs_0_, s32[1]{0:T(128)} %bitcast.refs_1_, f32[8,256]{1,0:T(8,128)S(1)} %get-tuple-element.40.refs_4_.refs_2_, f32[16,256]{1,0:T(8,128)S(1)} %get-tuple-element.42.refs_3_, ...), custom_call_target="tpu_custom_call" | custom-call | tf_op jit(solution)/shard_map/pallas_call | solution.py:712
  11.6 0.3 collective-permute-start
  11.9 1.6 %collective-permute-start.2 = (f32[16,256]{1,0:T(8,128)S(1)}, f32[16,256]{1,0:T(8,128)S(1)}, u32[]{:S(2)}, u32[]{:S(2)}) collective-permute-start(f32[16,256]{1,0:T(8,128)S(1)} %get-tuple-element.42.refs_3_), channel_id=1, source_target_pairs={{0,3},{1,2},{2,1},{3,0},{4,7},{5,6},{6,5},{7,4},{8,11},{9,10},{10,... | collective-permute-start | bytes 49160 | tf_op jit(solution)/shard_map/ppermute | solution.py:758
  13.5 0.1 collective-permute-start.1
  13.6 0.0 collective-permute-done.refs_9_
  13.6 1.4 %collective-permute-done.2.refs_11_ = f32[16,256]{1,0:T(8,128)S(1)} collective-permute-done((f32[16,256]{1,0:T(8,128)S(1)}, f32[16,256]{1,0:T(8,128)S(1)}, u32[]{:S(2)}, u32[]{:S(2)}) %collective-permute-start.2) | collective-permute-done | bytes 16416 | tf_op jit(solution)/shard_map/ppermute | solution.py:758
  15.0 0.0 collective-permute-done.1.refs_10_
  15.0 2.2 %all-to-all-done = f32[32,1,128]{2,1,0:T(1,128)S(1)} async-done(((f32[32,1,128]{2,1,0:T(1,128)}), f32[32,1,128]{2,1,0:T(1,128)S(1)}, u32[]{:S(2)}, u32[]{:S(2)}) %all-to-all-start) | async-done | bytes 16416 | tf_op jit(solution)/shard_map/all_to_all | solution.py:749
  17.3 1.4 %shard_map.114 = (f32[272,128]{1,0:T(8,128)S(1)}, f32[192,128]{1,0:T(8,128)S(1)}, f32[32,128]{1,0:T(8,128)}, bf16[2,192,256]{2,1,0:T(8,128)(2,1)S(1)}) custom-call(s32[1]{0:T(128)S(6)} %copy.15.refs_0_, s32[1]{0:T(128)} %bitcast.refs_1_, f32[272,128]{1,0:T(8,128)S(1)} %get-tuple-element.38.refs_2_, f32[32,128]{1,0:T(8,128)S(1)} %bitcast.14, ...), custom_call_target="tpu_custom_call" | custom-call | tf_op jit(solution)/shard_map/pallas_call | solution.py:712
  18.6 4.9 %all-to-all-start.1 = ((f32[32,1,128]{2,1,0:T(1,128)}), f32[32,1,128]{2,1,0:T(1,128)S(1)}, u32[]{:S(2)}, u32[]{:S(2)}) async-start(f32[32,1,128]{2,1,0:T(1,128)} %bitcast.16), calls=%async_computation.1 | async-start | bytes 32768 | tf_op jit(solution)/shard_map/all_to_all | solution.py:749
  23.6 0.6 %shard_map.115 = (f32[16,256]{1,0:T(8,128)S(1)}, bf16[4,144,512]{2,1,0:T(8,128)(2,1)S(1)}, bf16[4,144,512]{2,1,0:T(8,128)(2,1)S(1)}, f32[192,128]{1,0:T(8,128)S(1)}, f32[512,128]{1,0:T(8,128)S(1)}) custom-call(s32[1]{0:T(128)S(6)} %copy.15.refs_0_, s32[1]{0:T(128)} %bitcast.refs_1_, f32[272,128]{1,0:T(8,128)S(1)} %get-tuple-element.50.refs_2_, ...), custom_call_target="tpu_custom_call" | custom-call | tf_op jit(solution)/shard_map/pallas_call | solution.py:712
  24.2 0.8 %shard_map.116 = (f32[16,256]{1,0:T(8,128)S(1)}, f32[48,256]{1,0:T(8,128)S(1)}) custom-call(s32[1]{0:T(128)S(6)} %copy.15.refs_0_, s32[1]{0:T(128)} %bitcast.refs_1_, f32[8,256]{1,0:T(8,128)S(1)} %get-tuple-element.40.refs_4_.refs_2_, f32[16,256]{1,0:T(8,128)S(1)} %get-tuple-element.53.refs_3_, bf16[4,144,512]{2,1,0:T(8,128)(2,1)S(1)} %get-tuple-element.54.refs_4_.refs_6_, ...), custom_call_target="tpu_custom_call" | custom-call | tf_op jit(solution)/shard_map/pallas_call | solution.py:712
  25.0 0.3 collective-permute-start.3
  25.3 1.6 %collective-permute-start.5 = (f32[16,256]{1,0:T(8,128)S(1)}, f32[16,256]{1,0:T(8,128)S(1)}, u32[]{:S(2)}, u32[]{:S(2)}) collective-permute-start(f32[16,256]{1,0:T(8,128)S(1)} %get-tuple-element.53.refs_3_), channel_id=1, source_target_pairs={{0,3},{1,2},{2,1},{3,0},{4,7},{5,6},{6,5},{7,4},{8,11},{9,10},{10,... | collective-permute-start | bytes 49160 | tf_op jit(solution)/shard_map/ppermute | solution.py:758
  26.9 0.1 collective-permute-start.4
  27.0 0.0 collective-permute-done.3.refs_9_
  27.0 1.4 %collective-permute-done.5.refs_11_ = f32[16,256]{1,0:T(8,128)S(1)} collective-permute-done((f32[16,256]{1,0:T(8,128)S(1)}, f32[16,256]{1,0:T(8,128)S(1)}, u32[]{:S(2)}, u32[]{:S(2)}) %collective-permute-start.5) | collective-permute-done | bytes 16416 | tf_op jit(solution)/shard_map/ppermute | solution.py:758
  28.5 0.0 collective-permute-done.4.refs_10_
  28.5 2.2 %all-to-all-done.1 = f32[32,1,128]{2,1,0:T(1,128)S(1)} async-done(((f32[32,1,128]{2,1,0:T(1,128)}), f32[32,1,128]{2,1,0:T(1,128)S(1)}, u32[]{:S(2)}, u32[]{:S(2)}) %all-to-all-start.1) | async-done | bytes 16416 | tf_op jit(solution)/shard_map/all_to_all | solution.py:749
  30.7 1.1 %shard_map.117 = (f32[272,128]{1,0:T(8,128)S(1)}, f32[192,128]{1,0:T(8,128)S(1)}, f32[32,128]{1,0:T(8,128)}) custom-call(s32[1]{0:T(128)S(6)} %copy.15.refs_0_, s32[1]{0:T(128)} %bitcast.refs_1_, f32[272,128]{1,0:T(8,128)S(1)} %get-tuple-element.50.refs_2_, f32[32,128]{1,0:T(8,128)S(1)} %bitcast.15, f32[48,256]{1,0:T(8,128)S(1)} %get-tuple-element.59.refs_4_, ...), custom_call_target="tpu_custom_call" | custom-call | tf_op jit(solution)/shard_map/pallas_call | solution.py:712
  31.8 4.9 %all-to-all-start.2 = ((f32[32,1,128]{2,1,0:T(1,128)}), f32[32,1,128]{2,1,0:T(1,128)S(1)}, u32[]{:S(2)}, u32[]{:S(2)}) async-start(f32[32,1,128]{2,1,0:T(1,128)} %bitcast.17), calls=%async_computation.2 | async-start | bytes 32768 | tf_op jit(solution)/shard_map/all_to_all | solution.py:749
  36.8 0.6 %shard_map.118 = (f32[16,256]{1,0:T(8,128)S(1)}, bf16[4,144,512]{2,1,0:T(8,128)(2,1)S(1)}, bf16[4,144,512]{2,1,0:T(8,128)(2,1)S(1)}, f32[192,128]{1,0:T(8,128)S(1)}, f32[512,128]{1,0:T(8,128)S(1)}) custom-call(s32[1]{0:T(128)S(6)} %copy.15.refs_0_, s32[1]{0:T(128)} %bitcast.refs_1_, f32[272,128]{1,0:T(8,128)S(1)} %get-tuple-element.62.refs_2_, ...), custom_call_target="tpu_custom_call" | custom-call | tf_op jit(solution)/shard_map/pallas_call | solution.py:712
  37.4 0.8 %shard_map.119 = (f32[16,256]{1,0:T(8,128)S(1)}, f32[48,256]{1,0:T(8,128)S(1)}) custom-call(s32[1]{0:T(128)S(6)} %copy.15.refs_0_, s32[1]{0:T(128)} %bitcast.refs_1_, f32[8,256]{1,0:T(8,128)S(1)} %get-tuple-element.40.refs_4_.refs_2_, f32[16,256]{1,0:T(8,128)S(1)} %get-tuple-element.65.refs_3_, bf16[4,144,512]{2,1,0:T(8,128)(2,1)S(1)} %get-tuple-element.66.refs_4_.refs_6_, ...), custom_call_target="tpu_custom_call" | custom-call | tf_op jit(solution)/shard_map/pallas_call | solution.py:712
  38.2 0.3 collective-permute-start.6
  38.5 1.6 %collective-permute-start.8 = (f32[16,256]{1,0:T(8,128)S(1)}, f32[16,256]{1,0:T(8,128)S(1)}, u32[]{:S(2)}, u32[]{:S(2)}) collective-permute-start(f32[16,256]{1,0:T(8,128)S(1)} %get-tuple-element.65.refs_3_), channel_id=1, source_target_pairs={{0,3},{1,2},{2,1},{3,0},{4,7},{5,6},{6,5},{7,4},{8,11},{9,10},{10,... | collective-permute-start | bytes 49160 | tf_op jit(solution)/shard_map/ppermute | solution.py:758
  40.1 0.1 collective-permute-start.7
  40.2 0.0 collective-permute-done.6.refs_9_
  40.2 1.4 %collective-permute-done.8.refs_11_ = f32[16,256]{1,0:T(8,128)S(1)} collective-permute-done((f32[16,256]{1,0:T(8,128)S(1)}, f32[16,256]{1,0:T(8,128)S(1)}, u32[]{:S(2)}, u32[]{:S(2)}) %collective-permute-start.8) | collective-permute-done | bytes 16416 | tf_op jit(solution)/shard_map/ppermute | solution.py:758
  41.7 0.0 collective-permute-done.7.refs_10_
  41.7 2.2 %all-to-all-done.2 = f32[32,1,128]{2,1,0:T(1,128)S(1)} async-done(((f32[32,1,128]{2,1,0:T(1,128)}), f32[32,1,128]{2,1,0:T(1,128)S(1)}, u32[]{:S(2)}, u32[]{:S(2)}) %all-to-all-start.2) | async-done | bytes 16416 | tf_op jit(solution)/shard_map/all_to_all | solution.py:749
  43.9 1.4 %shard_map.120 = (f32[3,4096]{1,0:T(4,128)}, f32[3,4096]{1,0:T(4,128)}, f32[9,4096]{1,0:T(8,128)}, f32[9,4096]{1,0:T(8,128)}) custom-call(s32[1]{0:T(128)S(6)} %copy.15.refs_0_, s32[1]{0:T(128)} %bitcast.refs_1_, f32[272,128]{1,0:T(8,128)S(1)} %get-tuple-element.62.refs_2_, f32[32,128]{1,0:T(8,128)S(1)} %bitcast.13, ...), custom_call_target="tpu_custom_call" | custom-call | tf_op jit(solution)/shard_map/pallas_call | solution.py:712
Async XLA Ops:
  2.8 14.4 %all-to-all-start = ((f32[32,1,128]{2,1,0:T(1,128)}), f32[32,1,128]{2,1,0:T(1,128)S(1)}, u32[]{:S(2)}, u32[]{:S(2)}) async-start(f32[32,1,128]{2,1,0:T(1,128)} %bitcast.18), calls=%async_computation | async-start | bytes 32768 | tf_op jit(solution)/shard_map/all_to_all | solution.py:749
  11.6 2.0 %collective-permute-start = (f32[16,256]{1,0:T(8,128)S(1)}, f32[16,256]{1,0:T(8,128)S(1)}, u32[]{:S(2)}, u32[]{:S(2)}) collective-permute-start(f32[16,256]{1,0:T(8,128)S(1)} %get-tuple-element.49), channel_id=1, source_target_pairs={{0,1},{1,0},{2,3},{3,2},{4,5},{5,4},{6,7},{7,6},{8,9},{9,8},{10,11... | collective-permute-start | bytes 49160 | tf_op jit(solution)/shard_map/ppermute | solution.py:772
  11.9 3.2 %collective-permute-start.2 = (f32[16,256]{1,0:T(8,128)S(1)}, f32[16,256]{1,0:T(8,128)S(1)}, u32[]{:S(2)}, u32[]{:S(2)}) collective-permute-start(f32[16,256]{1,0:T(8,128)S(1)} %get-tuple-element.42.refs_3_), channel_id=1, source_target_pairs={{0,3},{1,2},{2,1},{3,0},{4,7},{5,6},{6,5},{7,4},{8,11},{9,10},{10,... | collective-permute-start | bytes 49160 | tf_op jit(solution)/shard_map/ppermute | solution.py:758
  13.5 1.5 %collective-permute-start.1 = (f32[16,256]{1,0:T(8,128)S(1)}, f32[16,256]{1,0:T(8,128)S(1)}, u32[]{:S(2)}, u32[]{:S(2)}) collective-permute-start(f32[16,256]{1,0:T(8,128)S(1)} %get-tuple-element.42.refs_3_), channel_id=1, source_target_pairs={{3,4},{7,8},{11,12},{15,16},{19,20},{23,24},{27,28},{2,5},{6,9},{1... | collective-permute-start | bytes 49160 | tf_op jit(solution)/shard_map/ppermute | solution.py:757
  18.6 12.0 %all-to-all-start.1 = ((f32[32,1,128]{2,1,0:T(1,128)}), f32[32,1,128]{2,1,0:T(1,128)S(1)}, u32[]{:S(2)}, u32[]{:S(2)}) async-start(f32[32,1,128]{2,1,0:T(1,128)} %bitcast.16), calls=%async_computation.1 | async-start | bytes 32768 | tf_op jit(solution)/shard_map/all_to_all | solution.py:749
  25.0 2.0 %collective-permute-start.3 = (f32[16,256]{1,0:T(8,128)S(1)}, f32[16,256]{1,0:T(8,128)S(1)}, u32[]{:S(2)}, u32[]{:S(2)}) collective-permute-start(f32[16,256]{1,0:T(8,128)S(1)} %get-tuple-element.60), channel_id=1, source_target_pairs={{0,1},{1,0},{2,3},{3,2},{4,5},{5,4},{6,7},{7,6},{8,9},{9,8},{10,11... | collective-permute-start | bytes 49160 | tf_op jit(solution)/shard_map/ppermute | solution.py:772
  25.3 3.2 %collective-permute-start.5 = (f32[16,256]{1,0:T(8,128)S(1)}, f32[16,256]{1,0:T(8,128)S(1)}, u32[]{:S(2)}, u32[]{:S(2)}) collective-permute-start(f32[16,256]{1,0:T(8,128)S(1)} %get-tuple-element.53.refs_3_), channel_id=1, source_target_pairs={{0,3},{1,2},{2,1},{3,0},{4,7},{5,6},{6,5},{7,4},{8,11},{9,10},{10,... | collective-permute-start | bytes 49160 | tf_op jit(solution)/shard_map/ppermute | solution.py:758
  26.9 1.5 %collective-permute-start.4 = (f32[16,256]{1,0:T(8,128)S(1)}, f32[16,256]{1,0:T(8,128)S(1)}, u32[]{:S(2)}, u32[]{:S(2)}) collective-permute-start(f32[16,256]{1,0:T(8,128)S(1)} %get-tuple-element.53.refs_3_), channel_id=1, source_target_pairs={{3,4},{7,8},{11,12},{15,16},{19,20},{23,24},{27,28},{2,5},{6,9},{1... | collective-permute-start | bytes 49160 | tf_op jit(solution)/shard_map/ppermute | solution.py:757
  31.8 12.0 %all-to-all-start.2 = ((f32[32,1,128]{2,1,0:T(1,128)}), f32[32,1,128]{2,1,0:T(1,128)S(1)}, u32[]{:S(2)}, u32[]{:S(2)}) async-start(f32[32,1,128]{2,1,0:T(1,128)} %bitcast.17), calls=%async_computation.2 | async-start | bytes 32768 | tf_op jit(solution)/shard_map/all_to_all | solution.py:749
  38.2 2.0 %collective-permute-start.6 = (f32[16,256]{1,0:T(8,128)S(1)}, f32[16,256]{1,0:T(8,128)S(1)}, u32[]{:S(2)}, u32[]{:S(2)}) collective-permute-start(f32[16,256]{1,0:T(8,128)S(1)} %get-tuple-element.71), channel_id=1, source_target_pairs={{0,1},{1,0},{2,3},{3,2},{4,5},{5,4},{6,7},{7,6},{8,9},{9,8},{10,11... | collective-permute-start | bytes 49160 | tf_op jit(solution)/shard_map/ppermute | solution.py:772
  38.5 3.2 %collective-permute-start.8 = (f32[16,256]{1,0:T(8,128)S(1)}, f32[16,256]{1,0:T(8,128)S(1)}, u32[]{:S(2)}, u32[]{:S(2)}) collective-permute-start(f32[16,256]{1,0:T(8,128)S(1)} %get-tuple-element.65.refs_3_), channel_id=1, source_target_pairs={{0,3},{1,2},{2,1},{3,0},{4,7},{5,6},{6,5},{7,4},{8,11},{9,10},{10,... | collective-permute-start | bytes 49160 | tf_op jit(solution)/shard_map/ppermute | solution.py:758
  40.1 1.5 %collective-permute-start.7 = (f32[16,256]{1,0:T(8,128)S(1)}, f32[16,256]{1,0:T(8,128)S(1)}, u32[]{:S(2)}, u32[]{:S(2)}) collective-permute-start(f32[16,256]{1,0:T(8,128)S(1)} %get-tuple-element.65.refs_3_), channel_id=1, source_target_pairs={{3,4},{7,8},{11,12},{15,16},{19,20},{23,24},{27,28},{2,5},{6,9},{1... | collective-permute-start | bytes 49160 | tf_op jit(solution)/shard_map/ppermute | solution.py:757

commit v6 on v5

--- a/solution.py
+++ b/solution.py
@@ -579,18 +579,32 @@
 
 
 def second_kernel(
-    bins, device_total, live, device, old_ref, speeds, own, geometry, highs, lows, along,
-    near, outer, inner, state_ref, motion_ref, new_speeds, sides_ref, shuffle, outbox, sem,
-):
+    bins, device_total, live, device, meta, old_ref, speeds, own, geometry, highs, lows, along,
+    near, outer, inner, state_ref, new_speeds, far, new_highs, new_lows, new_along, channels,
+    sides_ref, across, outbox, sem,
+):
+    rows = state_ref.shape[0] // ROWS
     around = halos(near, outer, inner, device, device_total)
     key = geometry[0:1, :]
     sides = [placing(block_numbers(block[7:8, :], bins), key, bins) for block in around]
     for side in range(2):
         sides_ref[side] = sides[side]
-    advance(
-        live, bins, device_total, device, old_ref, speeds, own, geometry, highs, lows, along, around,
-        sides, state_ref, motion_ref, new_speeds, shuffle, outbox, sem,
-    )
+
+    def started(velocity):
+        send_speed(velocity, old_ref[pl.ds(rows * MASS, rows), :], new_speeds, outbox, sem)
+
+    def finish(state, velocity, affine):
+        write_state(state_ref, state)
+        to_grid(
+            state, velocity, affine, state_ref, device, bins, meta, far, new_highs, new_lows,
+            new_along, channels, across,
+        )
+
+    to_particles(
+        None, old_ref, device, bins, device_total, geometry, own, sides, speeds, around, highs,
+        lows, along, channels, started, finish,
+    )
+    pltpu.make_async_copy(outbox, new_speeds, sem).wait()
 
 
 def later_kernel(
@@ -742,18 +756,14 @@
         + [pltpu.VMEM((half,), F32), pltpu.VMEM((half,), F32), pltpu.SemaphoreType.DMA((7,))],
         [anywhere] * 7,
     )
-    sides = ()
+    across = pltpu.VMEM((12 * rows, LANES), F32)
+    state, motion, speeds = results
     for step in range(STEPS):
-        state, motion, speeds = results[:3]
-        sides = sides + tuple(results[3:])
         speeds = lax.all_to_all(speeds, "space", 0, 0, tiled=True)
-        far, highs, lows, along, channels = call(
-            scatter_kernel,
-            (live_count, me),
-            (state, motion, meta),
-            grid_held,
-            [pltpu.VMEM((12 * rows, LANES), F32)],
-        )
+        if step != 1:
+            far, highs, lows, along, channels = call(
+                scatter_kernel, (live_count, me), (state, motion, meta), grid_held, [across]
+            )
         from_outer = lax.ppermute(far, "space", outer_pairs)
         from_inner = lax.ppermute(far, "space", inner_pairs)
         arguments = (meta, far, highs, lows, along, channels)
@@ -772,21 +782,24 @@
         from_near = lax.ppermute(near, "space", swap_pairs)
         arguments = (
             state, speeds, own, geometry, highs, lows, along, from_near, from_outer, from_inner,
-            *sides,
         )
-        if step < STEPS - 1:
-            results = call(
-                second_kernel if step == 0 else later_kernel,
+        if step == 0:
+            state, speeds, far, highs, lows, along, channels, sides = call(
+                second_kernel,
                 (live_count, me),
-                arguments,
-                held + ([sides_shape] if step == 0 else []),
-                [shuffle] + sending,
+                (meta, *arguments),
+                [held[0], speeds_shape, *grid_held, sides_shape],
+                [across] + sending,
+            )
+        elif step < STEPS - 1:
+            state, motion, speeds = call(
+                later_kernel, (live_count, me), (*arguments, sides), held, [shuffle] + sending
             )
     total = positions.shape[1]
     return call(
         last_kernel,
         (live_count, me),
-        arguments,
+        (*arguments, sides),
         [((count, total), F32) for count in (3, 3, 9, 9)],
         [shuffle] + [pltpu.VMEM((count * rows, LANES), F32) for count in (3, 3, 9, 9)],
         final=True,

time: 45.6 us -> 44.1 us (0.967)
  starting transfers between devices: 23.3 us -> 21.6 us
  waiting for transfers between devices: 10.9 us -> 11.5 us
    all_to_all x3, starting transfers between devices: 17.2 us -> 15.4 us  [local(): speeds = lax.all_to_all(speeds, 'space', 0, 0, tiled=True)]
    ppermute x3, waiting for transfers between devices: 4.24 us -> 3.19 us  [local(): from_inner = lax.ppermute(far, 'space', inner_pairs)]
    all_to_all x3, waiting for transfers between devices: 6.69 us -> 7.62 us  [local(): speeds = lax.all_to_all(speeds, 'space', 0, 0, tiled=True)]
    ppermute x3, waiting for transfers between devices: 0.01 us -> 0.71 us  [local(): from_near = lax.ppermute(near, 'space', swap_pairs)]
    pallas_call x10 -> x9, Pallas kernels: 9.75 us -> 9.41 us  [call(): pl.pallas_call(kernel, in_specs=[smem] * len(scalars) + in_specs, out_sha...]
  transfers between devices with their start and end apart: 12 -> 12, of which waited for: 6 -> 7; matrix products, arithmetic and copies ran while one was open for 0% -> 0% of each run, Pallas kernels for 9% -> 8%
where the time goes in v6:
time: 44.1 us; the launch traced here: 43.9 us
  starting transfers between devices  21.6 us (49%)
  waiting for transfers between devices  11.5 us (26%)
  Pallas kernels  9.41 us (21%)
  between operations  1.34 us (3%)
    all_to_all x3, starting transfers between devices, local(): speeds = lax.all_to_all(speeds, 'space', 0, 0, tiled=True)  15.4 us
    pallas_call x9, Pallas kernels, call(): pl.pallas_call(kernel, in_specs=[smem] * len(scalars) + in_specs, out_sha...  9.41 us
    all_to_all x3, waiting for transfers between devices, local(): speeds = lax.all_to_all(speeds, 'space', 0, 0, tiled=True)  7.62 us
    ppermute x3, starting transfers between devices, local(): from_inner = lax.ppermute(far, 'space', inner_pairs)  4.81 us
    ppermute x3, waiting for transfers between devices, local(): from_inner = lax.ppermute(far, 'space', inner_pairs)  3.19 us
  transfers between devices with their start and end apart: 12, of which 7 were waited for; matrix products, arithmetic and copies ran while one was open for 0% of the time, Pallas kernels for 8%

profile of v6, /device:TPU:0, one launch (start us, length us, event | category | flops | bytes accessed | tf_op | source)
XLA Modules:
  0.0 43.9 jit_solution(11976748065826682416)
XLA Ops:
  1.3 1.5 %shard_map.111 = (f32[272,128]{1,0:T(8,128)S(1)}, f32[192,128]{1,0:T(8,128)S(1)}, f32[32,128]{1,0:T(8,128)}, f32[8,256]{1,0:T(8,128)S(1)}) custom-call(s32[1]{0:T(128)S(6)} %copy.15.refs_0_, s32[1]{0:T(128)} %bitcast.refs_1_, s32[8]{0:T(128)} %refs_2_.1, f32[3,4096]{1,0:T(4,128)} %refs_3_.1, f32[3,4096]{1,0:T(4,128)} %refs_4_.1, f32[9,4096]{1,0:T(8,128)} %refs_5_.1, ...), custom_call_target="tpu_custom_call" | custom-call | tf_op jit(solution)/shard_map/pallas_call | solution.py:726
  2.8 7.3 %all-to-all-start = ((f32[32,1,128]{2,1,0:T(1,128)}), f32[32,1,128]{2,1,0:T(1,128)S(1)}, u32[]{:S(2)}, u32[]{:S(2)}) async-start(f32[32,1,128]{2,1,0:T(1,128)} %bitcast.18), calls=%async_computation | async-start | bytes 32768 | tf_op jit(solution)/shard_map/all_to_all | solution.py:762
  10.2 0.6 %shard_map.112 = (f32[16,256]{1,0:T(8,128)S(1)}, bf16[4,144,512]{2,1,0:T(8,128)(2,1)S(1)}, bf16[4,144,512]{2,1,0:T(8,128)(2,1)S(1)}, f32[192,128]{1,0:T(8,128)S(1)}, f32[512,128]{1,0:T(8,128)S(1)}) custom-call(s32[1]{0:T(128)S(6)} %copy.15.refs_0_, s32[1]{0:T(128)} %bitcast.refs_1_, f32[272,128]{1,0:T(8,128)S(1)} %get-tuple-element.38.refs_2_.refs_3_, ...), custom_call_target="tpu_custom_call" | custom-call | tf_op jit(solution)/shard_map/pallas_call | solution.py:726
  10.8 0.8 %shard_map.113 = (f32[16,256]{1,0:T(8,128)S(1)}, f32[48,256]{1,0:T(8,128)S(1)}, f32[24,256]{1,0:T(8,128)S(1)}, bf16[192,256]{1,0:T(8,128)(2,1)S(1)}) custom-call(s32[1]{0:T(128)S(6)} %copy.15.refs_0_, s32[1]{0:T(128)} %bitcast.refs_1_, f32[8,256]{1,0:T(8,128)S(1)} %get-tuple-element.37.refs_4_.refs_2_, f32[16,256]{1,0:T(8,128)S(1)} %get-tuple-element.41.refs_3_, ...), custom_call_target="tpu_custom_call" | custom-call | tf_op jit(solution)/shard_map/pallas_call | solution.py:726
  11.6 0.3 collective-permute-start
  11.9 1.6 %collective-permute-start.2 = (f32[16,256]{1,0:T(8,128)S(1)}, f32[16,256]{1,0:T(8,128)S(1)}, u32[]{:S(2)}, u32[]{:S(2)}) collective-permute-start(f32[16,256]{1,0:T(8,128)S(1)} %get-tuple-element.41.refs_3_), channel_id=1, source_target_pairs={{0,3},{1,2},{2,1},{3,0},{4,7},{5,6},{6,5},{7,4},{8,11},{9,10},{10,... | collective-permute-start | bytes 49160 | tf_op jit(solution)/shard_map/ppermute | solution.py:768
  13.5 0.1 collective-permute-start.1
  13.6 0.0 collective-permute-done.refs_10_
  13.6 1.4 %collective-permute-done.2.refs_12_ = f32[16,256]{1,0:T(8,128)S(1)} collective-permute-done((f32[16,256]{1,0:T(8,128)S(1)}, f32[16,256]{1,0:T(8,128)S(1)}, u32[]{:S(2)}, u32[]{:S(2)}) %collective-permute-start.2) | collective-permute-done | bytes 16416 | tf_op jit(solution)/shard_map/ppermute | solution.py:768
  15.0 0.0 collective-permute-done.1.refs_11_
  15.0 2.2 %all-to-all-done = f32[32,1,128]{2,1,0:T(1,128)S(1)} async-done(((f32[32,1,128]{2,1,0:T(1,128)}), f32[32,1,128]{2,1,0:T(1,128)S(1)}, u32[]{:S(2)}, u32[]{:S(2)}) %all-to-all-start) | async-done | bytes 16416 | tf_op jit(solution)/shard_map/all_to_all | solution.py:762
  17.3 1.7 %shard_map.114 = (f32[272,128]{1,0:T(8,128)S(1)}, f32[32,128]{1,0:T(8,128)}, f32[16,256]{1,0:T(8,128)S(1)}, bf16[4,144,512]{2,1,0:T(8,128)(2,1)S(1)}, bf16[4,144...) custom-call(s32[1]{0:T(128)S(6)} %copy.15.refs_0_, ...), custom_call_target="tpu_custom_call" | custom-call | tf_op jit(solution)/shard_map/pallas_call | solution.py:726
  19.0 4.9 %all-to-all-start.1 = ((f32[32,1,128]{2,1,0:T(1,128)}), f32[32,1,128]{2,1,0:T(1,128)S(1)}, u32[]{:S(2)}, u32[]{:S(2)}) async-start(f32[32,1,128]{2,1,0:T(1,128)} %bitcast.17), calls=%async_computation.1 | async-start | bytes 32768 | tf_op jit(solution)/shard_map/all_to_all | solution.py:762
  23.9 1.6 %collective-permute-start.5 = (f32[16,256]{1,0:T(8,128)S(1)}, f32[16,256]{1,0:T(8,128)S(1)}, u32[]{:S(2)}, u32[]{:S(2)}) collective-permute-start(f32[16,256]{1,0:T(8,128)S(1)} %get-tuple-element.51.refs_3_), channel_id=1, source_target_pairs={{0,3},{1,2},{2,1},{3,0},{4,7},{5,6},{6,5},{7,4},{8,11},{9,10},{10,... | collective-permute-start | bytes 49160 | tf_op jit(solution)/shard_map/ppermute | solution.py:768
  25.5 0.4 collective-permute-start.4
  25.9 0.8 %shard_map.115 = (f32[16,256]{1,0:T(8,128)S(1)}, f32[48,256]{1,0:T(8,128)S(1)}) custom-call(s32[1]{0:T(128)S(6)} %copy.15.refs_0_, s32[1]{0:T(128)} %bitcast.refs_1_, f32[8,256]{1,0:T(8,128)S(1)} %get-tuple-element.37.refs_4_.refs_2_, f32[16,256]{1,0:T(8,128)S(1)} %get-tuple-element.51.refs_3_, bf16[4,144,512]{2,1,0:T(8,128)(2,1)S(1)} %get-tuple-element.52.refs_4_.refs_6_, ...), custom_call_target="tpu_custom_call" | custom-call | tf_op jit(solution)/shard_map/pallas_call | solution.py:726
  26.6 0.1 collective-permute-start.3
  26.8 0.4 collective-permute-done.5.refs_11_
  27.1 0.0 collective-permute-done.4.refs_10_
  27.1 0.7 %collective-permute-done.3.refs_9_ = f32[16,256]{1,0:T(8,128)S(1)} collective-permute-done((f32[16,256]{1,0:T(8,128)S(1)}, f32[16,256]{1,0:T(8,128)S(1)}, u32[]{:S(2)}, u32[]{:S(2)}) %collective-permute-start.3) | collective-permute-done | bytes 16416 | tf_op jit(solution)/shard_map/ppermute | solution.py:782
  27.8 3.2 %all-to-all-done.1 = f32[32,1,128]{2,1,0:T(1,128)S(1)} async-done(((f32[32,1,128]{2,1,0:T(1,128)}), f32[32,1,128]{2,1,0:T(1,128)S(1)}, u32[]{:S(2)}, u32[]{:S(2)}) %all-to-all-start.1) | async-done | bytes 16416 | tf_op jit(solution)/shard_map/all_to_all | solution.py:762
  31.0 1.1 %shard_map.116 = (f32[272,128]{1,0:T(8,128)S(1)}, f32[192,128]{1,0:T(8,128)S(1)}, f32[32,128]{1,0:T(8,128)}) custom-call(s32[1]{0:T(128)S(6)} %copy.15.refs_0_, s32[1]{0:T(128)} %bitcast.refs_1_, f32[272,128]{1,0:T(8,128)S(1)} %get-tuple-element.49.refs_2_, f32[32,128]{1,0:T(8,128)S(1)} %bitcast.15, f32[48,256]{1,0:T(8,128)S(1)} %get-tuple-element.57.refs_4_, ...), custom_call_target="tpu_custom_call" | custom-call | tf_op jit(solution)/shard_map/pallas_call | solution.py:726
  32.2 3.2 %all-to-all-start.2 = ((f32[32,1,128]{2,1,0:T(1,128)}), f32[32,1,128]{2,1,0:T(1,128)S(1)}, u32[]{:S(2)}, u32[]{:S(2)}) async-start(f32[32,1,128]{2,1,0:T(1,128)} %bitcast.16), calls=%async_computation.2 | async-start | bytes 32768 | tf_op jit(solution)/shard_map/all_to_all | solution.py:762
  35.3 0.6 %shard_map.117 = (f32[16,256]{1,0:T(8,128)S(1)}, bf16[4,144,512]{2,1,0:T(8,128)(2,1)S(1)}, bf16[4,144,512]{2,1,0:T(8,128)(2,1)S(1)}, f32[192,128]{1,0:T(8,128)S(1)}, f32[512,128]{1,0:T(8,128)S(1)}) custom-call(s32[1]{0:T(128)S(6)} %copy.15.refs_0_, s32[1]{0:T(128)} %bitcast.refs_1_, f32[272,128]{1,0:T(8,128)S(1)} %get-tuple-element.60.refs_2_, ...), custom_call_target="tpu_custom_call" | custom-call | tf_op jit(solution)/shard_map/pallas_call | solution.py:726
  36.0 0.8 %shard_map.118 = (f32[16,256]{1,0:T(8,128)S(1)}, f32[48,256]{1,0:T(8,128)S(1)}) custom-call(s32[1]{0:T(128)S(6)} %copy.15.refs_0_, s32[1]{0:T(128)} %bitcast.refs_1_, f32[8,256]{1,0:T(8,128)S(1)} %get-tuple-element.37.refs_4_.refs_2_, f32[16,256]{1,0:T(8,128)S(1)} %get-tuple-element.63.refs_3_, bf16[4,144,512]{2,1,0:T(8,128)(2,1)S(1)} %get-tuple-element.64.refs_4_.refs_6_, ...), custom_call_target="tpu_custom_call" | custom-call | tf_op jit(solution)/shard_map/pallas_call | solution.py:726
  36.8 0.3 collective-permute-start.6
  37.0 1.6 %collective-permute-start.8 = (f32[16,256]{1,0:T(8,128)S(1)}, f32[16,256]{1,0:T(8,128)S(1)}, u32[]{:S(2)}, u32[]{:S(2)}) collective-permute-start(f32[16,256]{1,0:T(8,128)S(1)} %get-tuple-element.63.refs_3_), channel_id=1, source_target_pairs={{0,3},{1,2},{2,1},{3,0},{4,7},{5,6},{6,5},{7,4},{8,11},{9,10},{10,... | collective-permute-start | bytes 49160 | tf_op jit(solution)/shard_map/ppermute | solution.py:768
  38.7 0.1 collective-permute-start.7
  38.8 0.0 collective-permute-done.6.refs_9_
  38.8 1.4 %collective-permute-done.8.refs_11_ = f32[16,256]{1,0:T(8,128)S(1)} collective-permute-done((f32[16,256]{1,0:T(8,128)S(1)}, f32[16,256]{1,0:T(8,128)S(1)}, u32[]{:S(2)}, u32[]{:S(2)}) %collective-permute-start.8) | collective-permute-done | bytes 16416 | tf_op jit(solution)/shard_map/ppermute | solution.py:768
  40.2 0.0 collective-permute-done.7.refs_10_
  40.2 2.2 %all-to-all-done.2 = f32[32,1,128]{2,1,0:T(1,128)S(1)} async-done(((f32[32,1,128]{2,1,0:T(1,128)}), f32[32,1,128]{2,1,0:T(1,128)S(1)}, u32[]{:S(2)}, u32[]{:S(2)}) %all-to-all-start.2) | async-done | bytes 16416 | tf_op jit(solution)/shard_map/all_to_all | solution.py:762
  42.4 1.4 %shard_map.119 = (f32[3,4096]{1,0:T(4,128)}, f32[3,4096]{1,0:T(4,128)}, f32[9,4096]{1,0:T(8,128)}, f32[9,4096]{1,0:T(8,128)}) custom-call(s32[1]{0:T(128)S(6)} %copy.15.refs_0_, s32[1]{0:T(128)} %bitcast.refs_1_, f32[272,128]{1,0:T(8,128)S(1)} %get-tuple-element.60.refs_2_, f32[32,128]{1,0:T(8,128)S(1)} %bitcast.13, ...), custom_call_target="tpu_custom_call" | custom-call | tf_op jit(solution)/shard_map/pallas_call | solution.py:726
Async XLA Ops:
  2.8 14.4 %all-to-all-start = ((f32[32,1,128]{2,1,0:T(1,128)}), f32[32,1,128]{2,1,0:T(1,128)S(1)}, u32[]{:S(2)}, u32[]{:S(2)}) async-start(f32[32,1,128]{2,1,0:T(1,128)} %bitcast.18), calls=%async_computation | async-start | bytes 32768 | tf_op jit(solution)/shard_map/all_to_all | solution.py:762
  11.6 2.0 %collective-permute-start = (f32[16,256]{1,0:T(8,128)S(1)}, f32[16,256]{1,0:T(8,128)S(1)}, u32[]{:S(2)}, u32[]{:S(2)}) collective-permute-start(f32[16,256]{1,0:T(8,128)S(1)} %get-tuple-element.48), channel_id=1, source_target_pairs={{0,1},{1,0},{2,3},{3,2},{4,5},{5,4},{6,7},{7,6},{8,9},{9,8},{10,11... | collective-permute-start | bytes 49160 | tf_op jit(solution)/shard_map/ppermute | solution.py:782
  11.9 3.2 %collective-permute-start.2 = (f32[16,256]{1,0:T(8,128)S(1)}, f32[16,256]{1,0:T(8,128)S(1)}, u32[]{:S(2)}, u32[]{:S(2)}) collective-permute-start(f32[16,256]{1,0:T(8,128)S(1)} %get-tuple-element.41.refs_3_), channel_id=1, source_target_pairs={{0,3},{1,2},{2,1},{3,0},{4,7},{5,6},{6,5},{7,4},{8,11},{9,10},{10,... | collective-permute-start | bytes 49160 | tf_op jit(solution)/shard_map/ppermute | solution.py:768
  13.5 1.5 %collective-permute-start.1 = (f32[16,256]{1,0:T(8,128)S(1)}, f32[16,256]{1,0:T(8,128)S(1)}, u32[]{:S(2)}, u32[]{:S(2)}) collective-permute-start(f32[16,256]{1,0:T(8,128)S(1)} %get-tuple-element.41.refs_3_), channel_id=1, source_target_pairs={{3,4},{7,8},{11,12},{15,16},{19,20},{23,24},{27,28},{2,5},{6,9},{1... | collective-permute-start | bytes 49160 | tf_op jit(solution)/shard_map/ppermute | solution.py:767
  19.0 12.0 %all-to-all-start.1 = ((f32[32,1,128]{2,1,0:T(1,128)}), f32[32,1,128]{2,1,0:T(1,128)S(1)}, u32[]{:S(2)}, u32[]{:S(2)}) async-start(f32[32,1,128]{2,1,0:T(1,128)} %bitcast.17), calls=%async_computation.1 | async-start | bytes 32768 | tf_op jit(solution)/shard_map/all_to_all | solution.py:762
  23.9 3.2 %collective-permute-start.5 = (f32[16,256]{1,0:T(8,128)S(1)}, f32[16,256]{1,0:T(8,128)S(1)}, u32[]{:S(2)}, u32[]{:S(2)}) collective-permute-start(f32[16,256]{1,0:T(8,128)S(1)} %get-tuple-element.51.refs_3_), channel_id=1, source_target_pairs={{0,3},{1,2},{2,1},{3,0},{4,7},{5,6},{6,5},{7,4},{8,11},{9,10},{10,... | collective-permute-start | bytes 49160 | tf_op jit(solution)/shard_map/ppermute | solution.py:768
  25.5 1.7 %collective-permute-start.4 = (f32[16,256]{1,0:T(8,128)S(1)}, f32[16,256]{1,0:T(8,128)S(1)}, u32[]{:S(2)}, u32[]{:S(2)}) collective-permute-start(f32[16,256]{1,0:T(8,128)S(1)} %get-tuple-element.51.refs_3_), channel_id=1, source_target_pairs={{3,4},{7,8},{11,12},{15,16},{19,20},{23,24},{27,28},{2,5},{6,9},{1... | collective-permute-start | bytes 49160 | tf_op jit(solution)/shard_map/ppermute | solution.py:767
  26.6 1.2 %collective-permute-start.3 = (f32[16,256]{1,0:T(8,128)S(1)}, f32[16,256]{1,0:T(8,128)S(1)}, u32[]{:S(2)}, u32[]{:S(2)}) collective-permute-start(f32[16,256]{1,0:T(8,128)S(1)} %get-tuple-element.58), channel_id=1, source_target_pairs={{0,1},{1,0},{2,3},{3,2},{4,5},{5,4},{6,7},{7,6},{8,9},{9,8},{10,11... | collective-permute-start | bytes 49160 | tf_op jit(solution)/shard_map/ppermute | solution.py:782
  32.2 10.3 %all-to-all-start.2 = ((f32[32,1,128]{2,1,0:T(1,128)}), f32[32,1,128]{2,1,0:T(1,128)S(1)}, u32[]{:S(2)}, u32[]{:S(2)}) async-start(f32[32,1,128]{2,1,0:T(1,128)} %bitcast.16), calls=%async_computation.2 | async-start | bytes 32768 | tf_op jit(solution)/shard_map/all_to_all | solution.py:762
  36.8 2.0 %collective-permute-start.6 = (f32[16,256]{1,0:T(8,128)S(1)}, f32[16,256]{1,0:T(8,128)S(1)}, u32[]{:S(2)}, u32[]{:S(2)}) collective-permute-start(f32[16,256]{1,0:T(8,128)S(1)} %get-tuple-element.69), channel_id=1, source_target_pairs={{0,1},{1,0},{2,3},{3,2},{4,5},{5,4},{6,7},{7,6},{8,9},{9,8},{10,11... | collective-permute-start | bytes 49160 | tf_op jit(solution)/shard_map/ppermute | solution.py:782
  37.0 3.2 %collective-permute-start.8 = (f32[16,256]{1,0:T(8,128)S(1)}, f32[16,256]{1,0:T(8,128)S(1)}, u32[]{:S(2)}, u32[]{:S(2)}) collective-permute-start(f32[16,256]{1,0:T(8,128)S(1)} %get-tuple-element.63.refs_3_), channel_id=1, source_target_pairs={{0,3},{1,2},{2,1},{3,0},{4,7},{5,6},{6,5},{7,4},{8,11},{9,10},{10,... | collective-permute-start | bytes 49160 | tf_op jit(solution)/shard_map/ppermute | solution.py:768
  38.7 1.5 %collective-permute-start.7 = (f32[16,256]{1,0:T(8,128)S(1)}, f32[16,256]{1,0:T(8,128)S(1)}, u32[]{:S(2)}, u32[]{:S(2)}) collective-permute-start(f32[16,256]{1,0:T(8,128)S(1)} %get-tuple-element.63.refs_3_), channel_id=1, source_target_pairs={{3,4},{7,8},{11,12},{15,16},{19,20},{23,24},{27,28},{2,5},{6,9},{1... | collective-permute-start | bytes 49160 | tf_op jit(solution)/shard_map/ppermute | solution.py:767

commit v7 on v6

--- a/solution.py
+++ b/solution.py
@@ -292,6 +292,7 @@
     width = bins * SLOT
     nodes = bins * TILE
     fastest = jnp.max(speeds[...], axis=0, keepdims=True)
+    fastest = jnp.where(iota((1, LANES), 1) < META, fastest, 0.0)
     fastest = jnp.max(fastest, axis=1, keepdims=True)
     time_step = courant / (jnp.sqrt(fastest) + sound_speed)
 
@@ -486,12 +487,17 @@
             mass = m_ref[pl.ds(LANES * s, LANES)].reshape(1, LANES)
             counted = (mass > 0.0) & (b < live[0])
             fastest = jnp.maximum(fastest, jnp.where(counted, speed, 0.0))
-    outbox[...] = jnp.broadcast_to(jnp.max(fastest, axis=1, keepdims=True), outbox.shape)
+    copies[2].wait()
+    lane = iota((1, LANES), 1)
+    fastest = jnp.broadcast_to(jnp.max(fastest, axis=1, keepdims=True), (1, LANES))
+    for b in range(bins):
+        fastest = jnp.where(lane == META + b, blocks[b].astype(F32), fastest)
+    outbox[...] = jnp.broadcast_to(fastest, outbox.shape)
     pltpu.make_async_copy(outbox, speeds, sem).start()
 
     @pl.when(live[0] >= 0)
     def _():
-        for copy in copies[2:]:
+        for copy in copies[3:]:
             copy.wait()
         relay(v_ref, 3, motion_ref, 0)
         relay_flat(m_ref, MASS)
@@ -578,17 +584,27 @@
     place_own(own, low, middle, high, home[...])
 
 
+def sides_kernel(bins, device_total, live, device, speeds, geometry, sides_ref):
+    lane = iota((1, LANES), 1)
+    key = geometry[0:1, :]
+    left, right = jnp.maximum(device - 1, 0), jnp.minimum(device + 1, device_total - 1)
+    for side, index in enumerate((left, right)):
+        row = speeds[pl.ds(index, 1), :]
+        numbers = [
+            jnp.max(jnp.where(lane == META + b, row, 0.0), axis=1, keepdims=True)
+            for b in range(bins)
+        ]
+        sides_ref[side] = placing(numbers, key, bins)
+
+
 def second_kernel(
     bins, device_total, live, device, meta, old_ref, speeds, own, geometry, highs, lows, along,
-    near, outer, inner, state_ref, new_speeds, far, new_highs, new_lows, new_along, channels,
-    sides_ref, across, outbox, sem,
+    near, outer, inner, sides_ref, state_ref, new_speeds, far, new_highs, new_lows, new_along,
+    channels, across, outbox, sem,
 ):
     rows = state_ref.shape[0] // ROWS
     around = halos(near, outer, inner, device, device_total)
-    key = geometry[0:1, :]
-    sides = [placing(block_numbers(block[7:8, :], bins), key, bins) for block in around]
-    for side in range(2):
-        sides_ref[side] = sides[side]
+    sides = [sides_ref[0], sides_ref[1]]
 
     def started(velocity):
         send_speed(velocity, old_ref[pl.ds(rows * MASS, rows), :], new_speeds, outbox, sem)
@@ -784,11 +800,12 @@
             state, speeds, own, geometry, highs, lows, along, from_near, from_outer, from_inner,
         )
         if step == 0:
-            state, speeds, far, highs, lows, along, channels, sides = call(
+            (sides,) = call(sides_kernel, (live_count, me), (speeds, geometry), [sides_shape], [])
+            state, speeds, far, highs, lows, along, channels = call(
                 second_kernel,
                 (live_count, me),
-                (meta, *arguments),
-                [held[0], speeds_shape, *grid_held, sides_shape],
+                (meta, *arguments, sides),
+                [held[0], speeds_shape, *grid_held],
                 [across] + sending,
             )
         elif step < STEPS - 1:

time: 44.1 us -> 43.9 us (level)
    all_to_all x3, waiting for transfers between devices: 7.62 us -> 9.04 us  [local(): speeds = lax.all_to_all(speeds, 'space', 0, 0, tiled=True)]
    ppermute x3, waiting for transfers between devices: 3.19 us -> 1.77 us  [local(): from_inner = lax.ppermute(far, 'space', inner_pairs)]
    pallas_call x9 -> x10, Pallas kernels: 9.41 us -> 9.54 us  [call(): pl.pallas_call(kernel, in_specs=[smem] * len(scalars) + in_specs, out_sha...]
  transfers between devices with their start and end apart: 12 -> 12, of which waited for: 7 -> 6; matrix products, arithmetic and copies ran while one was open for 0% -> 0% of each run, Pallas kernels for 8% -> 9%
where the time goes in v7:
time: 43.9 us; the launch traced here: 43.7 us
  starting transfers between devices  21.3 us (49%)
  waiting for transfers between devices  11.5 us (26%)
  Pallas kernels  9.54 us (22%)
  between operations  1.37 us (3%)
    all_to_all x3, starting transfers between devices, local(): speeds = lax.all_to_all(speeds, 'space', 0, 0, tiled=True)  15.1 us
    pallas_call x10, Pallas kernels, call(): pl.pallas_call(kernel, in_specs=[smem] * len(scalars) + in_specs, out_sha...  9.54 us
    all_to_all x3, waiting for transfers between devices, local(): speeds = lax.all_to_all(speeds, 'space', 0, 0, tiled=True)  9.04 us
    ppermute x3, starting transfers between devices, local(): from_inner = lax.ppermute(far, 'space', inner_pairs)  4.82 us
    ppermute x3, waiting for transfers between devices, local(): from_inner = lax.ppermute(far, 'space', inner_pairs)  1.77 us
  transfers between devices with their start and end apart: 12, of which 6 were waited for; matrix products, arithmetic and copies ran while one was open for 0% of the time, Pallas kernels for 9%

profile of v7, /device:TPU:0, one launch (start us, length us, event | category | flops | bytes accessed | tf_op | source)
XLA Modules:
  0.0 43.7 jit_solution(17503692711054659944)
XLA Ops:
  1.3 1.6 %shard_map.111 = (f32[272,128]{1,0:T(8,128)S(1)}, f32[192,128]{1,0:T(8,128)S(1)}, f32[32,128]{1,0:T(8,128)}, f32[8,256]{1,0:T(8,128)S(1)}) custom-call(s32[1]{0:T(128)S(6)} %copy.15.refs_0_, s32[1]{0:T(128)} %bitcast.refs_1_, s32[8]{0:T(128)} %refs_2_.1, f32[3,4096]{1,0:T(4,128)} %refs_3_.1, f32[3,4096]{1,0:T(4,128)} %refs_4_.1, f32[9,4096]{1,0:T(8,128)} %refs_5_.1, ...), custom_call_target="tpu_custom_call" | custom-call | tf_op jit(solution)/shard_map/pallas_call | solution.py:742
  2.8 7.3 %all-to-all-start = ((f32[32,1,128]{2,1,0:T(1,128)}), f32[32,1,128]{2,1,0:T(1,128)S(1)}, u32[]{:S(2)}, u32[]{:S(2)}) async-start(f32[32,1,128]{2,1,0:T(1,128)} %bitcast.19), calls=%async_computation | async-start | bytes 32768 | tf_op jit(solution)/shard_map/all_to_all | solution.py:778
  10.2 0.6 %shard_map.112 = (f32[16,256]{1,0:T(8,128)S(1)}, bf16[4,144,512]{2,1,0:T(8,128)(2,1)S(1)}, bf16[4,144,512]{2,1,0:T(8,128)(2,1)S(1)}, f32[192,128]{1,0:T(8,128)S(1)}, f32[512,128]{1,0:T(8,128)S(1)}) custom-call(s32[1]{0:T(128)S(6)} %copy.15.refs_0_, s32[1]{0:T(128)} %bitcast.refs_1_, f32[272,128]{1,0:T(8,128)S(1)} %get-tuple-element.37.refs_2_.refs_3_, ...), custom_call_target="tpu_custom_call" | custom-call | tf_op jit(solution)/shard_map/pallas_call | solution.py:742
  10.8 0.8 %shard_map.113 = (f32[16,256]{1,0:T(8,128)S(1)}, f32[48,256]{1,0:T(8,128)S(1)}, f32[24,256]{1,0:T(8,128)S(1)}, bf16[192,256]{1,0:T(8,128)(2,1)S(1)}) custom-call(s32[1]{0:T(128)S(6)} %copy.15.refs_0_, s32[1]{0:T(128)} %bitcast.refs_1_, f32[8,256]{1,0:T(8,128)S(1)} %get-tuple-element.36.refs_4_.refs_2_, f32[16,256]{1,0:T(8,128)S(1)} %get-tuple-element.40.refs_3_, ...), custom_call_target="tpu_custom_call" | custom-call | tf_op jit(solution)/shard_map/pallas_call | solution.py:742
  11.6 0.3 collective-permute-start
  11.9 1.6 %collective-permute-start.2 = (f32[16,256]{1,0:T(8,128)S(1)}, f32[16,256]{1,0:T(8,128)S(1)}, u32[]{:S(2)}, u32[]{:S(2)}) collective-permute-start(f32[16,256]{1,0:T(8,128)S(1)} %get-tuple-element.40.refs_3_), channel_id=1, source_target_pairs={{0,3},{1,2},{2,1},{3,0},{4,7},{5,6},{6,5},{7,4},{8,11},{9,10},{10,... | collective-permute-start | bytes 49160 | tf_op jit(solution)/shard_map/ppermute | solution.py:784
  13.5 0.1 collective-permute-start.1
  13.6 3.7 %all-to-all-done = f32[32,1,128]{2,1,0:T(1,128)S(1)} async-done(((f32[32,1,128]{2,1,0:T(1,128)}), f32[32,1,128]{2,1,0:T(1,128)S(1)}, u32[]{:S(2)}, u32[]{:S(2)}) %all-to-all-start) | async-done | bytes 16416 | tf_op jit(solution)/shard_map/all_to_all | solution.py:778
  17.3 0.3 shard_map.114.refs_13_.refs_12_
  17.6 0.0 collective-permute-done.refs_10_
  17.6 0.0 collective-permute-done.2.refs_12_
  17.6 0.0 collective-permute-done.1.refs_11_
  17.6 1.5 %shard_map.115 = (f32[272,128]{1,0:T(8,128)S(1)}, f32[32,128]{1,0:T(8,128)}, f32[16,256]{1,0:T(8,128)S(1)}, bf16[4,144,512]{2,1,0:T(8,128)(2,1)S(1)}, bf16[4,144...) custom-call(s32[1]{0:T(128)S(6)} %copy.15.refs_0_, s32[1]{0:T(128)} %bitcast.refs_1_, ...), custom_call_target="tpu_custom_call" | custom-call | tf_op jit(solution)/shard_map/pallas_call | solution.py:742
  19.1 4.6 %all-to-all-start.1 = ((f32[32,1,128]{2,1,0:T(1,128)}), f32[32,1,128]{2,1,0:T(1,128)S(1)}, u32[]{:S(2)}, u32[]{:S(2)}) async-start(f32[32,1,128]{2,1,0:T(1,128)} %bitcast.18), calls=%async_computation.1 | async-start | bytes 32768 | tf_op jit(solution)/shard_map/all_to_all | solution.py:778
  23.8 1.6 %collective-permute-start.5 = (f32[16,256]{1,0:T(8,128)S(1)}, f32[16,256]{1,0:T(8,128)S(1)}, u32[]{:S(2)}, u32[]{:S(2)}) collective-permute-start(f32[16,256]{1,0:T(8,128)S(1)} %get-tuple-element.50.refs_3_), channel_id=1, source_target_pairs={{0,3},{1,2},{2,1},{3,0},{4,7},{5,6},{6,5},{7,4},{8,11},{9,10},{10,... | collective-permute-start | bytes 49160 | tf_op jit(solution)/shard_map/ppermute | solution.py:784
  25.3 0.4 collective-permute-start.4
  25.7 0.8 %shard_map.116 = (f32[16,256]{1,0:T(8,128)S(1)}, f32[48,256]{1,0:T(8,128)S(1)}) custom-call(s32[1]{0:T(128)S(6)} %copy.15.refs_0_, s32[1]{0:T(128)} %bitcast.refs_1_, f32[8,256]{1,0:T(8,128)S(1)} %get-tuple-element.36.refs_4_.refs_2_, f32[16,256]{1,0:T(8,128)S(1)} %get-tuple-element.50.refs_3_, bf16[4,144,512]{2,1,0:T(8,128)(2,1)S(1)} %get-tuple-element.51.refs_4_.refs_6_, ...), custom_call_target="tpu_custom_call" | custom-call | tf_op jit(solution)/shard_map/pallas_call | solution.py:742
  26.5 0.1 collective-permute-start.3
  26.6 0.4 collective-permute-done.5.refs_11_
  27.0 0.0 collective-permute-done.4.refs_10_
  27.0 0.7 %collective-permute-done.3.refs_9_ = f32[16,256]{1,0:T(8,128)S(1)} collective-permute-done((f32[16,256]{1,0:T(8,128)S(1)}, f32[16,256]{1,0:T(8,128)S(1)}, u32[]{:S(2)}, u32[]{:S(2)}) %collective-permute-start.3) | collective-permute-done | bytes 16416 | tf_op jit(solution)/shard_map/ppermute | solution.py:798
  27.7 3.2 %all-to-all-done.1 = f32[32,1,128]{2,1,0:T(1,128)S(1)} async-done(((f32[32,1,128]{2,1,0:T(1,128)}), f32[32,1,128]{2,1,0:T(1,128)S(1)}, u32[]{:S(2)}, u32[]{:S(2)}) %all-to-all-start.1) | async-done | bytes 16416 | tf_op jit(solution)/shard_map/all_to_all | solution.py:778
  30.9 1.1 %shard_map.117 = (f32[272,128]{1,0:T(8,128)S(1)}, f32[192,128]{1,0:T(8,128)S(1)}, f32[32,128]{1,0:T(8,128)}) custom-call(s32[1]{0:T(128)S(6)} %copy.15.refs_0_, s32[1]{0:T(128)} %bitcast.refs_1_, f32[272,128]{1,0:T(8,128)S(1)} %get-tuple-element.48.refs_2_, f32[32,128]{1,0:T(8,128)S(1)} %bitcast.16, f32[48,256]{1,0:T(8,128)S(1)} %get-tuple-element.56.refs_4_, ...), custom_call_target="tpu_custom_call" | custom-call | tf_op jit(solution)/shard_map/pallas_call | solution.py:742
  32.0 3.2 %all-to-all-start.2 = ((f32[32,1,128]{2,1,0:T(1,128)}), f32[32,1,128]{2,1,0:T(1,128)S(1)}, u32[]{:S(2)}, u32[]{:S(2)}) async-start(f32[32,1,128]{2,1,0:T(1,128)} %bitcast.17), calls=%async_computation.2 | async-start | bytes 32768 | tf_op jit(solution)/shard_map/all_to_all | solution.py:778
  35.2 0.6 %shard_map.118 = (f32[16,256]{1,0:T(8,128)S(1)}, bf16[4,144,512]{2,1,0:T(8,128)(2,1)S(1)}, bf16[4,144,512]{2,1,0:T(8,128)(2,1)S(1)}, f32[192,128]{1,0:T(8,128)S(1)}, f32[512,128]{1,0:T(8,128)S(1)}) custom-call(s32[1]{0:T(128)S(6)} %copy.15.refs_0_, s32[1]{0:T(128)} %bitcast.refs_1_, f32[272,128]{1,0:T(8,128)S(1)} %get-tuple-element.58.refs_2_, ...), custom_call_target="tpu_custom_call" | custom-call | tf_op jit(solution)/shard_map/pallas_call | solution.py:742
  35.8 0.8 %shard_map.119 = (f32[16,256]{1,0:T(8,128)S(1)}, f32[48,256]{1,0:T(8,128)S(1)}) custom-call(s32[1]{0:T(128)S(6)} %copy.15.refs_0_, s32[1]{0:T(128)} %bitcast.refs_1_, f32[8,256]{1,0:T(8,128)S(1)} %get-tuple-element.36.refs_4_.refs_2_, f32[16,256]{1,0:T(8,128)S(1)} %get-tuple-element.61.refs_3_, bf16[4,144,512]{2,1,0:T(8,128)(2,1)S(1)} %get-tuple-element.62.refs_4_.refs_6_, ...), custom_call_target="tpu_custom_call" | custom-call | tf_op jit(solution)/shard_map/pallas_call | solution.py:742
  36.6 0.3 collective-permute-start.6
  36.9 1.6 %collective-permute-start.8 = (f32[16,256]{1,0:T(8,128)S(1)}, f32[16,256]{1,0:T(8,128)S(1)}, u32[]{:S(2)}, u32[]{:S(2)}) collective-permute-start(f32[16,256]{1,0:T(8,128)S(1)} %get-tuple-element.61.refs_3_), channel_id=1, source_target_pairs={{0,3},{1,2},{2,1},{3,0},{4,7},{5,6},{6,5},{7,4},{8,11},{9,10},{10,... | collective-permute-start | bytes 49160 | tf_op jit(solution)/shard_map/ppermute | solution.py:784
  38.5 0.1 collective-permute-start.7
  38.6 0.0 collective-permute-done.6.refs_9_
  38.6 1.4 %collective-permute-done.8.refs_11_ = f32[16,256]{1,0:T(8,128)S(1)} collective-permute-done((f32[16,256]{1,0:T(8,128)S(1)}, f32[16,256]{1,0:T(8,128)S(1)}, u32[]{:S(2)}, u32[]{:S(2)}) %collective-permute-start.8) | collective-permute-done | bytes 16416 | tf_op jit(solution)/shard_map/ppermute | solution.py:784
  40.0 0.0 collective-permute-done.7.refs_10_
  40.1 2.2 %all-to-all-done.2 = f32[32,1,128]{2,1,0:T(1,128)S(1)} async-done(((f32[32,1,128]{2,1,0:T(1,128)}), f32[32,1,128]{2,1,0:T(1,128)S(1)}, u32[]{:S(2)}, u32[]{:S(2)}) %all-to-all-start.2) | async-done | bytes 16416 | tf_op jit(solution)/shard_map/all_to_all | solution.py:778
  42.3 1.4 %shard_map.120 = (f32[3,4096]{1,0:T(4,128)}, f32[3,4096]{1,0:T(4,128)}, f32[9,4096]{1,0:T(8,128)}, f32[9,4096]{1,0:T(8,128)}) custom-call(s32[1]{0:T(128)S(6)} %copy.15.refs_0_, s32[1]{0:T(128)} %bitcast.refs_1_, f32[272,128]{1,0:T(8,128)S(1)} %get-tuple-element.58.refs_2_, f32[32,128]{1,0:T(8,128)S(1)} %bitcast.15, ...), custom_call_target="tpu_custom_call" | custom-call | tf_op jit(solution)/shard_map/pallas_call | solution.py:742
Async XLA Ops:
  2.8 14.4 %all-to-all-start = ((f32[32,1,128]{2,1,0:T(1,128)}), f32[32,1,128]{2,1,0:T(1,128)S(1)}, u32[]{:S(2)}, u32[]{:S(2)}) async-start(f32[32,1,128]{2,1,0:T(1,128)} %bitcast.19), calls=%async_computation | async-start | bytes 32768 | tf_op jit(solution)/shard_map/all_to_all | solution.py:778
  11.6 5.9 %collective-permute-start = (f32[16,256]{1,0:T(8,128)S(1)}, f32[16,256]{1,0:T(8,128)S(1)}, u32[]{:S(2)}, u32[]{:S(2)}) collective-permute-start(f32[16,256]{1,0:T(8,128)S(1)} %get-tuple-element.47), channel_id=1, source_target_pairs={{0,1},{1,0},{2,3},{3,2},{4,5},{5,4},{6,7},{7,6},{8,9},{9,8},{10,11... | collective-permute-start | bytes 49160 | tf_op jit(solution)/shard_map/ppermute | solution.py:798
  11.9 5.7 %collective-permute-start.2 = (f32[16,256]{1,0:T(8,128)S(1)}, f32[16,256]{1,0:T(8,128)S(1)}, u32[]{:S(2)}, u32[]{:S(2)}) collective-permute-start(f32[16,256]{1,0:T(8,128)S(1)} %get-tuple-element.40.refs_3_), channel_id=1, source_target_pairs={{0,3},{1,2},{2,1},{3,0},{4,7},{5,6},{6,5},{7,4},{8,11},{9,10},{10,... | collective-permute-start | bytes 49160 | tf_op jit(solution)/shard_map/ppermute | solution.py:784
  13.5 4.1 %collective-permute-start.1 = (f32[16,256]{1,0:T(8,128)S(1)}, f32[16,256]{1,0:T(8,128)S(1)}, u32[]{:S(2)}, u32[]{:S(2)}) collective-permute-start(f32[16,256]{1,0:T(8,128)S(1)} %get-tuple-element.40.refs_3_), channel_id=1, source_target_pairs={{3,4},{7,8},{11,12},{15,16},{19,20},{23,24},{27,28},{2,5},{6,9},{1... | collective-permute-start | bytes 49160 | tf_op jit(solution)/shard_map/ppermute | solution.py:783
  19.1 11.7 %all-to-all-start.1 = ((f32[32,1,128]{2,1,0:T(1,128)}), f32[32,1,128]{2,1,0:T(1,128)S(1)}, u32[]{:S(2)}, u32[]{:S(2)}) async-start(f32[32,1,128]{2,1,0:T(1,128)} %bitcast.18), calls=%async_computation.1 | async-start | bytes 32768 | tf_op jit(solution)/shard_map/all_to_all | solution.py:778
  23.8 3.2 %collective-permute-start.5 = (f32[16,256]{1,0:T(8,128)S(1)}, f32[16,256]{1,0:T(8,128)S(1)}, u32[]{:S(2)}, u32[]{:S(2)}) collective-permute-start(f32[16,256]{1,0:T(8,128)S(1)} %get-tuple-element.50.refs_3_), channel_id=1, source_target_pairs={{0,3},{1,2},{2,1},{3,0},{4,7},{5,6},{6,5},{7,4},{8,11},{9,10},{10,... | collective-permute-start | bytes 49160 | tf_op jit(solution)/shard_map/ppermute | solution.py:784
  25.3 1.7 %collective-permute-start.4 = (f32[16,256]{1,0:T(8,128)S(1)}, f32[16,256]{1,0:T(8,128)S(1)}, u32[]{:S(2)}, u32[]{:S(2)}) collective-permute-start(f32[16,256]{1,0:T(8,128)S(1)} %get-tuple-element.50.refs_3_), channel_id=1, source_target_pairs={{3,4},{7,8},{11,12},{15,16},{19,20},{23,24},{27,28},{2,5},{6,9},{1... | collective-permute-start | bytes 49160 | tf_op jit(solution)/shard_map/ppermute | solution.py:783
  26.5 1.2 %collective-permute-start.3 = (f32[16,256]{1,0:T(8,128)S(1)}, f32[16,256]{1,0:T(8,128)S(1)}, u32[]{:S(2)}, u32[]{:S(2)}) collective-permute-start(f32[16,256]{1,0:T(8,128)S(1)} %get-tuple-element.57), channel_id=1, source_target_pairs={{0,1},{1,0},{2,3},{3,2},{4,5},{5,4},{6,7},{7,6},{8,9},{9,8},{10,11... | collective-permute-start | bytes 49160 | tf_op jit(solution)/shard_map/ppermute | solution.py:798
  32.0 10.3 %all-to-all-start.2 = ((f32[32,1,128]{2,1,0:T(1,128)}), f32[32,1,128]{2,1,0:T(1,128)S(1)}, u32[]{:S(2)}, u32[]{:S(2)}) async-start(f32[32,1,128]{2,1,0:T(1,128)} %bitcast.17), calls=%async_computation.2 | async-start | bytes 32768 | tf_op jit(solution)/shard_map/all_to_all | solution.py:778
  36.6 2.0 %collective-permute-start.6 = (f32[16,256]{1,0:T(8,128)S(1)}, f32[16,256]{1,0:T(8,128)S(1)}, u32[]{:S(2)}, u32[]{:S(2)}) collective-permute-start(f32[16,256]{1,0:T(8,128)S(1)} %get-tuple-element.67), channel_id=1, source_target_pairs={{0,1},{1,0},{2,3},{3,2},{4,5},{5,4},{6,7},{7,6},{8,9},{9,8},{10,11... | collective-permute-start | bytes 49160 | tf_op jit(solution)/shard_map/ppermute | solution.py:798
  36.9 3.2 %collective-permute-start.8 = (f32[16,256]{1,0:T(8,128)S(1)}, f32[16,256]{1,0:T(8,128)S(1)}, u32[]{:S(2)}, u32[]{:S(2)}) collective-permute-start(f32[16,256]{1,0:T(8,128)S(1)} %get-tuple-element.61.refs_3_), channel_id=1, source_target_pairs={{0,3},{1,2},{2,1},{3,0},{4,7},{5,6},{6,5},{7,4},{8,11},{9,10},{10,... | collective-permute-start | bytes 49160 | tf_op jit(solution)/shard_map/ppermute | solution.py:784
  38.5 1.5 %collective-permute-start.7 = (f32[16,256]{1,0:T(8,128)S(1)}, f32[16,256]{1,0:T(8,128)S(1)}, u32[]{:S(2)}, u32[]{:S(2)}) collective-permute-start(f32[16,256]{1,0:T(8,128)S(1)} %get-tuple-element.61.refs_3_), channel_id=1, source_target_pairs={{3,4},{7,8},{11,12},{15,16},{19,20},{23,24},{27,28},{2,5},{6,9},{1... | collective-permute-start | bytes 49160 | tf_op jit(solution)/shard_map/ppermute | solution.py:783

commit v8 on v7

--- a/solution.py
+++ b/solution.py
@@ -284,7 +284,7 @@
 
 def to_particles(
     live, old_ref, device, bins, device_total, geometry, own, sides, speeds, blocks_around,
-    highs, lows, along, shuffle, started, finish,
+    highs, lows, along, shuffle, started, finish, whole=False,
 ):
     rows = old_ref.shape[0] // ROWS
     quarters = rows // bins
@@ -383,11 +383,12 @@
             + shuffle[pl.ds(kind * span + 5 + c, rows, stride=8), :]
         )
 
-    gather((0, 1, 2) if live is None else (0,))
+    whole = whole or live is None
+    gather((0, 1, 2) if whole else (0,))
     started([take(0, c) for c in range(3)])
 
     def rest():
-        if live is not None:
+        if not whole:
             gather((1, 2))
         velocity = [take(0, c) for c in range(3)]
         affine = [None] * 9
@@ -617,8 +618,8 @@
         )
 
     to_particles(
-        None, old_ref, device, bins, device_total, geometry, own, sides, speeds, around, highs,
-        lows, along, channels, started, finish,
+        live, old_ref, device, bins, device_total, geometry, own, sides, speeds, around, highs,
+        lows, along, channels, started, finish, whole=True,
     )
     pltpu.make_async_copy(outbox, new_speeds, sem).wait()
 

time: 43.9 us -> 43.8 us (level)
  no operation moved by 1% of the time
where the time goes in v8:
time: 43.8 us; the launch traced here: 43.5 us
  starting transfers between devices  21.3 us (49%)
  waiting for transfers between devices  11.5 us (26%)
  Pallas kernels  9.37 us (21%)
  between operations  1.37 us (3%)
    all_to_all x3, starting transfers between devices, local(): speeds = lax.all_to_all(speeds, 'space', 0, 0, tiled=True)  15.1 us
    pallas_call x10, Pallas kernels, call(): pl.pallas_call(kernel, in_specs=[smem] * len(scalars) + in_specs, out_sha...  9.37 us
    all_to_all x3, waiting for transfers between devices, local(): speeds = lax.all_to_all(speeds, 'space', 0, 0, tiled=True)  9.05 us
    ppermute x3, starting transfers between devices, local(): from_inner = lax.ppermute(far, 'space', inner_pairs)  4.82 us
    ppermute x3, waiting for transfers between devices, local(): from_inner = lax.ppermute(far, 'space', inner_pairs)  1.77 us
  transfers between devices with their start and end apart: 12, of which 6 were waited for; matrix products, arithmetic and copies ran while one was open for 0% of the time, Pallas kernels for 9%

profile of v8, /device:TPU:0, one launch (start us, length us, event | category | flops | bytes accessed | tf_op | source)
XLA Modules:
  0.0 43.5 jit_solution(187585528980345200)
XLA Ops:
  1.3 1.6 %shard_map.111 = (f32[272,128]{1,0:T(8,128)S(1)}, f32[192,128]{1,0:T(8,128)S(1)}, f32[32,128]{1,0:T(8,128)}, f32[8,256]{1,0:T(8,128)S(1)}) custom-call(s32[1]{0:T(128)S(6)} %copy.15.refs_0_, s32[1]{0:T(128)} %bitcast.refs_1_, s32[8]{0:T(128)} %refs_2_.1, f32[3,4096]{1,0:T(4,128)} %refs_3_.1, f32[3,4096]{1,0:T(4,128)} %refs_4_.1, f32[9,4096]{1,0:T(8,128)} %refs_5_.1, ...), custom_call_target="tpu_custom_call" | custom-call | tf_op jit(solution)/shard_map/pallas_call | solution.py:743
  2.8 7.3 %all-to-all-start = ((f32[32,1,128]{2,1,0:T(1,128)}), f32[32,1,128]{2,1,0:T(1,128)S(1)}, u32[]{:S(2)}, u32[]{:S(2)}) async-start(f32[32,1,128]{2,1,0:T(1,128)} %bitcast.19), calls=%async_computation | async-start | bytes 32768 | tf_op jit(solution)/shard_map/all_to_all | solution.py:779
  10.2 0.6 %shard_map.112 = (f32[16,256]{1,0:T(8,128)S(1)}, bf16[4,144,512]{2,1,0:T(8,128)(2,1)S(1)}, bf16[4,144,512]{2,1,0:T(8,128)(2,1)S(1)}, f32[192,128]{1,0:T(8,128)S(1)}, f32[512,128]{1,0:T(8,128)S(1)}) custom-call(s32[1]{0:T(128)S(6)} %copy.15.refs_0_, s32[1]{0:T(128)} %bitcast.refs_1_, f32[272,128]{1,0:T(8,128)S(1)} %get-tuple-element.37.refs_2_.refs_3_, ...), custom_call_target="tpu_custom_call" | custom-call | tf_op jit(solution)/shard_map/pallas_call | solution.py:743
  10.8 0.8 %shard_map.113 = (f32[16,256]{1,0:T(8,128)S(1)}, f32[48,256]{1,0:T(8,128)S(1)}, f32[24,256]{1,0:T(8,128)S(1)}, bf16[192,256]{1,0:T(8,128)(2,1)S(1)}) custom-call(s32[1]{0:T(128)S(6)} %copy.15.refs_0_, s32[1]{0:T(128)} %bitcast.refs_1_, f32[8,256]{1,0:T(8,128)S(1)} %get-tuple-element.36.refs_4_.refs_2_, f32[16,256]{1,0:T(8,128)S(1)} %get-tuple-element.40.refs_3_, ...), custom_call_target="tpu_custom_call" | custom-call | tf_op jit(solution)/shard_map/pallas_call | solution.py:743
  11.6 0.3 collective-permute-start
  11.9 1.6 %collective-permute-start.2 = (f32[16,256]{1,0:T(8,128)S(1)}, f32[16,256]{1,0:T(8,128)S(1)}, u32[]{:S(2)}, u32[]{:S(2)}) collective-permute-start(f32[16,256]{1,0:T(8,128)S(1)} %get-tuple-element.40.refs_3_), channel_id=1, source_target_pairs={{0,3},{1,2},{2,1},{3,0},{4,7},{5,6},{6,5},{7,4},{8,11},{9,10},{10,... | collective-permute-start | bytes 49160 | tf_op jit(solution)/shard_map/ppermute | solution.py:785
  13.5 0.1 collective-permute-start.1
  13.6 3.7 %all-to-all-done = f32[32,1,128]{2,1,0:T(1,128)S(1)} async-done(((f32[32,1,128]{2,1,0:T(1,128)}), f32[32,1,128]{2,1,0:T(1,128)S(1)}, u32[]{:S(2)}, u32[]{:S(2)}) %all-to-all-start) | async-done | bytes 16416 | tf_op jit(solution)/shard_map/all_to_all | solution.py:779
  17.3 0.3 shard_map.114.refs_13_.refs_12_
  17.6 0.0 collective-permute-done.refs_10_
  17.6 0.0 collective-permute-done.2.refs_12_
  17.6 0.0 collective-permute-done.1.refs_11_
  17.6 1.4 %shard_map.115 = (f32[272,128]{1,0:T(8,128)S(1)}, f32[32,128]{1,0:T(8,128)}, f32[16,256]{1,0:T(8,128)S(1)}, bf16[4,144,512]{2,1,0:T(8,128)(2,1)S(1)}, bf16[4,144...) custom-call(s32[1]{0:T(128)S(6)} %copy.15.refs_0_, s32[1]{0:T(128)} %bitcast.refs_1_, ...), custom_call_target="tpu_custom_call" | custom-call | tf_op jit(solution)/shard_map/pallas_call | solution.py:743
  19.0 4.6 %all-to-all-start.1 = ((f32[32,1,128]{2,1,0:T(1,128)}), f32[32,1,128]{2,1,0:T(1,128)S(1)}, u32[]{:S(2)}, u32[]{:S(2)}) async-start(f32[32,1,128]{2,1,0:T(1,128)} %bitcast.18), calls=%async_computation.1 | async-start | bytes 32768 | tf_op jit(solution)/shard_map/all_to_all | solution.py:779
  23.6 1.6 %collective-permute-start.5 = (f32[16,256]{1,0:T(8,128)S(1)}, f32[16,256]{1,0:T(8,128)S(1)}, u32[]{:S(2)}, u32[]{:S(2)}) collective-permute-start(f32[16,256]{1,0:T(8,128)S(1)} %get-tuple-element.50.refs_3_), channel_id=1, source_target_pairs={{0,3},{1,2},{2,1},{3,0},{4,7},{5,6},{6,5},{7,4},{8,11},{9,10},{10,... | collective-permute-start | bytes 49160 | tf_op jit(solution)/shard_map/ppermute | solution.py:785
  25.1 0.4 collective-permute-start.4
  25.5 0.8 %shard_map.116 = (f32[16,256]{1,0:T(8,128)S(1)}, f32[48,256]{1,0:T(8,128)S(1)}) custom-call(s32[1]{0:T(128)S(6)} %copy.15.refs_0_, s32[1]{0:T(128)} %bitcast.refs_1_, f32[8,256]{1,0:T(8,128)S(1)} %get-tuple-element.36.refs_4_.refs_2_, f32[16,256]{1,0:T(8,128)S(1)} %get-tuple-element.50.refs_3_, bf16[4,144,512]{2,1,0:T(8,128)(2,1)S(1)} %get-tuple-element.51.refs_4_.refs_6_, ...), custom_call_target="tpu_custom_call" | custom-call | tf_op jit(solution)/shard_map/pallas_call | solution.py:743
  26.3 0.1 collective-permute-start.3
  26.5 0.4 collective-permute-done.5.refs_11_
  26.8 0.0 collective-permute-done.4.refs_10_
  26.8 0.7 %collective-permute-done.3.refs_9_ = f32[16,256]{1,0:T(8,128)S(1)} collective-permute-done((f32[16,256]{1,0:T(8,128)S(1)}, f32[16,256]{1,0:T(8,128)S(1)}, u32[]{:S(2)}, u32[]{:S(2)}) %collective-permute-start.3) | collective-permute-done | bytes 16416 | tf_op jit(solution)/shard_map/ppermute | solution.py:799
  27.5 3.2 %all-to-all-done.1 = f32[32,1,128]{2,1,0:T(1,128)S(1)} async-done(((f32[32,1,128]{2,1,0:T(1,128)}), f32[32,1,128]{2,1,0:T(1,128)S(1)}, u32[]{:S(2)}, u32[]{:S(2)}) %all-to-all-start.1) | async-done | bytes 16416 | tf_op jit(solution)/shard_map/all_to_all | solution.py:779
  30.7 1.1 %shard_map.117 = (f32[272,128]{1,0:T(8,128)S(1)}, f32[192,128]{1,0:T(8,128)S(1)}, f32[32,128]{1,0:T(8,128)}) custom-call(s32[1]{0:T(128)S(6)} %copy.15.refs_0_, s32[1]{0:T(128)} %bitcast.refs_1_, f32[272,128]{1,0:T(8,128)S(1)} %get-tuple-element.48.refs_2_, f32[32,128]{1,0:T(8,128)S(1)} %bitcast.16, f32[48,256]{1,0:T(8,128)S(1)} %get-tuple-element.56.refs_4_, ...), custom_call_target="tpu_custom_call" | custom-call | tf_op jit(solution)/shard_map/pallas_call | solution.py:743
  31.8 3.2 %all-to-all-start.2 = ((f32[32,1,128]{2,1,0:T(1,128)}), f32[32,1,128]{2,1,0:T(1,128)S(1)}, u32[]{:S(2)}, u32[]{:S(2)}) async-start(f32[32,1,128]{2,1,0:T(1,128)} %bitcast.17), calls=%async_computation.2 | async-start | bytes 32768 | tf_op jit(solution)/shard_map/all_to_all | solution.py:779
  35.0 0.6 %shard_map.118 = (f32[16,256]{1,0:T(8,128)S(1)}, bf16[4,144,512]{2,1,0:T(8,128)(2,1)S(1)}, bf16[4,144,512]{2,1,0:T(8,128)(2,1)S(1)}, f32[192,128]{1,0:T(8,128)S(1)}, f32[512,128]{1,0:T(8,128)S(1)}) custom-call(s32[1]{0:T(128)S(6)} %copy.15.refs_0_, s32[1]{0:T(128)} %bitcast.refs_1_, f32[272,128]{1,0:T(8,128)S(1)} %get-tuple-element.58.refs_2_, ...), custom_call_target="tpu_custom_call" | custom-call | tf_op jit(solution)/shard_map/pallas_call | solution.py:743
  35.7 0.8 %shard_map.119 = (f32[16,256]{1,0:T(8,128)S(1)}, f32[48,256]{1,0:T(8,128)S(1)}) custom-call(s32[1]{0:T(128)S(6)} %copy.15.refs_0_, s32[1]{0:T(128)} %bitcast.refs_1_, f32[8,256]{1,0:T(8,128)S(1)} %get-tuple-element.36.refs_4_.refs_2_, f32[16,256]{1,0:T(8,128)S(1)} %get-tuple-element.61.refs_3_, bf16[4,144,512]{2,1,0:T(8,128)(2,1)S(1)} %get-tuple-element.62.refs_4_.refs_6_, ...), custom_call_target="tpu_custom_call" | custom-call | tf_op jit(solution)/shard_map/pallas_call | solution.py:743
  36.4 0.3 collective-permute-start.6
  36.7 1.6 %collective-permute-start.8 = (f32[16,256]{1,0:T(8,128)S(1)}, f32[16,256]{1,0:T(8,128)S(1)}, u32[]{:S(2)}, u32[]{:S(2)}) collective-permute-start(f32[16,256]{1,0:T(8,128)S(1)} %get-tuple-element.61.refs_3_), channel_id=1, source_target_pairs={{0,3},{1,2},{2,1},{3,0},{4,7},{5,6},{6,5},{7,4},{8,11},{9,10},{10,... | collective-permute-start | bytes 49160 | tf_op jit(solution)/shard_map/ppermute | solution.py:785
  38.4 0.1 collective-permute-start.7
  38.5 0.0 collective-permute-done.6.refs_9_
  38.5 1.4 %collective-permute-done.8.refs_11_ = f32[16,256]{1,0:T(8,128)S(1)} collective-permute-done((f32[16,256]{1,0:T(8,128)S(1)}, f32[16,256]{1,0:T(8,128)S(1)}, u32[]{:S(2)}, u32[]{:S(2)}) %collective-permute-start.8) | collective-permute-done | bytes 16416 | tf_op jit(solution)/shard_map/ppermute | solution.py:785
  39.9 0.0 collective-permute-done.7.refs_10_
  39.9 2.2 %all-to-all-done.2 = f32[32,1,128]{2,1,0:T(1,128)S(1)} async-done(((f32[32,1,128]{2,1,0:T(1,128)}), f32[32,1,128]{2,1,0:T(1,128)S(1)}, u32[]{:S(2)}, u32[]{:S(2)}) %all-to-all-start.2) | async-done | bytes 16416 | tf_op jit(solution)/shard_map/all_to_all | solution.py:779
  42.1 1.4 %shard_map.120 = (f32[3,4096]{1,0:T(4,128)}, f32[3,4096]{1,0:T(4,128)}, f32[9,4096]{1,0:T(8,128)}, f32[9,4096]{1,0:T(8,128)}) custom-call(s32[1]{0:T(128)S(6)} %copy.15.refs_0_, s32[1]{0:T(128)} %bitcast.refs_1_, f32[272,128]{1,0:T(8,128)S(1)} %get-tuple-element.58.refs_2_, f32[32,128]{1,0:T(8,128)S(1)} %bitcast.15, ...), custom_call_target="tpu_custom_call" | custom-call | tf_op jit(solution)/shard_map/pallas_call | solution.py:743
Async XLA Ops:
  2.8 14.4 %all-to-all-start = ((f32[32,1,128]{2,1,0:T(1,128)}), f32[32,1,128]{2,1,0:T(1,128)S(1)}, u32[]{:S(2)}, u32[]{:S(2)}) async-start(f32[32,1,128]{2,1,0:T(1,128)} %bitcast.19), calls=%async_computation | async-start | bytes 32768 | tf_op jit(solution)/shard_map/all_to_all | solution.py:779
  11.6 5.9 %collective-permute-start = (f32[16,256]{1,0:T(8,128)S(1)}, f32[16,256]{1,0:T(8,128)S(1)}, u32[]{:S(2)}, u32[]{:S(2)}) collective-permute-start(f32[16,256]{1,0:T(8,128)S(1)} %get-tuple-element.47), channel_id=1, source_target_pairs={{0,1},{1,0},{2,3},{3,2},{4,5},{5,4},{6,7},{7,6},{8,9},{9,8},{10,11... | collective-permute-start | bytes 49160 | tf_op jit(solution)/shard_map/ppermute | solution.py:799
  11.9 5.7 %collective-permute-start.2 = (f32[16,256]{1,0:T(8,128)S(1)}, f32[16,256]{1,0:T(8,128)S(1)}, u32[]{:S(2)}, u32[]{:S(2)}) collective-permute-start(f32[16,256]{1,0:T(8,128)S(1)} %get-tuple-element.40.refs_3_), channel_id=1, source_target_pairs={{0,3},{1,2},{2,1},{3,0},{4,7},{5,6},{6,5},{7,4},{8,11},{9,10},{10,... | collective-permute-start | bytes 49160 | tf_op jit(solution)/shard_map/ppermute | solution.py:785
  13.5 4.1 %collective-permute-start.1 = (f32[16,256]{1,0:T(8,128)S(1)}, f32[16,256]{1,0:T(8,128)S(1)}, u32[]{:S(2)}, u32[]{:S(2)}) collective-permute-start(f32[16,256]{1,0:T(8,128)S(1)} %get-tuple-element.40.refs_3_), channel_id=1, source_target_pairs={{3,4},{7,8},{11,12},{15,16},{19,20},{23,24},{27,28},{2,5},{6,9},{1... | collective-permute-start | bytes 49160 | tf_op jit(solution)/shard_map/ppermute | solution.py:784
  19.0 11.7 %all-to-all-start.1 = ((f32[32,1,128]{2,1,0:T(1,128)}), f32[32,1,128]{2,1,0:T(1,128)S(1)}, u32[]{:S(2)}, u32[]{:S(2)}) async-start(f32[32,1,128]{2,1,0:T(1,128)} %bitcast.18), calls=%async_computation.1 | async-start | bytes 32768 | tf_op jit(solution)/shard_map/all_to_all | solution.py:779
  23.6 3.2 %collective-permute-start.5 = (f32[16,256]{1,0:T(8,128)S(1)}, f32[16,256]{1,0:T(8,128)S(1)}, u32[]{:S(2)}, u32[]{:S(2)}) collective-permute-start(f32[16,256]{1,0:T(8,128)S(1)} %get-tuple-element.50.refs_3_), channel_id=1, source_target_pairs={{0,3},{1,2},{2,1},{3,0},{4,7},{5,6},{6,5},{7,4},{8,11},{9,10},{10,... | collective-permute-start | bytes 49160 | tf_op jit(solution)/shard_map/ppermute | solution.py:785
  25.1 1.7 %collective-permute-start.4 = (f32[16,256]{1,0:T(8,128)S(1)}, f32[16,256]{1,0:T(8,128)S(1)}, u32[]{:S(2)}, u32[]{:S(2)}) collective-permute-start(f32[16,256]{1,0:T(8,128)S(1)} %get-tuple-element.50.refs_3_), channel_id=1, source_target_pairs={{3,4},{7,8},{11,12},{15,16},{19,20},{23,24},{27,28},{2,5},{6,9},{1... | collective-permute-start | bytes 49160 | tf_op jit(solution)/shard_map/ppermute | solution.py:784
  26.3 1.2 %collective-permute-start.3 = (f32[16,256]{1,0:T(8,128)S(1)}, f32[16,256]{1,0:T(8,128)S(1)}, u32[]{:S(2)}, u32[]{:S(2)}) collective-permute-start(f32[16,256]{1,0:T(8,128)S(1)} %get-tuple-element.57), channel_id=1, source_target_pairs={{0,1},{1,0},{2,3},{3,2},{4,5},{5,4},{6,7},{7,6},{8,9},{9,8},{10,11... | collective-permute-start | bytes 49160 | tf_op jit(solution)/shard_map/ppermute | solution.py:799
  31.8 10.3 %all-to-all-start.2 = ((f32[32,1,128]{2,1,0:T(1,128)}), f32[32,1,128]{2,1,0:T(1,128)S(1)}, u32[]{:S(2)}, u32[]{:S(2)}) async-start(f32[32,1,128]{2,1,0:T(1,128)} %bitcast.17), calls=%async_computation.2 | async-start | bytes 32768 | tf_op jit(solution)/shard_map/all_to_all | solution.py:779
  36.4 2.0 %collective-permute-start.6 = (f32[16,256]{1,0:T(8,128)S(1)}, f32[16,256]{1,0:T(8,128)S(1)}, u32[]{:S(2)}, u32[]{:S(2)}) collective-permute-start(f32[16,256]{1,0:T(8,128)S(1)} %get-tuple-element.67), channel_id=1, source_target_pairs={{0,1},{1,0},{2,3},{3,2},{4,5},{5,4},{6,7},{7,6},{8,9},{9,8},{10,11... | collective-permute-start | bytes 49160 | tf_op jit(solution)/shard_map/ppermute | solution.py:799
  36.7 3.2 %collective-permute-start.8 = (f32[16,256]{1,0:T(8,128)S(1)}, f32[16,256]{1,0:T(8,128)S(1)}, u32[]{:S(2)}, u32[]{:S(2)}) collective-permute-start(f32[16,256]{1,0:T(8,128)S(1)} %get-tuple-element.61.refs_3_), channel_id=1, source_target_pairs={{0,3},{1,2},{2,1},{3,0},{4,7},{5,6},{6,5},{7,4},{8,11},{9,10},{10,... | collective-permute-start | bytes 49160 | tf_op jit(solution)/shard_map/ppermute | solution.py:785
  38.4 1.5 %collective-permute-start.7 = (f32[16,256]{1,0:T(8,128)S(1)}, f32[16,256]{1,0:T(8,128)S(1)}, u32[]{:S(2)}, u32[]{:S(2)}) collective-permute-start(f32[16,256]{1,0:T(8,128)S(1)} %get-tuple-element.61.refs_3_), channel_id=1, source_target_pairs={{3,4},{7,8},{11,12},{15,16},{19,20},{23,24},{27,28},{2,5},{6,9},{1... | collective-permute-start | bytes 49160 | tf_op jit(solution)/shard_map/ppermute | solution.py:784
